TPU v7x, 128 devices: a whole 4x4x4 slice. The times are simulated.
128 devices in a mesh: space: 16 (over y_lo, x, core), tm: 8 (over z, y_hi).
Axes of the slice: x: 4, y: 4 (y_hi: 2, y_lo: 2; y = y_hi * 2 + y_lo), z: 4, core: 2. Of those that a mesh axis runs over, the one named last changes fastest.
Arguments:
- tokens: bfloat16 [16, 32, 64, 768], P('space', 'tm'), may hold values from -6 to 6
- grad_out: bfloat16 [16, 32, 64, 768], P('space', 'tm'), may hold values from -48 to 48
- w_qkv: bfloat16 [768, 1152], replicated, may hold values from -0.21875 to 0.21875
- w_out: bfloat16 [384, 768], replicated, may hold values from -0.3125 to 0.3125
- brain_mask: int32 [16], replicated, may hold values from 0 to 1, as said below
- block_table: int32 [16], replicated, may hold values from 0 to 15, each once
Outputs:
- token_grads: bfloat16 [16, 32, 64, 768], P('space', 'tm')
- qkv_grads: float32 [768, 1152], replicated
- out_grads: float32 [384, 768], replicated
Inputs may be any that keep to these rules, and one draw needn't show every extreme that they name: `brain_mask`: 1 marks a block inside the brain; between 8 and 12 of the 16 blocks are marked. Slot s holds block block_table[s]; every block appears once.
All inputs are finite; a program needn't handle non-finite values.
Results may differ from a plain program's by a relative error of at most 0.015.
The roundings to bfloat16 on the way count: a program that leaves them out, or rounds other values in their place, can miss the bound.
Values may be sent and summed in bfloat16 or wider, within the bound.
A program may use at most 192 MiB of HBM per device.

v0:
```python
from functools import partial

import jax
import jax.numpy as jnp
from jax import lax
from jax.sharding import PartitionSpec as P

D = 768
HEADS = 6
HD = 64
SIDE = 4
BP = 64
RAD_S = 3
RAD_T = 2


NEIGHBOURS = ((-1, -1), (-1, 0), (-1, 1), (0, -1), (0, 0), (0, 1), (1, -1), (1, 0), (1, 1))


def with_halo(cells, sides, width):
    for axis, dim in sides:
        count = lax.axis_size(axis)
        ends = count - 1
        head = lax.slice_in_dim(cells, 0, width, axis=dim)
        tail = lax.slice_in_dim(cells, cells.shape[dim] - width, cells.shape[dim], axis=dim)
        cells = jnp.concatenate(
            [
                lax.ppermute(tail, axis, [(i, (i + 1) % count) for i in range(ends)]),
                cells,
                lax.ppermute(head, axis, [((i + 1) % count, i) for i in range(ends)]),
            ],
            axis=dim,
        )
    return cells


def from_behind(value, axis, by):
    peers = lax.axis_size(axis)
    pairs = [(i, i + by) for i in range(peers) if 0 <= i + by < peers]
    return lax.ppermute(value, axis, pairs)


def lookup_many(values, indices):
    positions = jnp.arange(values.shape[0], dtype=jnp.int32)
    picked = jnp.where(indices[:, None] == positions[None, :], values[None, :], 0)
    return jnp.sum(picked, axis=1)


def inverse_table(block_table):
    positions = jnp.arange(block_table.shape[0], dtype=jnp.int32)
    picked = jnp.where(block_table[:, None] == positions[None, :], positions[:, None], 0)
    return jnp.sum(picked, axis=0)


def neighbour_blocks(block_number, brain_mask):
    offsets = jnp.array(NEIGHBOURS, dtype=jnp.int32)
    near_row = block_number // SIDE + offsets[:, 0]
    near_col = block_number % SIDE + offsets[:, 1]
    inside = (near_row >= 0) & (near_row < SIDE) & (near_col >= 0) & (near_col < SIDE)
    nearby = jnp.clip(near_row, 0, SIDE - 1) * SIDE + jnp.clip(near_col, 0, SIDE - 1)
    usable = inside & (lookup_many(brain_mask, nearby) == 1)
    return (nearby, usable)


def token_places(blocks, first_frame, frame_count):
    patches = jnp.arange(BP, dtype=jnp.int32)
    frames = first_frame + jnp.arange(frame_count, dtype=jnp.int32)
    grid_shape = (blocks.shape[0], frame_count, BP)
    place_x = jnp.broadcast_to(
        (blocks // SIDE)[:, None, None] * 4 + (patches // 16)[None, None, :], grid_shape
    )
    place_y = jnp.broadcast_to(
        (blocks % SIDE)[:, None, None] * 4 + (patches // 4 % 4)[None, None, :], grid_shape
    )
    place_t = jnp.broadcast_to(frames[None, :, None], grid_shape)
    return (place_x.reshape(-1), place_y.reshape(-1), place_t.reshape(-1))


def window_allowed(row_places, col_places):
    near_x = jnp.abs(row_places[0][:, None] - col_places[0][None, :]) <= RAD_S
    near_y = jnp.abs(row_places[1][:, None] - col_places[1][None, :]) <= RAD_S
    near_t = jnp.abs(row_places[2][:, None] - col_places[2][None, :]) <= RAD_T
    return near_x & near_y & near_t


def key_usable(usable, first_frame, frame_count, frames_total):
    frames = first_frame + jnp.arange(frame_count, dtype=jnp.int32)
    inside = (frames >= 0) & (frames < frames_total)
    full = usable[:, None, None] & inside[None, :, None] & jnp.ones((1, 1, BP), dtype=jnp.bool_)
    return full.reshape(-1)


def tile_grad(query_rows, grad_rows, key_rows, allowed, brain_flag, with_keys):
    row_count = query_rows.shape[0]
    key_count = key_rows.shape[0]
    features = query_rows.shape[1]
    scaling = HD ** (-0.5)
    query_heads = query_rows.reshape(row_count, HEADS, HD)
    grad_heads = grad_rows.reshape(row_count, HEADS, HD)
    key_heads = key_rows[:, :features].reshape(key_count, HEADS, HD)
    value_heads = key_rows[:, features:].reshape(key_count, HEADS, HD)
    scores = scaling * jnp.einsum(
        "rhd,khd->hrk", query_heads, key_heads, preferred_element_type=jnp.float32
    )
    exp_scores = jnp.where(allowed[None], jnp.exp(scores), 0.0)
    totals = jnp.sum(exp_scores, axis=2) + (1.0 - brain_flag)
    softmax_weights = exp_scores / totals[:, :, None]
    weights_low = softmax_weights.astype(jnp.bfloat16)
    attended = jnp.einsum(
        "hrk,khd->rhd", weights_low, value_heads, preferred_element_type=jnp.float32
    )
    attended = (attended * brain_flag).astype(jnp.bfloat16)
    deltas = jnp.sum(grad_heads.astype(jnp.float32) * attended.astype(jnp.float32), axis=2)
    grad_weights = jnp.einsum(
        "rhd,khd->hrk", grad_heads, value_heads, preferred_element_type=jnp.float32
    )
    grad_scores = (softmax_weights * (grad_weights - deltas.T[:, :, None])).astype(jnp.bfloat16)
    grad_query = (
        scaling
        * jnp.einsum("hrk,khd->rhd", grad_scores, key_heads, preferred_element_type=jnp.float32)
        * brain_flag
    )
    result = (
        grad_query.reshape(row_count, features),
        attended.reshape(row_count, features),
        totals.T,
        deltas,
    )
    grad_key = (
        scaling
        * jnp.einsum("hrk,rhd->khd", grad_scores, query_heads, preferred_element_type=jnp.float32)
        * brain_flag
    )
    grad_value = (
        jnp.einsum("hrk,rhd->khd", weights_low, grad_heads, preferred_element_type=jnp.float32)
        * brain_flag
    )
    result = result + (
        grad_key.reshape(key_count, features),
        grad_value.reshape(key_count, features),
    )
    return result


def tile_skip(row_count, key_count, features, with_keys):
    result = (
        jnp.zeros((row_count, features), jnp.float32),
        jnp.zeros((row_count, features), jnp.bfloat16),
        jnp.ones((row_count, HEADS), jnp.float32),
        jnp.zeros((row_count, HEADS), jnp.float32),
    )
    empty_keys = jnp.zeros((key_count, features), jnp.float32)
    result = result + (empty_keys, empty_keys)
    return result


def shards(tokens, grad_out, w_qkv, w_out, brain_mask, block_table):
    local_blocks = tokens.shape[0]
    local_frames = tokens.shape[1]
    features = HEADS * HD
    key_span = 2 + 2 * RAD_T
    tile_count = local_frames // 2
    frames_total = local_frames * lax.axis_size("tm")
    first_frame = lax.axis_index("tm") * local_frames
    first_slot = lax.axis_index("space") * local_blocks
    flat_tokens = tokens.reshape(-1, D)
    projected = jnp.dot(flat_tokens, w_qkv, preferred_element_type=jnp.float32).astype(jnp.bfloat16)
    projected = projected.reshape(local_blocks, local_frames, BP, 3 * features)
    queries = projected[..., :features]
    key_values = projected[..., features:]
    flat_grad = grad_out.reshape(-1, D)
    grad_attended = lax.dot_general(
        flat_grad, w_out, (((1,), (1,)), ((), ())), preferred_element_type=jnp.float32
    )
    grad_attended = grad_attended.astype(jnp.bfloat16).reshape(
        local_blocks, local_frames, BP, features
    )
    slot_of_block = inverse_table(block_table)
    framed = with_halo(key_values, (("tm", 1),), RAD_T)
    gathered = lax.all_gather(framed, "space", axis=0, tiled=True)
    slot_count = gathered.shape[0]
    key_partial = jnp.zeros((slot_count, local_frames + 2 * RAD_T, BP, features), jnp.float32)
    value_partial = jnp.zeros((slot_count, local_frames + 2 * RAD_T, BP, features), jnp.float32)
    query_blocks, attended_blocks, totals_blocks, deltas_blocks = ([], [], [], [])
    slot_index = jnp.reshape(first_slot + 0, (1,))
    block_number = lookup_many(block_table, slot_index)[0]
    brain_flag = lookup_many(brain_mask, block_number[None])[0].astype(jnp.float32)
    nearby, usable = neighbour_blocks(block_number, brain_mask)
    near_slots = lookup_many(slot_of_block, nearby)
    block_number, brain_flag, nearby, usable, near_slots = (
        block_number,
        brain_flag,
        nearby,
        usable,
        near_slots,
    )
    near_keys = jnp.take(gathered, near_slots, axis=0)
    query_tiles = []
    attended_tiles = []
    totals_tiles = []
    deltas_tiles = []
    for tile_index in range(tile_count):
        low_frame = 2 * tile_index
        key_rows = near_keys[:, low_frame : low_frame + key_span].reshape(-1, 2 * features)
        query_rows = queries[0, low_frame : low_frame + 2].reshape(-1, features)
        grad_rows = grad_attended[0, low_frame : low_frame + 2].reshape(-1, features)
        row_places = token_places(block_number[None], first_frame + low_frame, 2)
        col_places = token_places(nearby, first_frame + low_frame - RAD_T, key_span)
        allowed = window_allowed(row_places, col_places)
        allowed = (
            allowed
            & key_usable(usable, first_frame + low_frame - RAD_T, key_span, frames_total)[None, :]
        )
        outcome = lax.cond(
            brain_flag > 0,
            partial(tile_grad, query_rows, grad_rows, key_rows, allowed, brain_flag, True),
            partial(tile_skip, query_rows.shape[0], key_rows.shape[0], features, True),
        )
        query_tiles.append(outcome[0])
        attended_tiles.append(outcome[1])
        totals_tiles.append(outcome[2])
        deltas_tiles.append(outcome[3])
        near_frames = low_frame + jnp.arange(key_span, dtype=jnp.int32)
        key_partial = key_partial.at[near_slots[:, None], near_frames[None, :]].add(
            outcome[4].reshape(9, key_span, BP, features)
        )
        value_partial = value_partial.at[near_slots[:, None], near_frames[None, :]].add(
            outcome[5].reshape(9, key_span, BP, features)
        )
    query_blocks.append(jnp.concatenate(query_tiles, axis=0).reshape(local_frames, BP, features))
    attended_blocks.append(
        jnp.concatenate(attended_tiles, axis=0).reshape(local_frames, BP, features)
    )
    totals_blocks.append(jnp.concatenate(totals_tiles, axis=0).reshape(local_frames, BP, HEADS))
    deltas_blocks.append(jnp.concatenate(deltas_tiles, axis=0).reshape(local_frames, BP, HEADS))
    grad_query = jnp.stack(query_blocks, axis=0)
    attended_all = jnp.stack(attended_blocks, axis=0)
    key_sum, value_sum = (
        lax.psum_scatter(key_partial, "space", scatter_dimension=0, tiled=True),
        lax.psum_scatter(value_partial, "space", scatter_dimension=0, tiled=True),
    )
    both_sums = jnp.concatenate([key_sum, value_sum], axis=3)
    from_next = from_behind(both_sums[:, :RAD_T], "tm", -1)
    from_prev = from_behind(
        both_sums[:, local_frames + RAD_T :].astype(jnp.bfloat16), "tm", 1
    ).astype(jnp.float32)
    core = both_sums[:, RAD_T : RAD_T + local_frames]
    core = core.at[:, :RAD_T].add(from_prev)
    core = core.at[:, local_frames - RAD_T :].add(from_next)
    key_value_grads = core.astype(jnp.bfloat16)
    grads = jnp.concatenate([grad_query.astype(jnp.bfloat16), key_value_grads], axis=3).reshape(
        -1, 3 * features
    )
    token_grads = lax.dot_general(
        grads, w_qkv, (((1,), (1,)), ((), ())), preferred_element_type=jnp.float32
    )
    token_grads = token_grads.astype(jnp.bfloat16).reshape(tokens.shape)
    qkv_term = lax.dot_general(
        flat_tokens, grads, (((0,), (0,)), ((), ())), preferred_element_type=jnp.float32
    )
    out_term = lax.dot_general(
        attended_all.reshape(-1, features),
        flat_grad,
        (((0,), (0,)), ((), ())),
        preferred_element_type=jnp.float32,
    )
    qkv_grads, out_grads = lax.psum((qkv_term, out_term), ("space", "tm"))
    return (token_grads, qkv_grads, out_grads)


def solution(mesh):
    in_specs = (P("space", "tm", None, None), P("space", "tm", None, None), P(), P(), P(), P())
    out_specs = (P("space", "tm", None, None), P(), P())
    return jax.shard_map(shards, mesh=mesh, in_specs=in_specs, out_specs=out_specs, check_vma=False)
```

profile of v0, /device:TPU:1, one launch (start us, length us, event | category | flops | bytes accessed | tf_op | source)
XLA Modules:
  0.0 719.1 jit_solution(15771887390679589751)
XLA Ops:
  10.4 5.7 collective-permute-start
  19.6 6.8 collective-permute-done.1
  40.2 62.0 %all-gather.2.cloned.1.call-done = bf16[16,8,64,768]{3,2,1,0:T(8,128)(2,1)} async-done(((bf16[1,8,64,768]{3,2,1,0:T(8,128)(2,1)}), bf16[16,8,64,768]{3,2,1,0:T(8,128)(2,1)}) %all-gather.2.cloned.1.call-update) | async-done | bytes 12582928 | tf_op jit(solution)/shard_map/all_gather | solution.py:180
  102.2 9.4 %gather_fusion = bf16[9,8,64,768]{3,2,1,0:T(8,128)(2,1)} fusion(bf16[16,8,64,768]{3,2,1,0:T(8,128)(2,1)} %all-gather.2.cloned.1.call-done, s32[1024]{0:T(1024)S(1)} %pad_clamp_fusion), kind=kCustom, calls=%fused_computation | custom fusion | bytes 14155812 | tf_op jit(solution)/shard_map/jit(_take)/gather | solution.py:197
  111.7 6.7 broadcast_select_fusion
  119.5 101.7 %conditional.3 = (bf16[128,384]{0,1:T(8,128)(2,1)}, bf16[128,384]{0,1:T(8,128)(2,1)}, f32[9,6,64,384]{3,2,1,0:T(8,128)}, f32[9,6,64,384]{3,2,1,0:T(8,128)}) conditional(s32[]{:T(128)} %convert_element_type.85, () %tuple.49, (s32[]{:T(128)}, s32[1,2,1]{1,2,0:T(1,128)}, s32[1,6,1]{1,2,0:T(1,128)S(1)}, s32[128,3456]{1,0:T(8,128)S(1)}, ...), branch_computations={%region_9.10_spmd, %region_10.13_spmd} | conditional | flops 2088811904 | bytes 185301152 | solution.py:214
  132.6 3.6 copy.69
  139.8 2.9 slice.121
  142.6 2.9 fusion.65
  145.6 4.5 copy.63
  150.1 4.4 copy.64
  154.5 4.9 fusion.18
  159.5 3.8 multiply_reduce_fusion.1
  163.3 4.1 multiply_convert_fusion.1
  167.4 5.2 fusion.20
  175.2 3.3 fusion.19
  178.5 9.8 %reshape.590 = f32[9,6,64,384]{2,1,0,3:T(8,128)} reshape(f32[3456,6,64]{0,2,1:T(8,128)} %fusion.19) | data formatting | bytes 10616832 | tf_op jit(solution)/shard_map/reshape | solution.py:225
  188.2 11.5 %copy.76 = f32[9,6,64,384]{3,2,1,0:T(8,128)} copy(f32[9,6,64,384]{2,1,0,3:T(8,128)} %reshape.590) | data formatting | bytes 10616832 | tf_op jit(solution)/shard_map/reshape | solution.py:225
  199.8 9.8 %reshape.591 = f32[9,6,64,384]{2,1,0,3:T(8,128)} reshape(f32[3456,6,64]{0,2,1:T(8,128)} %fusion.20) | data formatting | bytes 10616832 | tf_op jit(solution)/shard_map/reshape | solution.py:228
  209.5 11.5 %copy.77 = f32[9,6,64,384]{3,2,1,0:T(8,128)} copy(f32[9,6,64,384]{2,1,0,3:T(8,128)} %reshape.591) | data formatting | bytes 10616832 | tf_op jit(solution)/shard_map/reshape | solution.py:228
  221.2 95.1 %conditional.2 = (bf16[128,384]{0,1:T(8,128)(2,1)}, bf16[128,384]{0,1:T(8,128)(2,1)}, f32[9,6,64,384]{3,2,1,0:T(8,128)}, f32[9,6,64,384]{3,2,1,0:T(8,128)}) conditional(s32[]{:T(128)} %convert_element_type.85, () %tuple.47, (s32[]{:T(128)}, s32[1,2,1]{1,2,0:T(1,128)}, s32[1,6,1]{1,2,0:T(1,128)}, s32[128,3456]{1,0:T(8,128)S(1)}, ...), branch_computations={%region_5.6_spmd, %region_6.9_spmd} | conditional | flops 2088811904 | bytes 184514656 | solution.py:214
  234.8 2.9 slice.116
  237.7 2.9 fusion.64
  240.6 4.6 copy.58
  245.2 4.4 copy.59
  249.6 4.8 fusion.1
  254.5 3.8 multiply_reduce_fusion
  258.3 4.0 multiply_convert_fusion
  262.3 5.1 fusion.3
  267.4 2.6 convolution_multiply_fusion.2
  270.0 3.3 fusion.2
  273.3 9.9 %reshape.588 = f32[9,6,64,384]{2,1,0,3:T(8,128)} reshape(f32[3456,6,64]{0,2,1:T(8,128)} %fusion.2) | data formatting | bytes 10616832 | tf_op jit(solution)/shard_map/reshape | solution.py:225
  283.2 11.6 %copy.74 = f32[9,6,64,384]{3,2,1,0:T(8,128)} copy(f32[9,6,64,384]{2,1,0,3:T(8,128)} %reshape.588) | data formatting | bytes 10616832 | tf_op jit(solution)/shard_map/reshape | solution.py:225
  294.7 9.9 %reshape.589 = f32[9,6,64,384]{2,1,0,3:T(8,128)} reshape(f32[3456,6,64]{0,2,1:T(8,128)} %fusion.3) | data formatting | bytes 10616832 | tf_op jit(solution)/shard_map/reshape | solution.py:228
  304.6 11.5 %copy.75 = f32[9,6,64,384]{3,2,1,0:T(8,128)} copy(f32[9,6,64,384]{2,1,0,3:T(8,128)} %reshape.589) | data formatting | bytes 10616832 | tf_op jit(solution)/shard_map/reshape | solution.py:228
  316.3 6.1 broadcast.645.clone
  322.4 16.5 %scatter_fusion = f32[16,8,64,384]{3,2,1,0:T(8,128)} fusion(f32[16,8,64,384]{3,2,1,0:T(8,128)} %broadcast.645.clone, s32[54]{0:T(128)S(1)} %copy-done.2, f32[54,64,384]{2,1,0:T(8,128)} %bitcast.39), kind=kCustom, calls=%fused_computation.1 | custom fusion | flops 1327104 | bytes 15925680 | tf_op jit(solution)/shard_map/scatter-add | solution.py:224
  338.9 16.4 %scatter_fusion.1 = f32[16,8,64,384]{3,2,1,0:T(8,128)} fusion(f32[16,8,64,384]{3,2,1,0:T(8,128)} %scatter_fusion, s32[54]{0:T(128)S(1)} %copy-done.1, f32[54,64,384]{2,1,0:T(8,128)} %bitcast.40), kind=kCustom, calls=%fused_computation.2 | custom fusion | flops 1327104 | bytes 15925680 | tf_op jit(solution)/shard_map/scatter-add | solution.py:224
  355.4 6.2 broadcast.645.clone.1
  361.5 16.4 %scatter_fusion.2 = f32[16,8,64,384]{3,2,1,0:T(8,128)} fusion(f32[16,8,64,384]{3,2,1,0:T(8,128)} %broadcast.645.clone.1, s32[54]{0:T(128)S(1)} %copy-done.2, f32[54,64,384]{2,1,0:T(8,128)} %bitcast.41), kind=kCustom, calls=%fused_computation.3 | custom fusion | flops 1327104 | bytes 15925680 | tf_op jit(solution)/shard_map/scatter-add | solution.py:227
  378.0 16.5 %scatter_fusion.3 = f32[16,8,64,384]{3,2,1,0:T(8,128)} fusion(f32[16,8,64,384]{3,2,1,0:T(8,128)} %scatter_fusion.2, s32[54]{0:T(128)S(1)} %copy-done.1, f32[54,64,384]{2,1,0:T(8,128)} %bitcast.42), kind=kCustom, calls=%fused_computation.4 | custom fusion | flops 1327104 | bytes 15925680 | tf_op jit(solution)/shard_map/scatter-add | solution.py:227
  394.5 40.7 %reduce-scatter.3.cloned.1.call-done = f32[1,8,64,384]{3,2,1,0:T(8,128)} async-done(((f32[16,8,64,384]{3,2,1,0:T(8,128)}), f32[1,8,64,384]{3,2,1,0:T(8,128)}) %reduce-scatter.3.cloned.1.call-update) | async-done | bytes 786448 | tf_op jit(solution)/shard_map/reduce_scatter | solution.py:239
  436.4 82.6 %reduce-scatter.5.cloned.1.call-done = f32[1,8,64,384]{3,2,1,0:T(8,128)} async-done(((f32[16,8,64,384]{3,2,1,0:T(8,128)}), f32[1,8,64,384]{3,2,1,0:T(8,128)}) %reduce-scatter.5.cloned.1.call-update) | async-done | bytes 786448 | tf_op jit(solution)/shard_map/reduce_scatter | solution.py:240
  521.4 4.5 collective-permute-start.2
  535.2 5.0 collective-permute-done.3
  540.3 3.6 convolution_bitcast_fusion
  545.4 160.7 %all-reduce.3.cloned.1.call-done = (f32[768,1152]{0,1:T(8,128)}, f32[384,768]{1,0:T(8,128)}) async-done(((f32[768,1152]{0,1:T(8,128)}, f32[384,768]{1,0:T(8,128)}), (f32[768,1152]{0,1:T(8,128)}, f32[384,768]{1,0:T(8,128)})) %all-reduce.3.cloned.1.call-update) | async-done | bytes 4718608 | tf_op jit(solution)/shard_map/psum | solution.py:267
  706.1 5.2 copy.73
  (151 shorter events, 64.0 us)
Async XLA Ops:
  7.2 1.5 copy-start
  7.2 28.4 %copy-start.21 = (s32[9,1]{0,1:T(1,128)S(1)}, s32[9,1]{0,1:T(1,128)}, u32[]{:S(2)}) copy-start(s32[9,1]{0,1:T(1,128)} %constant.286) | copy-start | bytes 112
  7.2 28.3 %copy-start.22 = (s32[9,1]{0,1:T(1,128)S(1)}, s32[9,1]{0,1:T(1,128)}, u32[]{:S(2)}) copy-start(s32[9,1]{0,1:T(1,128)} %constant.285) | copy-start | bytes 112
  7.2 20.2 %copy-start.24 = (s32[16]{0:T(128)S(1)}, s32[16]{0:T(128)}, u32[]{:S(2)}) copy-start(s32[16]{0:T(128)} %param.20) | copy-start | bytes 196
  7.2 26.1 %copy-start.23 = (s32[16]{0:T(128)S(1)}, s32[16]{0:T(128)}, u32[]{:S(2)}) copy-start(s32[16]{0:T(128)} %param.19) | copy-start | bytes 196
  7.2 30.2 %copy-start.11 = (bf16[384,768]{1,0:T(8,128)(2,1)S(1)}, bf16[384,768]{1,0:T(8,128)(2,1)}, u32[]{:S(2)}) copy-start(bf16[384,768]{1,0:T(8,128)(2,1)} %param.18) | copy-start | bytes 1769476
  7.2 30.2 %copy-start.9 = (bf16[1,4,64,768]{3,2,1,0:T(8,128)(2,1)S(1)}, bf16[1,4,64,768]{3,2,1,0:T(8,128)(2,1)}, u32[]{:S(2)}) copy-start(bf16[1,4,64,768]{3,2,1,0:T(8,128)(2,1)} %param.16) | copy-start | bytes 1179652
  7.2 95.0 %all-gather.2.cloned.1.call-start = ((), (), s32[]{:S(2)}) async-start(), calls=%async_computation.2 | async-start | bytes 13369344 | tf_op jit(solution)/shard_map/all_gather | solution.py:180
  10.4 7.0 copy-start.5
  10.4 9.2 %collective-permute-start = (bf16[1,2,64,768]{3,2,1,0:T(8,128)(2,1)S(1)}, bf16[1,2,64,768]{3,2,1,0:T(8,128)(2,1)S(1)}, u32[]{:S(2)}, u32[]{:S(2)}) collective-permute-start(bf16[1,2,64,768]{3,2,1,0:T(8,128)(2,1)S(1)} %get-tuple-element.377), channel_id=1, source_target_pairs={{0,1},{1,2},{2,3},{3,4},{4,5},{5,6},{6,7},{8,9},{9,10},{10,11},{11... | collective-permute-start | bytes 589832 | tf_op jit(solution)/shard_map/ppermute | solution.py:28
  16.1 10.3 %collective-permute-start.1 = (bf16[1,2,64,768]{3,2,1,0:T(8,128)(2,1)S(1)}, bf16[1,2,64,768]{3,2,1,0:T(8,128)(2,1)S(1)}, u32[]{:S(2)}, u32[]{:S(2)}) collective-permute-start(bf16[1,2,64,768]{3,2,1,0:T(8,128)(2,1)S(1)} %get-tuple-element.378), channel_id=1, source_target_pairs={{1,0},{2,1},{3,2},{4,3},{5,4},{6,5},{7,6},{9,8},{10,9},{11,10},{12... | collective-permute-start | bytes 589832 | tf_op jit(solution)/shard_map/ppermute | solution.py:30
  27.4 407.8 %reduce-scatter.3.cloned.1.call-start = ((), (), s32[]{:S(2)}) async-start(), calls=%async_computation.3 | async-start | bytes 13369344 | tf_op jit(solution)/shard_map/reduce_scatter | solution.py:239
  118.3 0.8 copy-start.18
  118.9 0.6 copy-start.17
  118.9 0.6 copy-start.19
  119.0 0.6 copy-start.20
  154.5 4.9 copy-start.7
  154.5 5.0 copy-start.13
  154.5 5.0 copy-start.16
  167.4 5.2 copy-start.3
  172.5 2.6 copy-start.12
  240.6 9.0 %copy-start.14 = (pred[128,3456]{1,0:T(8,128)(4,1)S(1)}, pred[128,3456]{1,0:T(8,128)(4,1)}, u32[]{:S(2)}) copy-start(pred[128,3456]{1,0:T(8,128)(4,1)} %fusion.8) | copy-start | bytes 1327108 | tf_op jit(solution)/shard_map/cond
  249.6 4.8 copy-start.8
  262.3 5.1 copy-start.4
  316.3 6.1 copy-start.2
  322.4 16.5 %copy-start.1 = (s32[54]{0:T(128)S(1)}, s32[54]{0:T(128)}, u32[]{:S(2)}) copy-start(s32[54]{0:T(128)} %reshape.569) | copy-start | bytes 652
  355.3 163.7 %reduce-scatter.5.cloned.1.call-start = ((), (), s32[]{:S(2)}) async-start(), calls=%async_computation.4 | async-start | bytes 13369344 | tf_op jit(solution)/shard_map/reduce_scatter | solution.py:240
  394.5 311.6 %all-reduce.3.cloned.1.call-start = ((), (), s32[]{:S(2)}) async-start(), calls=%async_computation.5 | async-start | bytes 9437184 | tf_op jit(solution)/shard_map/psum | solution.py:267
  520.2 1.1 copy-start.6
  521.4 7.1 collective-permute-start.2
  529.7 10.5 %collective-permute-start.3 = (f32[1,2,64,768]{3,2,1,0:T(8,128)S(1)}, f32[1,2,64,768]{3,2,1,0:T(8,128)S(1)}, u32[]{:S(2)}, u32[]{:S(2)}) collective-permute-start(f32[1,2,64,768]{3,2,1,0:T(8,128)S(1)} %get-tuple-element.375), channel_id=1, source_target_pairs={{1,0},{2,1},{3,2},{4,3},{5,4},{6,5},{7,6},{9,8},{10,9},{11,10},{12... | collective-permute-start | bytes 1179656 | tf_op jit(solution)/shard_map/ppermute | solution.py:40
  540.2 3.7 copy-start.15
  706.1 5.3 copy-start.10
Sparse Core Ops, SparseCore 0:
  27.5 74.6 all-gather.1
  355.4 79.7 reduce-scatter.2
  437.6 81.3 reduce-scatter.4
  544.0 162.0 all-reduce.2
where the time goes:
time: 728 us; the launch traced here: 719 us
  waiting for transfers between devices  361 us (50%)
  local copies, waits for them, and re-layouts  177 us (24%)
  other arithmetic  89.4 us (12%)
  matrix products  57.7 us (8%)
  between operations  20.2 us (3%)
  starting transfers between devices  12.9 us (2%)
    psum x1, waiting for transfers between devices, shards(): qkv_grads, out_grads = lax.psum((qkv_term, out_term), ('space', 'tm'))  161 us
    reduce_scatter x1, waiting for transfers between devices, shards(): lax.psum_scatter(value_partial, 'space', scatter_dimension=0, tiled=True)  82.6 us
    all_gather x1, waiting for transfers between devices, shards(): gathered = lax.all_gather(framed, 'space', axis=0, tiled=True)  62 us
    reshape x4, local copies, waits for them, and re-layouts, shards(): outcome[4].reshape(9, key_span, BP, features)  42.7 us
    reshape x4, local copies, waits for them, and re-layouts, shards(): outcome[5].reshape(9, key_span, BP, features)  42.7 us
    reduce_scatter x1, waiting for transfers between devices, shards(): lax.psum_scatter(key_partial, 'space', scatter_dimension=0, tiled=True)  40.7 us
    scatter-add x2, other arithmetic, shards(): value_partial.at[near_slots[:, None], near_frames[None, :]]  33 us
    scatter-add x2, other arithmetic, shards(): key_partial.at[near_slots[:, None], near_frames[None, :]]  32.9 us
  transfers between devices with their start and end apart: 8, of which 8 were waited for; matrix products, arithmetic and copies ran while one was open for 8% of the time, Pallas kernels for 0%

commit v1 on v0

v1 whole, which is shorter than its diff:
```python
import functools

import numpy as np
import jax
import jax.numpy as jnp
from jax import lax
from jax.experimental import pallas as pl
from jax.experimental.pallas import tpu as pltpu
from jax.sharding import PartitionSpec as P

D = 768
HEADS = 6
HD = 64
SIDE = 4
BP = 64
RAD_S = 3
RAD_T = 2
HW = HEADS * HD
LF = 4
KF = 6
KR = KF * BP
QR = 2 * BP
WORKERS = 2 * HEADS
ANY = pl.ANY


def where_lane(low, high):
    lane = lax.broadcasted_iota(jnp.int32, low.shape, low.ndim - 1)
    return jnp.where(lane < HD, low, high)


def project_kernel(tok_ref, gout_ref, wqkv_ref, wout_ref, out_ref):
    proj = jnp.dot(tok_ref[...], wqkv_ref[...], preferred_element_type=jnp.float32)
    gatt = lax.dot_general(
        gout_ref[...], wout_ref[...], (((1,), (1,)), ((), ())),
        preferred_element_type=jnp.float32,
    )

    def pair(low, high):
        first = where_lane(low, pltpu.roll(high, HD, 1)).astype(jnp.bfloat16)
        second = where_lane(pltpu.roll(low, HD, 1), high).astype(jnp.bfloat16)
        return first.reshape(LF, BP, 128), second.reshape(LF, BP, 128)

    for i in range(HEADS // 2):
        at = 128 * i
        keys = pair(proj[:, HW + at : HW + at + 128], proj[:, 2 * HW + at : 2 * HW + at + 128])
        queries = pair(proj[:, at : at + 128], gatt[:, at : at + 128])
        for j in range(2):
            out_ref[2 * i + j, 0:2] = queries[j][0:2]
            out_ref[2 * i + j, 2:6] = keys[j]
            out_ref[2 * i + j, 6:8] = queries[j][2:4]


def project(tokens, grad_out, w_qkv, w_out):
    vmem = pl.BlockSpec(memory_space=pltpu.VMEM)
    return pl.pallas_call(
        project_kernel,
        out_shape=jax.ShapeDtypeStruct((HEADS, 8, BP, 128), jnp.bfloat16),
        in_specs=[vmem] * 4,
        out_specs=vmem,
        compiler_params=pltpu.CompilerParams(vmem_limit_bytes=40 << 20),
        name="project",
    )(tokens, grad_out, w_qkv, w_out)


def spread_kernel(tm_size, src, main, halo, ssem, hsem, rsem, rhsem):
    me = lax.axis_index("space")
    t = lax.axis_index("tm")
    after = lax.rem(t + 1, tm_size)
    before = lax.rem(t + tm_size - 1, tm_size)

    def main_copy(w):
        return pltpu.make_async_remote_copy(
            src_ref=src.at[w // 2, pl.ds(2 * (w % 2), 6)],
            dst_ref=main.at[me],
            send_sem=ssem.at[w],
            recv_sem=rsem,
            device_id={"space": w, "tm": t},
            device_id_type=pl.DeviceIdType.MESH,
        )

    def halo_copy(h, half):
        return pltpu.make_async_remote_copy(
            src_ref=src.at[h, pl.ds(4 - 2 * half, 2)],
            dst_ref=halo.at[me],
            send_sem=hsem.at[2 * h + half],
            recv_sem=rhsem,
            device_id={"space": 2 * h + half, "tm": before if half else after},
            device_id_type=pl.DeviceIdType.MESH,
        )

    def send(i, carry):
        w = lax.rem(i + me, WORKERS)

        @pl.when(w != me)
        def _():
            main_copy(w).start()

        @pl.when(w == me)
        def _():
            pltpu.make_async_copy(
                src.at[w // 2, pl.ds(2 * (w % 2), 6)], main.at[me], rsem
            ).start()

        return carry

    def send_halo(i, carry):
        h = lax.rem(i + me // 2, HEADS)
        halo_copy(h, 0).start()
        halo_copy(h, 1).start()
        return carry

    lax.fori_loop(0, HEADS, send_halo, 0)
    lax.fori_loop(0, WORKERS, send, 0)

    def finish(w, carry):
        @pl.when(w != me)
        def _():
            main_copy(w).wait_send()

        return carry

    def finish_halo(h, carry):
        halo_copy(h, 0).wait_send()
        halo_copy(h, 1).wait_send()
        return carry

    @pl.when(me < WORKERS)
    def _():
        pltpu.make_async_copy(halo, halo, rhsem).wait()
        pltpu.make_async_copy(main, main, rsem).wait()

    lax.fori_loop(0, HEADS, finish_halo, 0)
    lax.fori_loop(0, WORKERS, finish, 0)


def spread(packed, slots, tm_size):
    any_spec = pl.BlockSpec(memory_space=ANY)
    return pl.pallas_call(
        functools.partial(spread_kernel, tm_size),
        out_shape=(
            jax.ShapeDtypeStruct((slots, 6, BP, 128), jnp.bfloat16),
            jax.ShapeDtypeStruct((slots, 2, BP, 128), jnp.bfloat16),
        ),
        in_specs=[any_spec],
        out_specs=(any_spec, any_spec),
        scratch_shapes=[
            pltpu.SemaphoreType.DMA((WORKERS,)),
            pltpu.SemaphoreType.DMA((WORKERS,)),
            pltpu.SemaphoreType.DMA,
            pltpu.SemaphoreType.DMA,
        ],
        compiler_params=pltpu.CompilerParams(has_side_effects=True),
        name="spread",
    )(packed)


def collect_kernel(slots, tm_size, main, halo, got, got_halo, ssem, hsem, rsem, rhsem):
    me = lax.axis_index("space")
    t = lax.axis_index("tm")
    head = me // 2
    half = me % 2
    other = lax.rem(t + tm_size + 2 * half - 1, tm_size)

    def main_copy(s):
        return pltpu.make_async_remote_copy(
            src_ref=main.at[s],
            dst_ref=got.at[half, head],
            send_sem=ssem.at[s],
            recv_sem=rsem,
            device_id={"space": s, "tm": t},
            device_id_type=pl.DeviceIdType.MESH,
        )

    def halo_copy(s):
        return pltpu.make_async_remote_copy(
            src_ref=halo.at[s],
            dst_ref=got_halo.at[half, head],
            send_sem=hsem.at[s],
            recv_sem=rhsem,
            device_id={"space": s, "tm": other},
            device_id_type=pl.DeviceIdType.MESH,
        )

    def send(i, carry):
        s = lax.rem(i + me, slots)

        @pl.when(s != me)
        def _():
            main_copy(s).start()

        @pl.when(s == me)
        def _():
            pltpu.make_async_copy(main.at[s], got.at[half, head], rsem).start()

        return carry

    def send_halo(i, carry):
        halo_copy(lax.rem(i + me, slots)).start()
        return carry

    def finish(s, carry):
        @pl.when(s != me)
        def _():
            main_copy(s).wait_send()

        return carry

    def finish_halo(s, carry):
        halo_copy(s).wait_send()
        return carry

    @pl.when(me < WORKERS)
    def _():
        lax.fori_loop(0, slots, send_halo, 0)
        lax.fori_loop(0, slots, send, 0)

    pltpu.make_async_copy(got_halo, got_halo, rhsem).wait()
    pltpu.make_async_copy(got, got, rsem).wait()

    @pl.when(me < WORKERS)
    def _():
        lax.fori_loop(0, slots, finish_halo, 0)
        lax.fori_loop(0, slots, finish, 0)


def collect(main, halo, slots, tm_size):
    any_spec = pl.BlockSpec(memory_space=ANY)
    return pl.pallas_call(
        functools.partial(collect_kernel, slots, tm_size),
        out_shape=(
            jax.ShapeDtypeStruct((2, HEADS, 6, BP, 128), jnp.bfloat16),
            jax.ShapeDtypeStruct((2, HEADS, 2, BP, 128), jnp.bfloat16),
        ),
        in_specs=[any_spec, any_spec],
        out_specs=(any_spec, any_spec),
        scratch_shapes=[
            pltpu.SemaphoreType.DMA((slots,)),
            pltpu.SemaphoreType.DMA((slots,)),
            pltpu.SemaphoreType.DMA,
            pltpu.SemaphoreType.DMA,
        ],
        compiler_params=pltpu.CompilerParams(has_side_effects=True),
        name="collect",
    )(main, halo)


def window_bias():
    patch = np.arange(BP)
    px, py = patch // 16, patch // 4 % 4
    out = np.zeros((9, KF, BP, 2, BP), np.float32)
    for n in range(9):
        dr, dc = n // 3 - 1, n % 3 - 1
        near_x = np.abs(px[:, None] + 4 * dr - px[None, :]) <= RAD_S
        near_y = np.abs(py[:, None] + 4 * dc - py[None, :]) <= RAD_S
        for j in range(KF):
            for i in range(2):
                near = near_x & near_y & (abs(j - RAD_T - i) <= RAD_T)
                out[n, j, :, i, :] = np.where(near, 0.0, -np.inf)
    return out.reshape(9, KR, QR)


def attend_kernel(
    tm_size, table, mask, main, halo, bias_hbm, out_main, out_halo,
    kv, kvt, q, bias, acc, scores, dots, low, res_q, res_kv, slot_of, near_slot, near_off, sem,
):
    me = lax.axis_index("space")
    t = lax.axis_index("tm")
    half = me % 2
    slots = kv.shape[0]
    scaling = HD ** (-0.5)

    @pl.when(me < WORKERS)
    def _():
        loads = [
            pltpu.make_async_copy(
                main.at[:, pl.ds(2 - 2 * half, 4)], kv.at[:, pl.ds(2 - 2 * half, 4)], sem.at[0]
            ),
            pltpu.make_async_copy(halo, kv.at[:, pl.ds(4 * half, 2)], sem.at[1]),
            pltpu.make_async_copy(main.at[:, pl.ds(4 * half, 2)], q, sem.at[2]),
            pltpu.make_async_copy(bias_hbm, bias, sem.at[3]),
        ]
        for load in loads:
            load.start()
        acc[...] = jnp.zeros_like(acc)
        res_q[...] = jnp.zeros_like(res_q)

        def place(s, carry):
            slot_of[table[s]] = s
            return carry

        lax.fori_loop(0, slots, place, 0)
        for load in loads:
            load.wait()

        @pl.when((t == 0) & (half == 0))
        def _():
            bias[:, 0 : 2 * BP, :] = jnp.full((9, 2 * BP, QR), -jnp.inf, jnp.float32)

        @pl.when((t == tm_size - 1) & (half == 1))
        def _():
            bias[:, 4 * BP : 6 * BP, :] = jnp.full((9, 2 * BP, QR), -jnp.inf, jnp.float32)

        def flip(s, carry):
            kvt[s] = kv[s].reshape(KR, 128).T
            return carry

        lax.fori_loop(0, slots, flip, 0)

        def one_block(g, carry):
            @pl.when(mask[g] == 1)
            def _():
                slot = slot_of[g]
                row = g // SIDE
                col = g % SIDE
                count = jnp.int32(0)
                for n in range(9):
                    nr = row + (n // 3 - 1)
                    nc = col + (n % 3 - 1)
                    inside = (nr >= 0) & (nr < SIDE) & (nc >= 0) & (nc < SIDE)
                    nb = jnp.clip(nr, 0, SIDE - 1) * SIDE + jnp.clip(nc, 0, SIDE - 1)
                    valid = inside & (mask[nb] == 1)
                    near_slot[count] = slot_of[nb]
                    near_off[count] = n
                    count = count + valid.astype(jnp.int32)

                rows = q[slot].reshape(QR, 128)
                cols = rows.T
                zero = jnp.zeros_like(cols)
                first = lax.broadcasted_iota(jnp.int32, cols.shape, 0) < HD
                left = lax.broadcasted_iota(jnp.int32, cols.shape, 1) < HD
                rhs_a = jnp.concatenate(
                    [jnp.where(first, cols, zero), jnp.where(first, zero, cols)], axis=1
                )
                rhs_d = jnp.concatenate(
                    [jnp.where(left, rows, zero), jnp.where(left, zero, rows)], axis=0
                )

                def score(k, total):
                    keys = kv[near_slot[k]].reshape(KR, 128)
                    both = jnp.dot(keys, rhs_a, preferred_element_type=jnp.float32)
                    e = jnp.exp(both[:, :QR] * scaling + bias[near_off[k]])
                    scores[k] = e
                    dots[k] = both[:, QR:]
                    return total + jnp.sum(e.reshape(KR // 8, 8, QR), axis=0)

                total = lax.fori_loop(0, count, score, jnp.zeros((8, QR), jnp.float32))
                inverse = 1.0 / jnp.sum(total, axis=0, keepdims=True)

                def weigh(k, out):
                    w = (scores[k] * inverse).astype(jnp.bfloat16)
                    low[k] = w
                    return out + jnp.dot(
                        kvt[near_slot[k], HD:, :], w, preferred_element_type=jnp.float32
                    )

                att = lax.fori_loop(0, count, weigh, jnp.zeros((HD, QR), jnp.float32))
                att = att.astype(jnp.bfloat16).astype(jnp.float32)
                delta = jnp.sum(cols[HD:].astype(jnp.float32) * att, axis=0, keepdims=True)

                def spread_grad(k, out):
                    ds = (scores[k] * inverse * (dots[k] - delta)).astype(jnp.bfloat16)
                    lhs = jnp.concatenate([ds, low[k]], axis=1)
                    acc[near_slot[k]] += jnp.dot(lhs, rhs_d, preferred_element_type=jnp.float32)
                    return out + jnp.dot(
                        kvt[near_slot[k], :HD, :], ds, preferred_element_type=jnp.float32
                    )

                dq = lax.fori_loop(0, count, spread_grad, jnp.zeros((HD, QR), jnp.float32))
                both = jnp.concatenate([dq * scaling, att], axis=0).T
                res_q[slot] = both.astype(jnp.bfloat16).reshape(2, BP, 128)

            return carry

        lax.fori_loop(0, slots, one_block, 0)

        def finish(s, carry):
            total = acc[s]
            res_kv[s] = where_lane(total * scaling, total).astype(jnp.bfloat16).reshape(KF, BP, 128)
            return carry

        lax.fori_loop(0, slots, finish, 0)
        stores = [
            pltpu.make_async_copy(
                res_kv.at[:, pl.ds(2 - 2 * half, 4)], out_main.at[:, pl.ds(2 - 2 * half, 4)], sem.at[0]
            ),
            pltpu.make_async_copy(res_kv.at[:, pl.ds(4 * half, 2)], out_halo, sem.at[1]),
            pltpu.make_async_copy(res_q, out_main.at[:, pl.ds(4 * half, 2)], sem.at[2]),
        ]
        for store in stores:
            store.start()
        for store in stores:
            store.wait()


def attend(block_table, brain_mask, main, halo, tm_size):
    slots = main.shape[0]
    any_spec = pl.BlockSpec(memory_space=ANY)
    smem = pl.BlockSpec(memory_space=pltpu.SMEM)
    return pl.pallas_call(
        functools.partial(attend_kernel, tm_size),
        out_shape=(
            jax.ShapeDtypeStruct((slots, 6, BP, 128), jnp.bfloat16),
            jax.ShapeDtypeStruct((slots, 2, BP, 128), jnp.bfloat16),
        ),
        in_specs=[smem, smem, any_spec, any_spec, any_spec],
        out_specs=(any_spec, any_spec),
        scratch_shapes=[
            pltpu.VMEM((slots, KF, BP, 128), jnp.bfloat16),
            pltpu.VMEM((slots, 128, KR), jnp.bfloat16),
            pltpu.VMEM((slots, 2, BP, 128), jnp.bfloat16),
            pltpu.VMEM((9, KR, QR), jnp.float32),
            pltpu.VMEM((slots, KR, 128), jnp.float32),
            pltpu.VMEM((9, KR, QR), jnp.float32),
            pltpu.VMEM((9, KR, QR), jnp.float32),
            pltpu.VMEM((9, KR, QR), jnp.bfloat16),
            pltpu.VMEM((slots, 2, BP, 128), jnp.bfloat16),
            pltpu.VMEM((slots, KF, BP, 128), jnp.bfloat16),
            pltpu.SMEM((16,), jnp.int32),
            pltpu.SMEM((16,), jnp.int32),
            pltpu.SMEM((16,), jnp.int32),
            pltpu.SemaphoreType.DMA((4,)),
        ],
        compiler_params=pltpu.CompilerParams(vmem_limit_bytes=56 << 20),
        name="attend",
    )(block_table, brain_mask, main, halo, jnp.asarray(window_bias()))


def last_kernel(got_ref, halo_ref, tok_ref, gout_ref, wqkv_ref, tg_ref, terms_ref, grads, att):
    def pair(a, b):
        low = where_lane(a, pltpu.roll(b, HD, 1))
        high = where_lane(pltpu.roll(a, HD, 1), b)
        return low.astype(jnp.bfloat16), high.astype(jnp.bfloat16)

    for i in range(HEADS // 2):
        at = 128 * i
        kvs, qas = [], []
        for h in (2 * i, 2 * i + 1):
            first = got_ref[0, h].astype(jnp.float32)
            second = got_ref[1, h].astype(jnp.float32)
            edge = jnp.concatenate([halo_ref[1, h], halo_ref[0, h]], axis=0).astype(jnp.float32)
            kvs.append((first[2:6] + second[0:4] + edge).reshape(LF * BP, 128))
            qas.append(jnp.concatenate([first[0:2], second[4:6]], axis=0).reshape(LF * BP, 128))
        dk, dv = pair(*kvs)
        dq, da = pair(*qas)
        grads[:, at : at + 128] = dq
        grads[:, HW + at : HW + at + 128] = dk
        grads[:, 2 * HW + at : 2 * HW + at + 128] = dv
        att[:, at : at + 128] = da
    tg_ref[...] = lax.dot_general(
        grads[...], wqkv_ref[...], (((1,), (1,)), ((), ())), preferred_element_type=jnp.float32
    ).astype(jnp.bfloat16)
    tok_t = tok_ref[...].T
    att_t = att[...].T
    for i in range(9):
        terms_ref[768 * i : 768 * (i + 1), :] = jnp.dot(
            tok_t, grads[:, 128 * i : 128 * (i + 1)], preferred_element_type=jnp.float32
        ).astype(terms_ref.dtype)
    for i in range(6):
        terms_ref[6912 + 384 * i : 6912 + 384 * (i + 1), :] = jnp.dot(
            att_t, gout_ref[:, 128 * i : 128 * (i + 1)], preferred_element_type=jnp.float32
        ).astype(terms_ref.dtype)


def last(got, got_halo, tokens, grad_out, w_qkv):
    vmem = pl.BlockSpec(memory_space=pltpu.VMEM)
    return pl.pallas_call(
        last_kernel,
        out_shape=(
            jax.ShapeDtypeStruct((LF * BP, D), jnp.bfloat16),
            jax.ShapeDtypeStruct((9216, 128), jnp.float32),
        ),
        in_specs=[vmem] * 5,
        out_specs=(vmem, vmem),
        scratch_shapes=[
            pltpu.VMEM((LF * BP, 3 * HW), jnp.bfloat16),
            pltpu.VMEM((LF * BP, HW), jnp.bfloat16),
        ],
        compiler_params=pltpu.CompilerParams(vmem_limit_bytes=40 << 20),
        name="last",
    )(got, got_halo, tokens, grad_out, w_qkv)


def shards(tokens, grad_out, w_qkv, w_out, brain_mask, block_table):
    slots = lax.axis_size("space")
    tm_size = lax.axis_size("tm")
    flat_tokens = tokens.reshape(-1, D)
    flat_grad = grad_out.reshape(-1, D)
    packed = project(flat_tokens, flat_grad, w_qkv, w_out)
    main, halo = spread(packed, slots, tm_size)
    main, halo = attend(block_table, brain_mask, main, halo, tm_size)
    got, got_halo = collect(main, halo, slots, tm_size)
    token_grads, terms = last(got, got_halo, flat_tokens, flat_grad, w_qkv)
    terms = lax.psum(terms, ("space", "tm"))
    qkv_grads = terms[:6912].reshape(9, D, 128).transpose(1, 0, 2).reshape(D, 3 * HW)
    out_grads = terms[6912:].reshape(6, HW, 128).transpose(1, 0, 2).reshape(HW, D)
    return (token_grads.reshape(tokens.shape), qkv_grads, out_grads)


def solution(mesh):
    in_specs = (P("space", "tm", None, None), P("space", "tm", None, None), P(), P(), P(), P())
    out_specs = (P("space", "tm", None, None), P(), P())
    return jax.shard_map(shards, mesh=mesh, in_specs=in_specs, out_specs=out_specs, check_vma=False)
```

time: 728 us -> 301 us (0.41); the launches traced: 719 us -> 300 us
  waiting for transfers between devices: 361 us -> 155 us
  local copies, waits for them, and re-layouts: 177 us -> 23.1 us
  Pallas kernels: 0 us -> 108 us
  other arithmetic: 89.4 us -> 0 us
  matrix products: 57.7 us -> 0 us
  starting transfers between devices: 12.9 us -> 0.04 us
    reduce_scatter x2 -> x0, waiting for transfers between devices: 123 us -> none  [the longest x1 82.6 us: shards(): lax.psum_scatter(value_partial, 'space', scatter_dimension=0, tiled=True)]
    pallas_call x0 -> x5, Pallas kernels: none -> 108 us  [the longest x1 41.1 us: spread(): pl.pallas_call(functools.partial(spread_kernel, tm_size), out_shape=(jax....]
    reshape x8 -> x2, local copies, waits for them, and re-layouts: 85.4 us -> 3.66 us  [the longest x1 3.3 us: shards(): terms[:6912].reshape(9, D, 128).transpose(1, 0, 2).reshape(D, 3 * HW)]
    scatter-add x5 -> x0, other arithmetic: 65.9 us -> none  [the longest x2 33 us: shards(): value_partial.at[near_slots[:, None], near_frames[None, :]]]
    all_gather x1 -> x0, waiting for transfers between devices: 62 us -> none  [shards(): gathered = lax.all_gather(framed, 'space', axis=0, tiled=True)]
    dot_general x17 -> x0, matrix products: 57.7 us -> none  [the longest x2 10.3 us: tile_grad(): jnp.einsum('hrk,rhd->khd', weights_low, grad_heads, preferred_element_typ...]
    slice x16 -> x3, local copies, waits for them, and re-layouts: 34.8 us -> 5.29 us  [the longest x1 4.02 us: shards(): terms[:6912].reshape(9, D, 128).transpose(1, 0, 2).reshape(D, 3 * HW)]
    another operation x13 -> x0, local copies, waits for them, and re-layouts: 25.1 us -> none
  transfers between devices with their start and end apart: 8 -> 1, of which waited for: 8 -> 1; matrix products, arithmetic and copies ran while one was open for 8% -> 0% of each run, Pallas kernels for 0% -> 0%
where the time goes in v1:
time: 301 us; the launch traced here: 300 us
  waiting for transfers between devices  155 us (51%)
  Pallas kernels  108 us (36%)
  local copies, waits for them, and re-layouts  23.1 us (8%)
  between operations  14.2 us (5%)
    psum x1, waiting for transfers between devices, shards(): terms = lax.psum(terms, ('space', 'tm'))  155 us
    pallas_call x1, Pallas kernels, spread(): pl.pallas_call(functools.partial(spread_kernel, tm_size), out_shape=(jax....  41.1 us
    pallas_call x1, Pallas kernels, collect(): pl.pallas_call(functools.partial(collect_kernel, slots, tm_size), out_sha...  38.7 us
    pallas_call x1, Pallas kernels, attend(): pl.pallas_call(functools.partial(attend_kernel, tm_size), out_shape=(jax....  25.3 us
    unnamed x24, local copies, waits for them, and re-layouts  14.2 us
  transfers between devices with their start and end apart: 1, of which 1 were waited for; matrix products, arithmetic and copies ran while one was open for 0% of the time, Pallas kernels for 0%

profile of v1, /device:TPU:1, one launch (start us, length us, event | category | flops | bytes accessed | tf_op | source)
XLA Modules:
  0.0 300.4 jit_solution(18023590426464099829)
XLA Ops:
  7.2 0.0 all-reduce.2.cloned.1.call-start
  7.2 0.0 copy-start
  7.2 1.5 copy-done
  8.7 0.0 copy-start.4
  8.7 1.0 copy-done.4
  9.7 0.0 copy-start.6
  9.7 1.0 copy-done.6
  10.7 0.0 copy-start.9
  10.7 1.1 copy-done.9
  11.7 1.0 project.1.src
  12.7 0.0 copy-start.3
  12.7 0.9 copy-done.3
  13.6 41.1 %spread.1 = (bf16[16,6,64,128]{3,2,1,0:T(8,128)(2,1)}, bf16[16,2,64,128]{3,2,1,0:T(8,128)(2,1)}) custom-call(bf16[6,8,64,128]{3,2,1,0:T(8,128)(2,1)} %copy-done.3), custom_call_target="tpu_custom_call" | custom-call | tf_op jit(solution)/shard_map/spread/pallas_call | solution.py:139
  54.7 0.0 copy-start.5
  54.7 0.0 copy-start.7
  54.8 25.3 %attend.1 = (bf16[16,6,64,128]{3,2,1,0:T(8,128)(2,1)}, bf16[16,2,64,128]{3,2,1,0:T(8,128)(2,1)}) custom-call(s32[16]{0:T(128)} %table.1, s32[16]{0:T(128)} %mask.1, bf16[16,6,64,128]{3,2,1,0:T(8,128)(2,1)} %get-tuple-element.11.main, bf16[16,2,64,128]{3,2,1,0:T(8,128)(2,1)} %get-tuple-element.12.halo, f32[9,384,128]{2,1,0:T(8,128)} %constant.2.clone.bias_hbm), custom_call_target="tpu_custom_call" | custom-call | tf_op jit(solution)/shard_map/attend/pallas_call | solution.py:400
  80.0 0.0 copy-start.1
  80.1 38.7 %collect.1 = (bf16[2,6,6,64,128]{4,3,2,1,0:T(8,128)(2,1)}, bf16[2,6,2,64,128]{4,3,2,1,0:T(8,128)(2,1)}) custom-call(bf16[16,6,64,128]{3,2,1,0:T(8,128)(2,1)} %get-tuple-element.13.main, bf16[16,2,64,128]{3,2,1,0:T(8,128)(2,1)} %get-tuple-element.14.halo), custom_call_target="tpu_custom_call" | custom-call | tf_op jit(solution)/shard_map/collect/pallas_call | solution.py:229
  118.8 0.0 copy-done.5
  118.8 0.0 copy-done.7
  118.8 0.0 copy-done.1
  118.8 0.0 copy-start.8
  118.8 1.3 copy-done.8
  120.1 0.0 copy-start.10
  120.1 1.0 copy-done.10
  121.1 2.0 last.1
  123.1 0.0 copy-start.2
  123.1 2.2 copy-done.2
  125.3 0.0 all-reduce.2.cloned.1.call-update
  125.3 154.9 %all-reduce.2.cloned.1.call-done = f32[9216,128]{1,0:T(8,128)} async-done(((f32[9216,128]{1,0:T(8,128)}), f32[9216,128]{1,0:T(8,128)}) %all-reduce.2.cloned.1.call-update) | async-done | bytes 4718608 | tf_op jit(solution)/shard_map/psum | solution.py:494
  280.2 4.0 %slice.8 = f32[6912,128]{1,0:T(8,128)} slice(f32[9216,128]{1,0:T(8,128)} %all-reduce.2.cloned.1.call-done), slice={[0:6912], [0:128]} | slice | bytes 7077888 | tf_op jit(solution)/shard_map/slice | solution.py:495
  284.2 3.3 %copy.12 = f32[9,768,128]{1,2,0:T(8,128)S(1)} copy(f32[9,768,128]{2,1,0:T(8,128)} %bitcast.16) | data formatting | bytes 7077888 | tf_op jit(solution)/shard_map/reshape | solution.py:495
  287.5 2.9 copy.14
  290.5 0.0 slice-start
  290.5 1.3 slice-done
  291.8 0.4 copy.13
  292.1 1.4 copy.15
Async XLA Ops:
  7.2 273.1 %all-reduce.2.cloned.1.call-start = ((), (), s32[]{:S(2)}) async-start(), calls=%async_computation | async-start | bytes 9437184 | tf_op jit(solution)/shard_map/psum | solution.py:494
  7.2 1.5 copy-start
  8.7 1.0 copy-start.4
  9.7 1.0 copy-start.6
  10.7 1.1 copy-start.9
  12.7 0.9 copy-start.3
  54.7 64.0 %copy-start.5 = (bf16[1,4,64,768]{3,2,1,0:T(8,128)(2,1)S(1)}, bf16[1,4,64,768]{3,2,1,0:T(8,128)(2,1)}, u32[]{:S(2)}) copy-start(bf16[1,4,64,768]{3,2,1,0:T(8,128)(2,1)} %param.7) | copy-start | bytes 1179652
  54.7 64.0 %copy-start.7 = (bf16[1,4,64,768]{3,2,1,0:T(8,128)(2,1)S(1)}, bf16[1,4,64,768]{3,2,1,0:T(8,128)(2,1)}, u32[]{:S(2)}) copy-start(bf16[1,4,64,768]{3,2,1,0:T(8,128)(2,1)} %param.8) | copy-start | bytes 1179652
  80.0 38.7 %copy-start.1 = (bf16[768,1152]{1,0:T(8,128)(2,1)S(1)}, bf16[768,1152]{1,0:T(8,128)(2,1)}, u32[]{:S(2)}) copy-start(bf16[768,1152]{1,0:T(8,128)(2,1)} %wqkv_ref.3) | copy-start | bytes 5308420
  118.8 1.3 copy-start.8
  120.1 1.0 copy-start.10
  123.1 2.2 copy-start.2
  290.5 1.3 slice-start
Sparse Core Ops, SparseCore 0:
  125.4 154.7 all-reduce.1

commit v2 on v1

--- a/solution.py
+++ b/solution.py
@@ -468,7 +468,7 @@
         last_kernel,
         out_shape=(
             jax.ShapeDtypeStruct((LF * BP, D), jnp.bfloat16),
-            jax.ShapeDtypeStruct((9216, 128), jnp.float32),
+            jax.ShapeDtypeStruct((9216, 128), jnp.bfloat16),
         ),
         in_specs=[vmem] * 5,
         out_specs=(vmem, vmem),
@@ -481,6 +481,212 @@
     )(got, got_halo, tokens, grad_out, w_qkv)
 
 
+ROWS = 9216
+HALF = ROWS // 2
+GROUP = 8
+CHUNK = HALF // GROUP
+PIECE = CHUNK // GROUP
+
+
+def sum_kernel(src, out, b0, hs, b1, s1, b2, b3, ss0, r0, ss1, r1, ss2, r2, ss3, r3, ss4, r4, ss5, r5):
+    s = lax.axis_index("space")
+    t = lax.axis_index("tm")
+    core = s % 2
+    chip = s // 2
+    rank1 = (1 - core) * chip + core * t
+    rank2 = (1 - core) * t + core * chip
+    base = core * HALF
+    far = HALF - base
+    sibling = {"space": s + 1 - 2 * core, "tm": t}
+
+    def peer1(i):
+        return {"space": (1 - core) * (2 * i + core) + core * s, "tm": (1 - core) * t + core * i}
+
+    def peer2(j):
+        return {"space": core * (2 * j + core) + (1 - core) * s, "tm": core * t + (1 - core) * j}
+
+    def remote(a, b, send, recv, device):
+        return pltpu.make_async_remote_copy(
+            src_ref=a, dst_ref=b, send_sem=send, recv_sem=recv,
+            device_id=device, device_id_type=pl.DeviceIdType.MESH,
+        )
+
+    def rows(start, index):
+        return pl.ds(pl.multiple_of(start + index * CHUNK, CHUNK), CHUNK)
+
+    barrier = pltpu.get_barrier_semaphore()
+    pl.semaphore_signal(barrier, inc=1, device_id=sibling, device_id_type=pl.DeviceIdType.MESH)
+
+    def greet(n, carry):
+        i = (rank1 + n) % GROUP
+        j = (rank2 + n) % GROUP
+        pl.semaphore_signal(barrier, inc=1, device_id=peer1(i), device_id_type=pl.DeviceIdType.MESH)
+        pl.semaphore_signal(barrier, inc=1, device_id=peer2(j), device_id_type=pl.DeviceIdType.MESH)
+        return carry
+
+    lax.fori_loop(1, GROUP, greet, 0)
+    pl.semaphore_wait(barrier, 2 * GROUP - 1)
+
+    def copy0(k):
+        return remote(src.at[rows(far, k)], b0.at[k], ss0.at[k], r0.at[k], sibling)
+
+    def copy1(i, slot):
+        return remote(hs.at[i], b1.at[slot], ss1.at[i], r1.at[slot], peer1(i))
+
+    def copy2(j, slot):
+        return remote(s1.at[j], b2.at[slot], ss2.at[j], r2.at[slot], peer2(j))
+
+    def copy3(j, slot):
+        return remote(b3.at[slot], b3.at[slot], ss3.at[j], r3.at[slot], peer2(j))
+
+    def copy4(i, chunk):
+        return remote(
+            out.at[rows(base, chunk)], out.at[rows(base, chunk)], ss4.at[i], r4.at[chunk], peer1(i)
+        )
+
+    def copy5(chunk, start):
+        return remote(
+            out.at[rows(start, chunk)], out.at[rows(start, chunk)], ss5.at[chunk], r5.at[chunk], sibling
+        )
+
+    def start0(n, carry):
+        copy0((rank2 + 1 + n) % GROUP).start()
+        return carry
+
+    lax.fori_loop(0, GROUP, start0, 0)
+
+    def stage0(n, carry):
+        i = (rank1 + n) % GROUP
+        copy0(i).wait_recv()
+        hs[i] = (
+            src[rows(base, i), :].astype(jnp.float32) + b0[i].astype(jnp.float32)
+        ).astype(jnp.bfloat16)
+        copy1(i, rank1).start()
+        return carry
+
+    lax.fori_loop(1, GROUP, stage0, 0)
+    copy0(rank1).wait_recv()
+    own = src[rows(base, rank1), :].astype(jnp.float32) + b0[rank1].astype(jnp.float32)
+    s1[...] = own.reshape(GROUP, PIECE, 128)
+
+    def stage1(n, carry):
+        i = (rank1 + GROUP - n) % GROUP
+        copy1(i, i).wait_recv()
+        s1[...] += b1[i].astype(jnp.float32).reshape(GROUP, PIECE, 128)
+        return carry
+
+    lax.fori_loop(1, GROUP, stage1, 0)
+
+    def start2(n, carry):
+        copy2((rank2 + n) % GROUP, rank2).start()
+        return carry
+
+    lax.fori_loop(1, GROUP, start2, 0)
+    b3[rank2] = s1[rank2]
+
+    def stage2(n, carry):
+        j = (rank2 + GROUP - n) % GROUP
+        copy2(j, j).wait_recv()
+        b3[rank2] += b2[j]
+        return carry
+
+    lax.fori_loop(1, GROUP, stage2, 0)
+
+    def start3(n, carry):
+        copy3((rank2 + n) % GROUP, rank2).start()
+        return carry
+
+    lax.fori_loop(1, GROUP, start3, 0)
+
+    def stage3(n, carry):
+        j = (rank2 + GROUP - n) % GROUP
+        copy3(j, j).wait_recv()
+        return carry
+
+    lax.fori_loop(1, GROUP, stage3, 0)
+    out[rows(base, rank1), :] = b3[...].reshape(CHUNK, 128).astype(jnp.bfloat16)
+
+    def start4(n, carry):
+        copy4((rank1 + n) % GROUP, rank1).start()
+        return carry
+
+    lax.fori_loop(1, GROUP, start4, 0)
+    copy5(rank1, base).start()
+
+    def stage4(n, carry):
+        i = (rank1 + GROUP - n) % GROUP
+        copy4(i, i).wait_recv()
+        copy5(i, base).start()
+        return carry
+
+    lax.fori_loop(1, GROUP, stage4, 0)
+
+    def stage5(n, carry):
+        copy5(n, far).wait_recv()
+        copy5(n, base).wait_send()
+        copy0(n).wait_send()
+        return carry
+
+    lax.fori_loop(0, GROUP, stage5, 0)
+
+    def done(n, carry):
+        i = (rank1 + n) % GROUP
+        j = (rank2 + n) % GROUP
+        copy1(i, rank1).wait_send()
+        copy2(j, rank2).wait_send()
+        copy3(j, rank2).wait_send()
+        copy4(i, rank1).wait_send()
+        return carry
+
+    lax.fori_loop(1, GROUP, done, 0)
+
+
+def sum_all(terms):
+    vmem = pl.BlockSpec(memory_space=pltpu.VMEM)
+    return pl.pallas_call(
+        sum_kernel,
+        out_shape=jax.ShapeDtypeStruct((ROWS, 128), jnp.bfloat16),
+        in_specs=[vmem],
+        out_specs=vmem,
+        scratch_shapes=[
+            pltpu.VMEM((GROUP, CHUNK, 128), jnp.bfloat16),
+            pltpu.VMEM((GROUP, CHUNK, 128), jnp.bfloat16),
+            pltpu.VMEM((GROUP, CHUNK, 128), jnp.bfloat16),
+            pltpu.VMEM((GROUP, PIECE, 128), jnp.float32),
+            pltpu.VMEM((GROUP, PIECE, 128), jnp.float32),
+            pltpu.VMEM((GROUP, PIECE, 128), jnp.float32),
+        ]
+        + [pltpu.SemaphoreType.DMA((GROUP,))] * 12,
+        compiler_params=pltpu.CompilerParams(
+            has_side_effects=True, collective_id=3, vmem_limit_bytes=32 << 20
+        ),
+        name="sum_all",
+    )(terms)
+
+
+def widen_kernel(src, qkv, out):
+    for i in range(9):
+        qkv[:, 128 * i : 128 * (i + 1)] = src[D * i : D * (i + 1), :].astype(jnp.float32)
+    for i in range(6):
+        start = 9 * D + HW * i
+        out[:, 128 * i : 128 * (i + 1)] = src[start : start + HW, :].astype(jnp.float32)
+
+
+def widen(terms):
+    vmem = pl.BlockSpec(memory_space=pltpu.VMEM)
+    return pl.pallas_call(
+        widen_kernel,
+        out_shape=(
+            jax.ShapeDtypeStruct((D, 3 * HW), jnp.float32),
+            jax.ShapeDtypeStruct((HW, D), jnp.float32),
+        ),
+        in_specs=[vmem],
+        out_specs=(vmem, vmem),
+        compiler_params=pltpu.CompilerParams(vmem_limit_bytes=32 << 20),
+        name="widen",
+    )(terms)
+
+
 def shards(tokens, grad_out, w_qkv, w_out, brain_mask, block_table):
     slots = lax.axis_size("space")
     tm_size = lax.axis_size("tm")
@@ -491,9 +697,7 @@
     main, halo = attend(block_table, brain_mask, main, halo, tm_size)
     got, got_halo = collect(main, halo, slots, tm_size)
     token_grads, terms = last(got, got_halo, flat_tokens, flat_grad, w_qkv)
-    terms = lax.psum(terms, ("space", "tm"))
-    qkv_grads = terms[:6912].reshape(9, D, 128).transpose(1, 0, 2).reshape(D, 3 * HW)
-    out_grads = terms[6912:].reshape(6, HW, 128).transpose(1, 0, 2).reshape(HW, D)
+    qkv_grads, out_grads = widen(sum_all(terms))
     return (token_grads.reshape(tokens.shape), qkv_grads, out_grads)
 
 

time: 301 us -> 181 us (0.60)
  waiting for transfers between devices: 155 us -> 0 us
  Pallas kernels: 108 us -> 172 us
  local copies, waits for them, and re-layouts: 23.1 us -> 7.68 us
  between operations: 14.2 us -> 0.75 us
    psum x1 -> x0, waiting for transfers between devices: 155 us -> none  [shards(): terms = lax.psum(terms, ('space', 'tm'))]
    pallas_call x0 -> x2, Pallas kernels: none -> 49.1 us  [the longest x1 46.7 us: sum_all(): pl.pallas_call(sum_kernel, out_shape=jax.ShapeDtypeStruct((ROWS, 128), jn...]
    pallas_call x1, Pallas kernels: 25.3 us -> 40 us  [attend(): pl.pallas_call(functools.partial(attend_kernel, tm_size), out_shape=(jax....]
    unnamed x24 -> x20, local copies, waits for them, and re-layouts: 14.2 us -> 7.68 us
    slice x3 -> x0, local copies, waits for them, and re-layouts: 5.29 us -> none  [the longest x1 4.02 us: shards(): terms[:6912].reshape(9, D, 128).transpose(1, 0, 2).reshape(D, 3 * HW)]
    reshape x2 -> x0, local copies, waits for them, and re-layouts: 3.66 us -> none  [the longest x1 3.3 us: shards(): terms[:6912].reshape(9, D, 128).transpose(1, 0, 2).reshape(D, 3 * HW)]
  transfers between devices with their start and end apart: 1 -> 0, of which waited for: 1 -> 0; matrix products, arithmetic and copies ran while one was open for 0% -> 0% of each run, Pallas kernels for 0% -> 0%
where the time goes in v2:
time: 181 us
  Pallas kernels  172 us (95%)
  local copies, waits for them, and re-layouts  7.68 us (4%)
    pallas_call x1, Pallas kernels, sum_all(): pl.pallas_call(sum_kernel, out_shape=jax.ShapeDtypeStruct((ROWS, 128), jn...  46.7 us
    pallas_call x1, Pallas kernels, spread(): pl.pallas_call(functools.partial(spread_kernel, tm_size), out_shape=(jax....  41.1 us
    pallas_call x1, Pallas kernels, attend(): pl.pallas_call(functools.partial(attend_kernel, tm_size), out_shape=(jax....  40 us
    pallas_call x1, Pallas kernels, collect(): pl.pallas_call(functools.partial(collect_kernel, slots, tm_size), out_sha...  38.7 us
    unnamed x20, local copies, waits for them, and re-layouts  7.68 us

profile of v2, /device:TPU:1, one launch (start us, length us, event | category | flops | bytes accessed | tf_op | source)
XLA Modules:
  0.0 180.8 jit_solution(6548504117072086998)
XLA Ops:
  0.6 0.0 copy-start
  0.6 1.5 copy-done
  2.1 0.0 copy-start.3
  2.1 1.0 copy-done.3
  3.1 0.0 copy-start.5
  3.1 1.0 copy-done.5
  4.1 0.0 copy-start.8
  4.1 1.1 copy-done.8
  5.2 1.0 project.1.src
  6.1 0.0 copy-start.2
  6.1 0.9 copy-done.2
  7.0 41.1 %spread.1 = (bf16[16,6,64,128]{3,2,1,0:T(8,128)(2,1)}, bf16[16,2,64,128]{3,2,1,0:T(8,128)(2,1)}) custom-call(bf16[6,8,64,128]{3,2,1,0:T(8,128)(2,1)} %copy-done.2), custom_call_target="tpu_custom_call" | custom-call | tf_op jit(solution)/shard_map/spread/pallas_call | solution.py:139
  48.1 0.0 copy-start.4
  48.2 0.0 copy-start.6
  48.2 40.0 %attend.1 = (bf16[16,6,64,128]{3,2,1,0:T(8,128)(2,1)}, bf16[16,2,64,128]{3,2,1,0:T(8,128)(2,1)}) custom-call(s32[16]{0:T(128)} %table.1, s32[16]{0:T(128)} %mask.1, bf16[16,6,64,128]{3,2,1,0:T(8,128)(2,1)} %get-tuple-element.13.main, bf16[16,2,64,128]{3,2,1,0:T(8,128)(2,1)} %get-tuple-element.14.halo, f32[9,384,128]{2,1,0:T(8,128)} %constant.2.clone.bias_hbm), custom_call_target="tpu_custom_call" | custom-call | tf_op jit(solution)/shard_map/attend/pallas_call | solution.py:400
  88.2 0.0 copy-start.1
  88.2 38.7 %collect.1 = (bf16[2,6,6,64,128]{4,3,2,1,0:T(8,128)(2,1)}, bf16[2,6,2,64,128]{4,3,2,1,0:T(8,128)(2,1)}) custom-call(bf16[16,6,64,128]{3,2,1,0:T(8,128)(2,1)} %get-tuple-element.15.main, bf16[16,2,64,128]{3,2,1,0:T(8,128)(2,1)} %get-tuple-element.16.halo), custom_call_target="tpu_custom_call" | custom-call | tf_op jit(solution)/shard_map/collect/pallas_call | solution.py:229
  126.9 0.0 copy-done.4
  126.9 0.0 copy-done.6
  126.9 0.0 copy-done.1
  126.9 0.0 copy-start.7
  127.0 1.3 copy-done.7
  128.2 0.0 copy-start.9
  128.2 1.0 copy-done.9
  129.2 2.5 %last.1 = (bf16[256,768]{1,0:T(8,128)(2,1)}, bf16[9216,128]{1,0:T(8,128)(2,1)S(1)}) custom-call(bf16[2,6,6,64,128]{4,3,2,1,0:T(8,128)(2,1)S(1)} %copy-done.7, bf16[2,6,2,64,128]{4,3,2,1,0:T(8,128)(2,1)S(1)} %copy-done.9, bf16[256,768]{1,0:T(8,128)(2,1)S(1)} %bitcast.4, bf16[256,768]{1,0:T(8,128)(2,1)S(1)} %bitcast.6, bf16[768,1152]{1,0:T(8,128)(2,1)S(1)} %copy-done.1), custom_call_target="tpu_custom_call" | custom-call | tf_op jit(solution)/shard_map/last/pallas_call | solution.py:467
  131.7 46.7 %sum_all.1.src = bf16[9216,128]{1,0:T(8,128)(2,1)S(1)} custom-call(bf16[9216,128]{1,0:T(8,128)(2,1)S(1)} %get-tuple-element.20.src), custom_call_target="tpu_custom_call" | custom-call | tf_op jit(solution)/shard_map/sum_all/pallas_call | solution.py:646
  178.4 2.4 %widen.1 = (f32[768,1152]{1,0:T(8,128)}, f32[384,768]{1,0:T(8,128)}) custom-call(bf16[9216,128]{1,0:T(8,128)(2,1)S(1)} %sum_all.1.src), custom_call_target="tpu_custom_call" | custom-call | tf_op jit(solution)/shard_map/widen/pallas_call | solution.py:677
Async XLA Ops:
  0.6 1.5 copy-start
  2.1 1.0 copy-start.3
  3.1 1.0 copy-start.5
  4.1 1.1 copy-start.8
  6.1 0.9 copy-start.2
  48.1 78.8 %copy-start.4 = (bf16[1,4,64,768]{3,2,1,0:T(8,128)(2,1)S(1)}, bf16[1,4,64,768]{3,2,1,0:T(8,128)(2,1)}, u32[]{:S(2)}) copy-start(bf16[1,4,64,768]{3,2,1,0:T(8,128)(2,1)} %param.7) | copy-start | bytes 1179652
  48.2 78.8 %copy-start.6 = (bf16[1,4,64,768]{3,2,1,0:T(8,128)(2,1)S(1)}, bf16[1,4,64,768]{3,2,1,0:T(8,128)(2,1)}, u32[]{:S(2)}) copy-start(bf16[1,4,64,768]{3,2,1,0:T(8,128)(2,1)} %param.8) | copy-start | bytes 1179652
  88.2 38.8 %copy-start.1 = (bf16[768,1152]{1,0:T(8,128)(2,1)S(1)}, bf16[768,1152]{1,0:T(8,128)(2,1)}, u32[]{:S(2)}) copy-start(bf16[768,1152]{1,0:T(8,128)(2,1)} %wqkv_ref.3) | copy-start | bytes 5308420
  126.9 1.3 copy-start.7
  128.2 1.0 copy-start.9

commit v3 on v1

--- a/solution.py
+++ b/solution.py
@@ -29,11 +29,68 @@
     return jnp.where(lane < HD, low, high)
 
 
-def project_kernel(tok_ref, gout_ref, wqkv_ref, wout_ref, out_ref):
-    proj = jnp.dot(tok_ref[...], wqkv_ref[...], preferred_element_type=jnp.float32)
+MESH = pl.DeviceIdType.MESH
+
+
+def worker_space(w):
+    return w + (w // 8) * (w - 8)
+
+
+def worker_of(space):
+    return 1 - (space // 8) * (space % 2), space - (space // 8) * ((space - 8) // 2)
+
+
+def signal(semaphore, space, tm):
+    pl.semaphore_signal(semaphore, inc=1, device_id={"space": space, "tm": tm}, device_id_type=MESH)
+
+
+def remote(src, dst, send, recv, device):
+    return pltpu.make_async_remote_copy(
+        src_ref=src, dst_ref=dst, send_sem=send, recv_sem=recv, device_id=device, device_id_type=MESH
+    )
+
+
+def spread_kernel(
+    slots, tm_size, tok_hbm, gout_hbm, wqkv_hbm, wout_hbm, main, halo,
+    tok, gout, wqkv, wout, packed, lsem, ssem, hsem, rsem, rhsem,
+):
+    me = lax.axis_index("space")
+    t = lax.axis_index("tm")
+    after = lax.rem(t + 1, tm_size)
+    before = lax.rem(t + tm_size - 1, tm_size)
+    is_worker, worker = worker_of(me)
+    loads = [
+        pltpu.make_async_copy(wqkv_hbm, wqkv, lsem.at[0]),
+        pltpu.make_async_copy(tok_hbm, tok, lsem.at[1]),
+        pltpu.make_async_copy(wout_hbm, wout, lsem.at[2]),
+        pltpu.make_async_copy(gout_hbm, gout, lsem.at[3]),
+    ]
+    for load in loads:
+        load.start()
+
+    barrier = pltpu.get_barrier_semaphore()
+
+    @pl.when(is_worker == 1)
+    def _():
+        half = worker % 2
+        source = lax.rem(t + tm_size - 1 + 2 * half, tm_size)
+
+        def greet(i, carry):
+            signal(barrier, lax.rem(me + i, slots), t)
+            return carry
+
+        def greet_halo(i, carry):
+            signal(barrier, i, source)
+            return carry
+
+        lax.fori_loop(1, slots, greet, 0)
+        lax.fori_loop(0, slots, greet_halo, 0)
+
+    for load in loads:
+        load.wait()
+    proj = jnp.dot(tok[...], wqkv[...], preferred_element_type=jnp.float32)
     gatt = lax.dot_general(
-        gout_ref[...], wout_ref[...], (((1,), (1,)), ((), ())),
-        preferred_element_type=jnp.float32,
+        gout[...], wout[...], (((1,), (1,)), ((), ())), preferred_element_type=jnp.float32
     )
 
     def pair(low, high):
@@ -46,60 +103,35 @@
         keys = pair(proj[:, HW + at : HW + at + 128], proj[:, 2 * HW + at : 2 * HW + at + 128])
         queries = pair(proj[:, at : at + 128], gatt[:, at : at + 128])
         for j in range(2):
-            out_ref[2 * i + j, 0:2] = queries[j][0:2]
-            out_ref[2 * i + j, 2:6] = keys[j]
-            out_ref[2 * i + j, 6:8] = queries[j][2:4]
-
-
-def project(tokens, grad_out, w_qkv, w_out):
-    vmem = pl.BlockSpec(memory_space=pltpu.VMEM)
-    return pl.pallas_call(
-        project_kernel,
-        out_shape=jax.ShapeDtypeStruct((HEADS, 8, BP, 128), jnp.bfloat16),
-        in_specs=[vmem] * 4,
-        out_specs=vmem,
-        compiler_params=pltpu.CompilerParams(vmem_limit_bytes=40 << 20),
-        name="project",
-    )(tokens, grad_out, w_qkv, w_out)
-
-
-def spread_kernel(tm_size, src, main, halo, ssem, hsem, rsem, rhsem):
-    me = lax.axis_index("space")
-    t = lax.axis_index("tm")
-    after = lax.rem(t + 1, tm_size)
-    before = lax.rem(t + tm_size - 1, tm_size)
+            packed[2 * i + j, 0:2] = queries[j][0:2]
+            packed[2 * i + j, 2:6] = keys[j]
+            packed[2 * i + j, 6:8] = queries[j][2:4]
+
+    pl.semaphore_wait(barrier, 2 * WORKERS - is_worker)
 
     def main_copy(w):
-        return pltpu.make_async_remote_copy(
-            src_ref=src.at[w // 2, pl.ds(2 * (w % 2), 6)],
-            dst_ref=main.at[me],
-            send_sem=ssem.at[w],
-            recv_sem=rsem,
-            device_id={"space": w, "tm": t},
-            device_id_type=pl.DeviceIdType.MESH,
+        return remote(
+            packed.at[w // 2, pl.ds(2 * (w % 2), 6)], main.at[me], ssem.at[w], rsem,
+            {"space": worker_space(w), "tm": t},
         )
 
     def halo_copy(h, half):
-        return pltpu.make_async_remote_copy(
-            src_ref=src.at[h, pl.ds(4 - 2 * half, 2)],
-            dst_ref=halo.at[me],
-            send_sem=hsem.at[2 * h + half],
-            recv_sem=rhsem,
-            device_id={"space": 2 * h + half, "tm": before if half else after},
-            device_id_type=pl.DeviceIdType.MESH,
+        return remote(
+            packed.at[h, pl.ds(4 - 2 * half, 2)], halo.at[me], hsem.at[2 * h + half], rhsem,
+            {"space": worker_space(2 * h + half), "tm": before if half else after},
         )
 
     def send(i, carry):
         w = lax.rem(i + me, WORKERS)
 
-        @pl.when(w != me)
+        @pl.when(worker_space(w) != me)
         def _():
             main_copy(w).start()
 
-        @pl.when(w == me)
+        @pl.when(worker_space(w) == me)
         def _():
             pltpu.make_async_copy(
-                src.at[w // 2, pl.ds(2 * (w % 2), 6)], main.at[me], rsem
+                packed.at[w // 2, pl.ds(2 * (w % 2), 6)], main.at[me], rsem
             ).start()
 
         return carry
@@ -114,7 +146,7 @@
     lax.fori_loop(0, WORKERS, send, 0)
 
     def finish(w, carry):
-        @pl.when(w != me)
+        @pl.when(worker_space(w) != me)
         def _():
             main_copy(w).wait_send()
 
@@ -125,7 +157,7 @@
         halo_copy(h, 1).wait_send()
         return carry
 
-    @pl.when(me < WORKERS)
+    @pl.when(is_worker == 1)
     def _():
         pltpu.make_async_copy(halo, halo, rhsem).wait()
         pltpu.make_async_copy(main, main, rsem).wait()
@@ -134,115 +166,33 @@
     lax.fori_loop(0, WORKERS, finish, 0)
 
 
-def spread(packed, slots, tm_size):
+def spread(tokens, grad_out, w_qkv, w_out, slots, tm_size):
     any_spec = pl.BlockSpec(memory_space=ANY)
     return pl.pallas_call(
-        functools.partial(spread_kernel, tm_size),
+        functools.partial(spread_kernel, slots, tm_size),
         out_shape=(
             jax.ShapeDtypeStruct((slots, 6, BP, 128), jnp.bfloat16),
             jax.ShapeDtypeStruct((slots, 2, BP, 128), jnp.bfloat16),
         ),
-        in_specs=[any_spec],
+        in_specs=[any_spec] * 4,
         out_specs=(any_spec, any_spec),
         scratch_shapes=[
+            pltpu.VMEM(tokens.shape, jnp.bfloat16),
+            pltpu.VMEM(grad_out.shape, jnp.bfloat16),
+            pltpu.VMEM(w_qkv.shape, jnp.bfloat16),
+            pltpu.VMEM(w_out.shape, jnp.bfloat16),
+            pltpu.VMEM((HEADS, 8, BP, 128), jnp.bfloat16),
+            pltpu.SemaphoreType.DMA((4,)),
             pltpu.SemaphoreType.DMA((WORKERS,)),
             pltpu.SemaphoreType.DMA((WORKERS,)),
             pltpu.SemaphoreType.DMA,
             pltpu.SemaphoreType.DMA,
         ],
-        compiler_params=pltpu.CompilerParams(has_side_effects=True),
+        compiler_params=pltpu.CompilerParams(
+            has_side_effects=True, collective_id=1, vmem_limit_bytes=60 << 20
+        ),
         name="spread",
-    )(packed)
-
-
-def collect_kernel(slots, tm_size, main, halo, got, got_halo, ssem, hsem, rsem, rhsem):
-    me = lax.axis_index("space")
-    t = lax.axis_index("tm")
-    head = me // 2
-    half = me % 2
-    other = lax.rem(t + tm_size + 2 * half - 1, tm_size)
-
-    def main_copy(s):
-        return pltpu.make_async_remote_copy(
-            src_ref=main.at[s],
-            dst_ref=got.at[half, head],
-            send_sem=ssem.at[s],
-            recv_sem=rsem,
-            device_id={"space": s, "tm": t},
-            device_id_type=pl.DeviceIdType.MESH,
-        )
-
-    def halo_copy(s):
-        return pltpu.make_async_remote_copy(
-            src_ref=halo.at[s],
-            dst_ref=got_halo.at[half, head],
-            send_sem=hsem.at[s],
-            recv_sem=rhsem,
-            device_id={"space": s, "tm": other},
-            device_id_type=pl.DeviceIdType.MESH,
-        )
-
-    def send(i, carry):
-        s = lax.rem(i + me, slots)
-
-        @pl.when(s != me)
-        def _():
-            main_copy(s).start()
-
-        @pl.when(s == me)
-        def _():
-            pltpu.make_async_copy(main.at[s], got.at[half, head], rsem).start()
-
-        return carry
-
-    def send_halo(i, carry):
-        halo_copy(lax.rem(i + me, slots)).start()
-        return carry
-
-    def finish(s, carry):
-        @pl.when(s != me)
-        def _():
-            main_copy(s).wait_send()
-
-        return carry
-
-    def finish_halo(s, carry):
-        halo_copy(s).wait_send()
-        return carry
-
-    @pl.when(me < WORKERS)
-    def _():
-        lax.fori_loop(0, slots, send_halo, 0)
-        lax.fori_loop(0, slots, send, 0)
-
-    pltpu.make_async_copy(got_halo, got_halo, rhsem).wait()
-    pltpu.make_async_copy(got, got, rsem).wait()
-
-    @pl.when(me < WORKERS)
-    def _():
-        lax.fori_loop(0, slots, finish_halo, 0)
-        lax.fori_loop(0, slots, finish, 0)
-
-
-def collect(main, halo, slots, tm_size):
-    any_spec = pl.BlockSpec(memory_space=ANY)
-    return pl.pallas_call(
-        functools.partial(collect_kernel, slots, tm_size),
-        out_shape=(
-            jax.ShapeDtypeStruct((2, HEADS, 6, BP, 128), jnp.bfloat16),
-            jax.ShapeDtypeStruct((2, HEADS, 2, BP, 128), jnp.bfloat16),
-        ),
-        in_specs=[any_spec, any_spec],
-        out_specs=(any_spec, any_spec),
-        scratch_shapes=[
-            pltpu.SemaphoreType.DMA((slots,)),
-            pltpu.SemaphoreType.DMA((slots,)),
-            pltpu.SemaphoreType.DMA,
-            pltpu.SemaphoreType.DMA,
-        ],
-        compiler_params=pltpu.CompilerParams(has_side_effects=True),
-        name="collect",
-    )(main, halo)
+    )(tokens, grad_out, w_qkv, w_out)
 
 
 def window_bias():
@@ -266,11 +216,12 @@
 ):
     me = lax.axis_index("space")
     t = lax.axis_index("tm")
-    half = me % 2
+    is_worker, worker = worker_of(me)
+    half = worker % 2
     slots = kv.shape[0]
     scaling = HD ** (-0.5)
 
-    @pl.when(me < WORKERS)
+    @pl.when(is_worker == 1)
     def _():
         loads = [
             pltpu.make_async_copy(
@@ -426,7 +377,123 @@
     )(block_table, brain_mask, main, halo, jnp.asarray(window_bias()))
 
 
-def last_kernel(got_ref, halo_ref, tok_ref, gout_ref, wqkv_ref, tg_ref, terms_ref, grads, att):
+ROWS = 9216
+HALF = ROWS // 2
+PART = 576
+PARTS = HALF // PART
+PIECE = 72
+FIRST = (8, 4)
+SECOND = (8, 16)
+
+
+def finish_kernel(
+    slots, tm_size, main, halo, tok_hbm, gout_hbm, wqkv_hbm, tg_ref, out,
+    got, got_halo, tok, gout, wqkv, grads, att, src, b0, hs, b1, s1, b2, b3,
+    lsem, cs, ch, cr, crh, ss0, r0, ss1, r1, ss2, r2, ss3, r3, ss4, r4, ss5, r5,
+):
+    s = lax.axis_index("space")
+    t = lax.axis_index("tm")
+    core = s % 2
+    chip = s // 2
+    is_worker, worker = worker_of(s)
+    head = worker // 2
+    half = worker % 2
+    other = lax.rem(t + tm_size + 2 * half - 1, tm_size)
+    after = lax.rem(t + 1, tm_size)
+    before = lax.rem(t + tm_size - 1, tm_size)
+    sibling = {"space": s + 1 - 2 * core, "tm": t}
+
+    def rank1(c):
+        return t // 2 if c else chip
+
+    def rank2(c):
+        return 2 * chip + t % 2 if c else t
+
+    def peer1(c, i):
+        return {"space": s, "tm": 2 * i + t % 2} if c else {"space": 2 * i, "tm": t}
+
+    def peer2(c, j):
+        return {"space": 2 * (j // 2) + 1, "tm": 2 * (t // 2) + j % 2} if c else {"space": s, "tm": j}
+
+    loads = [
+        pltpu.make_async_copy(tok_hbm, tok, lsem.at[0]),
+        pltpu.make_async_copy(gout_hbm, gout, lsem.at[1]),
+        pltpu.make_async_copy(wqkv_hbm, wqkv, lsem.at[2]),
+    ]
+    for load in loads:
+        load.start()
+
+    barrier = pltpu.get_barrier_semaphore()
+
+    def greet(i, carry):
+        w = lax.rem(i + s, WORKERS)
+
+        @pl.when(worker_space(w) != s)
+        def _():
+            signal(barrier, worker_space(w), t)
+
+        signal(barrier, worker_space(w), (1 - w % 2) * after + (w % 2) * before)
+        return carry
+
+    lax.fori_loop(0, WORKERS, greet, 0)
+    signal(barrier, sibling["space"], t)
+    for c in range(2):
+
+        @pl.when(core == c)
+        def _(c=c):
+            def greet1(n, carry):
+                peer = peer1(c, (rank1(c) + n) % FIRST[c])
+                signal(barrier, peer["space"], peer["tm"])
+                return carry
+
+            def greet2(n, carry):
+                peer = peer2(c, (rank2(c) + n) % SECOND[c])
+                signal(barrier, peer["space"], peer["tm"])
+                return carry
+
+            lax.fori_loop(1, FIRST[c], greet1, 0)
+            lax.fori_loop(1, SECOND[c], greet2, 0)
+
+    pl.semaphore_wait(barrier, is_worker * (2 * slots - 1) + 15 + 4 * core)
+
+    def main_copy(i):
+        return remote(
+            main.at[i], got.at[half, head], cs.at[i], cr, {"space": i, "tm": t}
+        )
+
+    def halo_copy(i):
+        return remote(
+            halo.at[i], got_halo.at[half, head], ch.at[i], crh, {"space": i, "tm": other}
+        )
+
+    @pl.when(is_worker == 1)
+    def _():
+        def send_halo(i, carry):
+            halo_copy(lax.rem(i + s, slots)).start()
+            return carry
+
+        def send(i, carry):
+            to = lax.rem(i + s, slots)
+
+            @pl.when(to != s)
+            def _():
+                main_copy(to).start()
+
+            @pl.when(to == s)
+            def _():
+                pltpu.make_async_copy(main.at[to], got.at[half, head], cr).start()
+
+            return carry
+
+        lax.fori_loop(0, slots, send_halo, 0)
+        lax.fori_loop(0, slots, send, 0)
+
+    for load in loads:
+        load.wait()
+    tok_t = tok[...].T
+    pltpu.make_async_copy(got_halo, got_halo, crh).wait()
+    pltpu.make_async_copy(got, got, cr).wait()
+
     def pair(a, b):
         low = where_lane(a, pltpu.roll(b, HD, 1))
         high = where_lane(pltpu.roll(a, HD, 1), b)
@@ -436,49 +503,257 @@
         at = 128 * i
         kvs, qas = [], []
         for h in (2 * i, 2 * i + 1):
-            first = got_ref[0, h].astype(jnp.float32)
-            second = got_ref[1, h].astype(jnp.float32)
-            edge = jnp.concatenate([halo_ref[1, h], halo_ref[0, h]], axis=0).astype(jnp.float32)
-            kvs.append((first[2:6] + second[0:4] + edge).reshape(LF * BP, 128))
-            qas.append(jnp.concatenate([first[0:2], second[4:6]], axis=0).reshape(LF * BP, 128))
+            low = got[0, h].astype(jnp.float32)
+            high = got[1, h].astype(jnp.float32)
+            edge = jnp.concatenate([got_halo[1, h], got_halo[0, h]], axis=0).astype(jnp.float32)
+            kvs.append((low[2:6] + high[0:4] + edge).reshape(LF * BP, 128))
+            qas.append(jnp.concatenate([low[0:2], high[4:6]], axis=0).reshape(LF * BP, 128))
         dk, dv = pair(*kvs)
         dq, da = pair(*qas)
         grads[:, at : at + 128] = dq
         grads[:, HW + at : HW + at + 128] = dk
         grads[:, 2 * HW + at : 2 * HW + at + 128] = dv
         att[:, at : at + 128] = da
-    tg_ref[...] = lax.dot_general(
-        grads[...], wqkv_ref[...], (((1,), (1,)), ((), ())), preferred_element_type=jnp.float32
-    ).astype(jnp.bfloat16)
-    tok_t = tok_ref[...].T
+    for i in range(9):
+        src[D * i : D * (i + 1), :] = jnp.dot(
+            tok_t, grads[:, 128 * i : 128 * (i + 1)], preferred_element_type=jnp.float32
+        ).astype(jnp.bfloat16)
     att_t = att[...].T
+    for i in range(6):
+        start = 9 * D + HW * i
+        src[start : start + HW, :] = jnp.dot(
+            att_t, gout[:, 128 * i : 128 * (i + 1)], preferred_element_type=jnp.float32
+        ).astype(jnp.bfloat16)
+
+    def token_grads():
+        tg_ref[...] = lax.dot_general(
+            grads[...], wqkv[...], (((1,), (1,)), ((), ())), preferred_element_type=jnp.float32
+        ).astype(jnp.bfloat16)
+
+    def sum_all(c):
+        first, second = FIRST[c], SECOND[c]
+        length = HALF // first
+        parts = PARTS // first
+        base = c * HALF
+        far = HALF - base
+        here1, here2 = rank1(c), rank2(c)
+
+        def part(k):
+            return pl.ds(pl.multiple_of(k * PART, PART), PART)
+
+        def rows(start, index, size):
+            return pl.ds(pl.multiple_of(start + index * size, PART), size)
+
+        def copy0(k):
+            return remote(src.at[rows(far, k, PART)], b0.at[part(k)], ss0.at[k], r0.at[k], sibling)
+
+        def copy1(i, slot):
+            return remote(
+                hs.at[rows(0, i, length)], b1.at[rows(0, slot, length)], ss1.at[i], r1.at[slot],
+                peer1(c, i),
+            )
+
+        def copy2(j, slot):
+            return remote(s1.at[j], b2.at[slot], ss2.at[j], r2.at[slot], peer2(c, j))
+
+        def copy3(j, slot):
+            return remote(b3.at[slot], b3.at[slot], ss3.at[j], r3.at[slot], peer2(c, j))
+
+        def copy4(i, chunk):
+            where = rows(base, chunk, length)
+            return remote(out.at[where], out.at[where], ss4.at[i], r4.at[chunk], peer1(c, i))
+
+        def copy5(chunk):
+            where = rows(base, chunk, length)
+            return remote(out.at[where], out.at[where], ss5.at[chunk], r5.at[chunk], sibling)
+
+        def from_sibling(chunk):
+            where = rows(far, chunk, HALF // FIRST[1 - c])
+            return remote(out.at[where], out.at[where], ss5.at[chunk], r5.at[chunk], sibling)
+
+        begin = ((rank1(1 - c) + 1) % FIRST[1 - c]) * (PARTS // FIRST[1 - c])
+
+        def start0(n, carry):
+            copy0((begin + n) % PARTS).start()
+            return carry
+
+        lax.fori_loop(0, PARTS, start0, 0)
+        token_grads()
+
+        def both(k):
+            copy0(k).wait_recv()
+            return src[rows(base, k, PART), :].astype(jnp.float32) + b0[part(k), :].astype(jnp.float32)
+
+        def stage0(n, carry):
+            i = (here1 + n) % first
+            for p in range(parts):
+                hs[part(i * parts + p), :] = both(i * parts + p).astype(jnp.bfloat16)
+            copy1(i, here1).start()
+            return carry
+
+        lax.fori_loop(1, first, stage0, 0)
+        pieces = PART // PIECE
+        for p in range(parts):
+            s1[p * pieces : (p + 1) * pieces] = both(here1 * parts + p).reshape(pieces, PIECE, 128)
+
+        def stage1(n, carry):
+            i = (here1 + first - n) % first
+            copy1(i, i).wait_recv()
+            s1[0:second] += b1[rows(0, i, length), :].astype(jnp.float32).reshape(second, PIECE, 128)
+            return carry
+
+        lax.fori_loop(1, first, stage1, 0)
+
+        def start2(n, carry):
+            copy2((here2 + n) % second, here2).start()
+            return carry
+
+        lax.fori_loop(1, second, start2, 0)
+        b3[here2] = s1[here2]
+
+        def stage2(n, carry):
+            j = (here2 + second - n) % second
+            copy2(j, j).wait_recv()
+            b3[here2] += b2[j]
+            return carry
+
+        lax.fori_loop(1, second, stage2, 0)
+
+        def start3(n, carry):
+            copy3((here2 + n) % second, here2).start()
+            return carry
+
+        lax.fori_loop(1, second, start3, 0)
+
+        def stage3(n, carry):
+            j = (here2 + second - n) % second
+            copy3(j, j).wait_recv()
+            return carry
+
+        lax.fori_loop(1, second, stage3, 0)
+        out[rows(base, here1, length), :] = b3[0:second].reshape(length, 128).astype(jnp.bfloat16)
+
+        def start4(n, carry):
+            copy4((here1 + n) % first, here1).start()
+            return carry
+
+        lax.fori_loop(1, first, start4, 0)
+        copy5(here1).start()
+
+        def stage4(n, carry):
+            i = (here1 + first - n) % first
+            copy4(i, i).wait_recv()
+            copy5(i).start()
+            return carry
+
+        lax.fori_loop(1, first, stage4, 0)
+
+        def stage5(n, carry):
+            from_sibling(n).wait_recv()
+            return carry
+
+        lax.fori_loop(0, FIRST[1 - c], stage5, 0)
+
+        def sent0(n, carry):
+            copy0(n).wait_send()
+            return carry
+
+        lax.fori_loop(0, PARTS, sent0, 0)
+
+        def sent1(n, carry):
+            i = (here1 + n) % first
+            copy1(i, here1).wait_send()
+            copy4(i, here1).wait_send()
+            copy5(i).wait_send()
+            return carry
+
+        lax.fori_loop(1, first, sent1, 0)
+        copy5(here1).wait_send()
+
+        def sent2(n, carry):
+            j = (here2 + n) % second
+            copy2(j, here2).wait_send()
+            copy3(j, here2).wait_send()
+            return carry
+
+        lax.fori_loop(1, second, sent2, 0)
+
+    for c in range(2):
+        pl.when(core == c)(functools.partial(sum_all, c))
+
+    @pl.when(is_worker == 1)
+    def _():
+        def finish(i, carry):
+            halo_copy(i).wait_send()
+
+            @pl.when(i != s)
+            def _():
+                main_copy(i).wait_send()
+
+            return carry
+
+        lax.fori_loop(0, slots, finish, 0)
+
+
+def finish(main, halo, tokens, grad_out, w_qkv, slots, tm_size):
+    any_spec = pl.BlockSpec(memory_space=ANY)
+    vmem = pl.BlockSpec(memory_space=pltpu.VMEM)
+    dma = pltpu.SemaphoreType.DMA
+    return pl.pallas_call(
+        functools.partial(finish_kernel, slots, tm_size),
+        out_shape=(
+            jax.ShapeDtypeStruct((LF * BP, D), jnp.bfloat16),
+            jax.ShapeDtypeStruct((ROWS, 128), jnp.bfloat16),
+        ),
+        in_specs=[any_spec] * 5,
+        out_specs=(vmem, vmem),
+        scratch_shapes=[
+            pltpu.VMEM((2, HEADS, 6, BP, 128), jnp.bfloat16),
+            pltpu.VMEM((2, HEADS, 2, BP, 128), jnp.bfloat16),
+            pltpu.VMEM(tokens.shape, jnp.bfloat16),
+            pltpu.VMEM(grad_out.shape, jnp.bfloat16),
+            pltpu.VMEM(w_qkv.shape, jnp.bfloat16),
+            pltpu.VMEM((LF * BP, 3 * HW), jnp.bfloat16),
+            pltpu.VMEM((LF * BP, HW), jnp.bfloat16),
+            pltpu.VMEM((ROWS, 128), jnp.bfloat16),
+            pltpu.VMEM((HALF, 128), jnp.bfloat16),
+            pltpu.VMEM((HALF, 128), jnp.bfloat16),
+            pltpu.VMEM((HALF, 128), jnp.bfloat16),
+            pltpu.VMEM((16, PIECE, 128), jnp.float32),
+            pltpu.VMEM((16, PIECE, 128), jnp.float32),
+            pltpu.VMEM((16, PIECE, 128), jnp.float32),
+            dma((3,)), dma((slots,)), dma((slots,)), dma, dma,
+            dma((8,)), dma((8,)), dma((8,)), dma((8,)), dma((16,)), dma((16,)),
+            dma((16,)), dma((16,)), dma((8,)), dma((8,)), dma((8,)), dma((8,)),
+        ],
+        compiler_params=pltpu.CompilerParams(
+            has_side_effects=True, collective_id=2, vmem_limit_bytes=60 << 20
+        ),
+        name="finish",
+    )(main, halo, tokens, grad_out, w_qkv)
+
+
+def widen_kernel(src, qkv, out):
     for i in range(9):
-        terms_ref[768 * i : 768 * (i + 1), :] = jnp.dot(
-            tok_t, grads[:, 128 * i : 128 * (i + 1)], preferred_element_type=jnp.float32
-        ).astype(terms_ref.dtype)
+        qkv[:, 128 * i : 128 * (i + 1)] = src[D * i : D * (i + 1), :].astype(jnp.float32)
     for i in range(6):
-        terms_ref[6912 + 384 * i : 6912 + 384 * (i + 1), :] = jnp.dot(
-            att_t, gout_ref[:, 128 * i : 128 * (i + 1)], preferred_element_type=jnp.float32
-        ).astype(terms_ref.dtype)
-
-
-def last(got, got_halo, tokens, grad_out, w_qkv):
+        start = 9 * D + HW * i
+        out[:, 128 * i : 128 * (i + 1)] = src[start : start + HW, :].astype(jnp.float32)
+
+
+def widen(terms):
     vmem = pl.BlockSpec(memory_space=pltpu.VMEM)
     return pl.pallas_call(
-        last_kernel,
+        widen_kernel,
         out_shape=(
-            jax.ShapeDtypeStruct((LF * BP, D), jnp.bfloat16),
-            jax.ShapeDtypeStruct((9216, 128), jnp.float32),
+            jax.ShapeDtypeStruct((D, 3 * HW), jnp.float32),
+            jax.ShapeDtypeStruct((HW, D), jnp.float32),
         ),
-        in_specs=[vmem] * 5,
+        in_specs=[vmem],
         out_specs=(vmem, vmem),
-        scratch_shapes=[
-            pltpu.VMEM((LF * BP, 3 * HW), jnp.bfloat16),
-            pltpu.VMEM((LF * BP, HW), jnp.bfloat16),
-        ],
-        compiler_params=pltpu.CompilerParams(vmem_limit_bytes=40 << 20),
-        name="last",
-    )(got, got_halo, tokens, grad_out, w_qkv)
+        compiler_params=pltpu.CompilerParams(vmem_limit_bytes=32 << 20),
+        name="widen",
+    )(terms)
 
 
 def shards(tokens, grad_out, w_qkv, w_out, brain_mask, block_table):
@@ -486,14 +761,10 @@
     tm_size = lax.axis_size("tm")
     flat_tokens = tokens.reshape(-1, D)
     flat_grad = grad_out.reshape(-1, D)
-    packed = project(flat_tokens, flat_grad, w_qkv, w_out)
-    main, halo = spread(packed, slots, tm_size)
+    main, halo = spread(flat_tokens, flat_grad, w_qkv, w_out, slots, tm_size)
     main, halo = attend(block_table, brain_mask, main, halo, tm_size)
-    got, got_halo = collect(main, halo, slots, tm_size)
-    token_grads, terms = last(got, got_halo, flat_tokens, flat_grad, w_qkv)
-    terms = lax.psum(terms, ("space", "tm"))
-    qkv_grads = terms[:6912].reshape(9, D, 128).transpose(1, 0, 2).reshape(D, 3 * HW)
-    out_grads = terms[6912:].reshape(6, HW, 128).transpose(1, 0, 2).reshape(HW, D)
+    token_grads, terms = finish(main, halo, flat_tokens, flat_grad, w_qkv, slots, tm_size)
+    qkv_grads, out_grads = widen(terms)
     return (token_grads.reshape(tokens.shape), qkv_grads, out_grads)
 
 

time: 301 us -> 139 us (0.46)
  waiting for transfers between devices: 155 us -> 0 us
  Pallas kernels: 108 us -> 134 us
  local copies, waits for them, and re-layouts: 23.1 us -> 2.41 us
  between operations: 14.2 us -> 0.66 us
    psum x1 -> x0, waiting for transfers between devices: 155 us -> none  [shards(): terms = lax.psum(terms, ('space', 'tm'))]
    pallas_call x4 -> x3, Pallas kernels: 82.8 us -> 110 us  [the longest x1 73.7 us: finish(): pl.pallas_call(functools.partial(finish_kernel, slots, tm_size), out_shap...]
    unnamed x24 -> x5, local copies, waits for them, and re-layouts: 14.2 us -> 2.41 us
    slice x3 -> x0, local copies, waits for them, and re-layouts: 5.29 us -> none  [the longest x1 4.02 us: shards(): terms[:6912].reshape(9, D, 128).transpose(1, 0, 2).reshape(D, 3 * HW)]
    reshape x2 -> x0, local copies, waits for them, and re-layouts: 3.66 us -> none  [the longest x1 3.3 us: shards(): terms[:6912].reshape(9, D, 128).transpose(1, 0, 2).reshape(D, 3 * HW)]
  transfers between devices with their start and end apart: 1 -> 0, of which waited for: 1 -> 0; matrix products, arithmetic and copies ran while one was open for 0% -> 0% of each run, Pallas kernels for 0% -> 0%
where the time goes in v3:
time: 139 us; the launch traced here: 137 us
  Pallas kernels  134 us (96%)
  local copies, waits for them, and re-layouts  2.41 us (2%)
    pallas_call x1, Pallas kernels, finish(): pl.pallas_call(functools.partial(finish_kernel, slots, tm_size), out_shap...  73.7 us
    pallas_call x1, Pallas kernels, spread(): pl.pallas_call(functools.partial(spread_kernel, slots, tm_size), out_shap...  34.1 us
    pallas_call x1, Pallas kernels, attend(): pl.pallas_call(functools.partial(attend_kernel, tm_size), out_shape=(jax....  24 us

profile of v3, /device:TPU:1, one launch (start us, length us, event | category | flops | bytes accessed | tf_op | source)
XLA Modules:
  0.0 137.2 jit_solution(3371038815503139629)
XLA Ops:
  0.6 34.1 %spread.1 = (bf16[16,6,64,128]{3,2,1,0:T(8,128)(2,1)}, bf16[16,2,64,128]{3,2,1,0:T(8,128)(2,1)}) custom-call(bf16[256,768]{1,0:T(8,128)(2,1)} %bitcast.3, bf16[256,768]{1,0:T(8,128)(2,1)} %bitcast.5, bf16[768,1152]{1,0:T(8,128)(2,1)} %wqkv_hbm.3, bf16[384,768]{1,0:T(8,128)(2,1)} %wout_hbm.1), custom_call_target="tpu_custom_call" | custom-call | tf_op jit(solution)/shard_map/spread/pallas_call | solution.py:171
  34.7 24.0 %attend.1 = (bf16[16,6,64,128]{3,2,1,0:T(8,128)(2,1)}, bf16[16,2,64,128]{3,2,1,0:T(8,128)(2,1)}) custom-call(s32[16]{0:T(128)} %table.1, s32[16]{0:T(128)} %mask.1, bf16[16,6,64,128]{3,2,1,0:T(8,128)(2,1)} %get-tuple-element.11.main, bf16[16,2,64,128]{3,2,1,0:T(8,128)(2,1)} %get-tuple-element.12.halo, f32[9,384,128]{2,1,0:T(8,128)} %constant.2.clone.bias_hbm), custom_call_target="tpu_custom_call" | custom-call | tf_op jit(solution)/shard_map/attend/pallas_call | solution.py:351
  58.7 73.7 %finish.1 = (bf16[256,768]{1,0:T(8,128)(2,1)}, bf16[9216,128]{1,0:T(8,128)(2,1)}) custom-call(bf16[16,6,64,128]{3,2,1,0:T(8,128)(2,1)} %get-tuple-element.13.main, bf16[16,2,64,128]{3,2,1,0:T(8,128)(2,1)} %get-tuple-element.14.halo, bf16[256,768]{1,0:T(8,128)(2,1)} %bitcast.4, bf16[256,768]{1,0:T(8,128)(2,1)} %bitcast.6, bf16[768,1152]{1,0:T(8,128)(2,1)} %wqkv_hbm.3), custom_call_target="tpu_custom_call" | custom-call | tf_op jit(solution)/shard_map/finish/pallas_call | solution.py:702
  132.4 0.0 copy-start
  132.4 1.7 %copy-done = bf16[9216,128]{1,0:T(8,128)(2,1)S(1)} copy-done((bf16[9216,128]{1,0:T(8,128)(2,1)S(1)}, bf16[9216,128]{1,0:T(8,128)(2,1)}, u32[]{:S(2)}) %copy-start) | copy-done | bytes 2359320
  134.1 0.0 copy-start.1
  134.1 2.4 %widen.1 = (f32[768,1152]{1,0:T(8,128)}, f32[384,768]{1,0:T(8,128)}) custom-call(bf16[9216,128]{1,0:T(8,128)(2,1)S(1)} %copy-done), custom_call_target="tpu_custom_call" | custom-call | tf_op jit(solution)/shard_map/widen/pallas_call | solution.py:746
  136.5 0.0 copy-done.1
  136.5 0.7 copy.11
Async XLA Ops:
  132.4 1.7 %copy-start = (bf16[9216,128]{1,0:T(8,128)(2,1)S(1)}, bf16[9216,128]{1,0:T(8,128)(2,1)}, u32[]{:S(2)}) copy-start(bf16[9216,128]{1,0:T(8,128)(2,1)} %get-tuple-element.16.src) | copy-start | bytes 7077892
  134.1 2.4 %copy-start.1 = (bf16[256,768]{1,0:T(8,128)(2,1)S(1)}, bf16[256,768]{1,0:T(8,128)(2,1)}, u32[]{:S(2)}) copy-start(bf16[256,768]{1,0:T(8,128)(2,1)} %get-tuple-element.15) | copy-start | bytes 1179652

commit v4 on v3

--- a/solution.py
+++ b/solution.py
@@ -51,8 +51,8 @@
 
 
 def spread_kernel(
-    slots, tm_size, tok_hbm, gout_hbm, wqkv_hbm, wout_hbm, main, halo,
-    tok, gout, wqkv, wout, packed, lsem, ssem, hsem, rsem, rhsem,
+    slots, tm_size, tok_hbm, gout_hbm, wqkv_hbm, wout_hbm, q, kv,
+    tok, gout, wqkv, wout, qpack, kpack, lsem, qsem, ssem, hsem, rqsem, rsem,
 ):
     me = lax.axis_index("space")
     t = lax.axis_index("tm")
@@ -103,21 +103,29 @@
         keys = pair(proj[:, HW + at : HW + at + 128], proj[:, 2 * HW + at : 2 * HW + at + 128])
         queries = pair(proj[:, at : at + 128], gatt[:, at : at + 128])
         for j in range(2):
-            packed[2 * i + j, 0:2] = queries[j][0:2]
-            packed[2 * i + j, 2:6] = keys[j]
-            packed[2 * i + j, 6:8] = queries[j][2:4]
+            qpack[2 * i + j] = queries[j]
+            kpack[2 * i + j] = keys[j]
 
     pl.semaphore_wait(barrier, 2 * WORKERS - is_worker)
 
-    def main_copy(w):
-        return remote(
-            packed.at[w // 2, pl.ds(2 * (w % 2), 6)], main.at[me], ssem.at[w], rsem,
-            {"space": worker_space(w), "tm": t},
-        )
+    def query_refs(w):
+        return qpack.at[w // 2, pl.ds(2 * (w % 2), 2)], q.at[me]
+
+    def key_refs(w):
+        return kpack.at[w // 2], kv.at[me, pl.ds(2 - 2 * (w % 2), 4)]
+
+    def query_copy(w):
+        src, dst = query_refs(w)
+        return remote(src, dst, qsem.at[w], rqsem, {"space": worker_space(w), "tm": t})
+
+    def key_copy(w):
+        src, dst = key_refs(w)
+        return remote(src, dst, ssem.at[w], rsem, {"space": worker_space(w), "tm": t})
 
     def halo_copy(h, half):
         return remote(
-            packed.at[h, pl.ds(4 - 2 * half, 2)], halo.at[me], hsem.at[2 * h + half], rhsem,
+            kpack.at[h, pl.ds(2 - 2 * half, 2)], kv.at[me, pl.ds(4 * half, 2)],
+            hsem.at[2 * h + half], rsem,
             {"space": worker_space(2 * h + half), "tm": before if half else after},
         )
 
@@ -126,13 +134,15 @@
 
         @pl.when(worker_space(w) != me)
         def _():
-            main_copy(w).start()
+            key_copy(w).start()
+            query_copy(w).start()
 
         @pl.when(worker_space(w) == me)
         def _():
-            pltpu.make_async_copy(
-                packed.at[w // 2, pl.ds(2 * (w % 2), 6)], main.at[me], rsem
-            ).start()
+            src, dst = key_refs(w)
+            pltpu.make_async_copy(src, dst, rsem).start()
+            src, dst = query_refs(w)
+            pltpu.make_async_copy(src, dst, rqsem).start()
 
         return carry
 
@@ -148,7 +158,8 @@
     def finish(w, carry):
         @pl.when(worker_space(w) != me)
         def _():
-            main_copy(w).wait_send()
+            key_copy(w).wait_send()
+            query_copy(w).wait_send()
 
         return carry
 
@@ -159,8 +170,8 @@
 
     @pl.when(is_worker == 1)
     def _():
-        pltpu.make_async_copy(halo, halo, rhsem).wait()
-        pltpu.make_async_copy(main, main, rsem).wait()
+        pltpu.make_async_copy(kv, kv, rsem).wait()
+        pltpu.make_async_copy(q, q, rqsem).wait()
 
     lax.fori_loop(0, HEADS, finish_halo, 0)
     lax.fori_loop(0, WORKERS, finish, 0)
@@ -168,37 +179,45 @@
 
 def spread(tokens, grad_out, w_qkv, w_out, slots, tm_size):
     any_spec = pl.BlockSpec(memory_space=ANY)
+    vmem = pl.BlockSpec(memory_space=pltpu.VMEM)
     return pl.pallas_call(
         functools.partial(spread_kernel, slots, tm_size),
         out_shape=(
-            jax.ShapeDtypeStruct((slots, 6, BP, 128), jnp.bfloat16),
             jax.ShapeDtypeStruct((slots, 2, BP, 128), jnp.bfloat16),
+            jax.ShapeDtypeStruct((slots, KF, BP, 128), jnp.bfloat16),
         ),
         in_specs=[any_spec] * 4,
-        out_specs=(any_spec, any_spec),
+        out_specs=(vmem, vmem),
         scratch_shapes=[
             pltpu.VMEM(tokens.shape, jnp.bfloat16),
             pltpu.VMEM(grad_out.shape, jnp.bfloat16),
             pltpu.VMEM(w_qkv.shape, jnp.bfloat16),
             pltpu.VMEM(w_out.shape, jnp.bfloat16),
-            pltpu.VMEM((HEADS, 8, BP, 128), jnp.bfloat16),
+            pltpu.VMEM((HEADS, LF, BP, 128), jnp.bfloat16),
+            pltpu.VMEM((HEADS, LF, BP, 128), jnp.bfloat16),
             pltpu.SemaphoreType.DMA((4,)),
+            pltpu.SemaphoreType.DMA((WORKERS,)),
             pltpu.SemaphoreType.DMA((WORKERS,)),
             pltpu.SemaphoreType.DMA((WORKERS,)),
             pltpu.SemaphoreType.DMA,
             pltpu.SemaphoreType.DMA,
         ],
         compiler_params=pltpu.CompilerParams(
-            has_side_effects=True, collective_id=1, vmem_limit_bytes=60 << 20
+            has_side_effects=True, collective_id=1, vmem_limit_bytes=28 << 20
         ),
         name="spread",
     )(tokens, grad_out, w_qkv, w_out)
 
 
+UNROLL = 8
+MOST = 12
+PAIRS = 72
+
+
 def window_bias():
     patch = np.arange(BP)
     px, py = patch // 16, patch // 4 % 4
-    out = np.zeros((9, KF, BP, 2, BP), np.float32)
+    out = np.full((10, KF, BP, 2, BP), -np.inf, np.float32)
     for n in range(9):
         dr, dc = n // 3 - 1, n % 3 - 1
         near_x = np.abs(px[:, None] + 4 * dr - px[None, :]) <= RAD_S
@@ -207,12 +226,13 @@
             for i in range(2):
                 near = near_x & near_y & (abs(j - RAD_T - i) <= RAD_T)
                 out[n, j, :, i, :] = np.where(near, 0.0, -np.inf)
-    return out.reshape(9, KR, QR)
+    return out.reshape(10, KR, QR)
 
 
 def attend_kernel(
-    tm_size, table, mask, main, halo, bias_hbm, out_main, out_halo,
-    kv, kvt, q, bias, acc, scores, dots, low, res_q, res_kv, slot_of, near_slot, near_off, sem,
+    tm_size, table, mask, q, kv, bias_hbm, res_q, res_kv,
+    kvt, bias, acc, scores, dots, low, rhs_a, rhs_d, total, inverse, delta, att, dq,
+    slot_of, brain, pair_q, pair_k, pair_off, sem,
 ):
     me = lax.axis_index("space")
     t = lax.axis_index("tm")
@@ -223,158 +243,186 @@
 
     @pl.when(is_worker == 1)
     def _():
-        loads = [
-            pltpu.make_async_copy(
-                main.at[:, pl.ds(2 - 2 * half, 4)], kv.at[:, pl.ds(2 - 2 * half, 4)], sem.at[0]
-            ),
-            pltpu.make_async_copy(halo, kv.at[:, pl.ds(4 * half, 2)], sem.at[1]),
-            pltpu.make_async_copy(main.at[:, pl.ds(4 * half, 2)], q, sem.at[2]),
-            pltpu.make_async_copy(bias_hbm, bias, sem.at[3]),
-        ]
-        for load in loads:
-            load.start()
+        load = pltpu.make_async_copy(bias_hbm, bias, sem)
+        load.start()
+
+        def place(s, carry):
+            slot_of[table[s]] = s
+            return carry
+
+        lax.fori_loop(0, slots, place, 0)
+
+        def list_block(g, carry):
+            blocks, pairs = carry
+            inside_brain = mask[g] == 1
+            slot = slot_of[g]
+            brain[blocks] = slot
+            row = g // SIDE
+            col = g % SIDE
+            for n in range(9):
+                nr = row + (n // 3 - 1)
+                nc = col + (n % 3 - 1)
+                inside = (nr >= 0) & (nr < SIDE) & (nc >= 0) & (nc < SIDE)
+                nb = jnp.clip(nr, 0, SIDE - 1) * SIDE + jnp.clip(nc, 0, SIDE - 1)
+                valid = inside_brain & inside & (mask[nb] == 1)
+                pair_q[pairs] = slot
+                pair_k[pairs] = slot_of[nb]
+                pair_off[pairs] = n
+                pairs = jnp.minimum(pairs + valid.astype(jnp.int32), PAIRS)
+            return (blocks + inside_brain.astype(jnp.int32), pairs)
+
+        blocks, pairs = lax.fori_loop(0, slots, list_block, (jnp.int32(0), jnp.int32(0)))
+        for n in range(UNROLL):
+            pair_q[pairs + n] = brain[0]
+            pair_k[pairs + n] = brain[0]
+            pair_off[pairs + n] = 9
+        steps = (pairs + (UNROLL - 1)) // UNROLL
+
         acc[...] = jnp.zeros_like(acc)
         res_q[...] = jnp.zeros_like(res_q)
-
-        def place(s, carry):
-            slot_of[table[s]] = s
-            return carry
-
-        lax.fori_loop(0, slots, place, 0)
-        for load in loads:
-            load.wait()
+        total[...] = jnp.zeros_like(total)
+        att[...] = jnp.zeros_like(att)
+        dq[...] = jnp.zeros_like(dq)
+
+        def prepare(b, carry):
+            slot = brain[b]
+            kvt[slot] = kv[slot].reshape(KR, 128).T
+            rows = q[slot].reshape(QR, 128)
+            cols = rows.T
+            zero = jnp.zeros_like(cols)
+            first = lax.broadcasted_iota(jnp.int32, cols.shape, 0) < HD
+            left = lax.broadcasted_iota(jnp.int32, cols.shape, 1) < HD
+            rhs_a[slot, :, :QR] = jnp.where(first, cols * scaling, zero)
+            rhs_a[slot, :, QR:] = jnp.where(first, zero, cols)
+            rhs_d[slot, :QR, :] = jnp.where(left, rows, zero)
+            rhs_d[slot, QR:, :] = jnp.where(left, zero, rows)
+            return carry
+
+        lax.fori_loop(0, blocks, prepare, 0)
+        load.wait()
 
         @pl.when((t == 0) & (half == 0))
         def _():
-            bias[:, 0 : 2 * BP, :] = jnp.full((9, 2 * BP, QR), -jnp.inf, jnp.float32)
+            bias[:, 0 : 2 * BP, :] = jnp.full((10, 2 * BP, QR), -jnp.inf, jnp.float32)
 
         @pl.when((t == tm_size - 1) & (half == 1))
         def _():
-            bias[:, 4 * BP : 6 * BP, :] = jnp.full((9, 2 * BP, QR), -jnp.inf, jnp.float32)
-
-        def flip(s, carry):
-            kvt[s] = kv[s].reshape(KR, 128).T
-            return carry
-
-        lax.fori_loop(0, slots, flip, 0)
-
-        def one_block(g, carry):
-            @pl.when(mask[g] == 1)
-            def _():
-                slot = slot_of[g]
-                row = g // SIDE
-                col = g % SIDE
-                count = jnp.int32(0)
-                for n in range(9):
-                    nr = row + (n // 3 - 1)
-                    nc = col + (n % 3 - 1)
-                    inside = (nr >= 0) & (nr < SIDE) & (nc >= 0) & (nc < SIDE)
-                    nb = jnp.clip(nr, 0, SIDE - 1) * SIDE + jnp.clip(nc, 0, SIDE - 1)
-                    valid = inside & (mask[nb] == 1)
-                    near_slot[count] = slot_of[nb]
-                    near_off[count] = n
-                    count = count + valid.astype(jnp.int32)
-
-                rows = q[slot].reshape(QR, 128)
-                cols = rows.T
-                zero = jnp.zeros_like(cols)
-                first = lax.broadcasted_iota(jnp.int32, cols.shape, 0) < HD
-                left = lax.broadcasted_iota(jnp.int32, cols.shape, 1) < HD
-                rhs_a = jnp.concatenate(
-                    [jnp.where(first, cols, zero), jnp.where(first, zero, cols)], axis=1
+            bias[:, 4 * BP : 6 * BP, :] = jnp.full((10, 2 * BP, QR), -jnp.inf, jnp.float32)
+
+        def by_rows(x):
+            return x.reshape(KR // 8, 8, QR)
+
+        def score(step, carry):
+            for u in range(UNROLL):
+                p = step * UNROLL + u
+                keys = kv[pair_k[p]].reshape(KR, 128)
+                both = jnp.dot(keys, rhs_a[pair_q[p]], preferred_element_type=jnp.float32)
+                e = jnp.exp(both[:, :QR] + bias[pair_off[p]])
+                scores[p] = e
+                dots[p] = both[:, QR:]
+                total[pair_q[p]] += jnp.sum(by_rows(e), axis=0)
+            return carry
+
+        lax.fori_loop(0, steps, score, 0)
+
+        def invert(b, carry):
+            slot = brain[b]
+            whole = jnp.sum(total[slot], axis=0, keepdims=True)
+            inverse[slot] = jnp.broadcast_to(1.0 / whole, (8, QR))
+            return carry
+
+        lax.fori_loop(0, blocks, invert, 0)
+
+        def weigh(step, carry):
+            for u in range(UNROLL):
+                p = step * UNROLL + u
+                w = by_rows(scores[p]) * inverse[pair_q[p]][None]
+                w = w.reshape(KR, QR).astype(jnp.bfloat16)
+                low[p] = w
+                att[pair_q[p]] += jnp.dot(
+                    kvt[pair_k[p], HD:, :], w, preferred_element_type=jnp.float32
                 )
-                rhs_d = jnp.concatenate(
-                    [jnp.where(left, rows, zero), jnp.where(left, zero, rows)], axis=0
-                )
-
-                def score(k, total):
-                    keys = kv[near_slot[k]].reshape(KR, 128)
-                    both = jnp.dot(keys, rhs_a, preferred_element_type=jnp.float32)
-                    e = jnp.exp(both[:, :QR] * scaling + bias[near_off[k]])
-                    scores[k] = e
-                    dots[k] = both[:, QR:]
-                    return total + jnp.sum(e.reshape(KR // 8, 8, QR), axis=0)
-
-                total = lax.fori_loop(0, count, score, jnp.zeros((8, QR), jnp.float32))
-                inverse = 1.0 / jnp.sum(total, axis=0, keepdims=True)
-
-                def weigh(k, out):
-                    w = (scores[k] * inverse).astype(jnp.bfloat16)
-                    low[k] = w
-                    return out + jnp.dot(
-                        kvt[near_slot[k], HD:, :], w, preferred_element_type=jnp.float32
-                    )
-
-                att = lax.fori_loop(0, count, weigh, jnp.zeros((HD, QR), jnp.float32))
-                att = att.astype(jnp.bfloat16).astype(jnp.float32)
-                delta = jnp.sum(cols[HD:].astype(jnp.float32) * att, axis=0, keepdims=True)
-
-                def spread_grad(k, out):
-                    ds = (scores[k] * inverse * (dots[k] - delta)).astype(jnp.bfloat16)
-                    lhs = jnp.concatenate([ds, low[k]], axis=1)
-                    acc[near_slot[k]] += jnp.dot(lhs, rhs_d, preferred_element_type=jnp.float32)
-                    return out + jnp.dot(
-                        kvt[near_slot[k], :HD, :], ds, preferred_element_type=jnp.float32
-                    )
-
-                dq = lax.fori_loop(0, count, spread_grad, jnp.zeros((HD, QR), jnp.float32))
-                both = jnp.concatenate([dq * scaling, att], axis=0).T
-                res_q[slot] = both.astype(jnp.bfloat16).reshape(2, BP, 128)
-
-            return carry
-
-        lax.fori_loop(0, slots, one_block, 0)
-
-        def finish(s, carry):
-            total = acc[s]
-            res_kv[s] = where_lane(total * scaling, total).astype(jnp.bfloat16).reshape(KF, BP, 128)
-            return carry
-
-        lax.fori_loop(0, slots, finish, 0)
-        stores = [
-            pltpu.make_async_copy(
-                res_kv.at[:, pl.ds(2 - 2 * half, 4)], out_main.at[:, pl.ds(2 - 2 * half, 4)], sem.at[0]
-            ),
-            pltpu.make_async_copy(res_kv.at[:, pl.ds(4 * half, 2)], out_halo, sem.at[1]),
-            pltpu.make_async_copy(res_q, out_main.at[:, pl.ds(4 * half, 2)], sem.at[2]),
-        ]
-        for store in stores:
-            store.start()
-        for store in stores:
-            store.wait()
-
-
-def attend(block_table, brain_mask, main, halo, tm_size):
-    slots = main.shape[0]
-    any_spec = pl.BlockSpec(memory_space=ANY)
+            return carry
+
+        lax.fori_loop(0, steps, weigh, 0)
+
+        def rest(b, carry):
+            slot = brain[b]
+            rounded = att[slot].astype(jnp.bfloat16).astype(jnp.float32)
+            att[slot] = rounded
+            grad = rhs_a[slot, HD:, QR:].astype(jnp.float32)
+            one = jnp.sum(grad * rounded, axis=0, keepdims=True)
+            delta[slot] = jnp.broadcast_to(one, (8, QR))
+            return carry
+
+        lax.fori_loop(0, blocks, rest, 0)
+
+        def spread_grad(step, carry):
+            for u in range(UNROLL):
+                p = step * UNROLL + u
+                qs = pair_q[p]
+                ds = by_rows(scores[p]) * inverse[qs][None] * (by_rows(dots[p]) - delta[qs][None])
+                ds = ds.reshape(KR, QR).astype(jnp.bfloat16)
+                lhs = jnp.concatenate([ds, low[p]], axis=1)
+                acc[pair_k[p]] += jnp.dot(lhs, rhs_d[qs], preferred_element_type=jnp.float32)
+                dq[qs] += jnp.dot(kvt[pair_k[p], :HD, :], ds, preferred_element_type=jnp.float32)
+            return carry
+
+        lax.fori_loop(0, steps, spread_grad, 0)
+
+        def give(b, carry):
+            slot = brain[b]
+            both = jnp.concatenate([dq[slot] * scaling, att[slot]], axis=0).T
+            res_q[slot] = both.astype(jnp.bfloat16).reshape(2, BP, 128)
+            return carry
+
+        lax.fori_loop(0, blocks, give, 0)
+
+        def finish_keys(s, carry):
+            whole = acc[s]
+            res_kv[s] = where_lane(whole * scaling, whole).astype(jnp.bfloat16).reshape(KF, BP, 128)
+            return carry
+
+        lax.fori_loop(0, slots, finish_keys, 0)
+
+
+def attend(block_table, brain_mask, q, kv, tm_size):
+    slots = q.shape[0]
     smem = pl.BlockSpec(memory_space=pltpu.SMEM)
+    vmem = pl.BlockSpec(memory_space=pltpu.VMEM)
+    store = (PAIRS + UNROLL, KR, QR)
     return pl.pallas_call(
         functools.partial(attend_kernel, tm_size),
         out_shape=(
-            jax.ShapeDtypeStruct((slots, 6, BP, 128), jnp.bfloat16),
             jax.ShapeDtypeStruct((slots, 2, BP, 128), jnp.bfloat16),
+            jax.ShapeDtypeStruct((slots, KF, BP, 128), jnp.bfloat16),
         ),
-        in_specs=[smem, smem, any_spec, any_spec, any_spec],
-        out_specs=(any_spec, any_spec),
+        in_specs=[smem, smem, vmem, vmem, pl.BlockSpec(memory_space=ANY)],
+        out_specs=(vmem, vmem),
         scratch_shapes=[
-            pltpu.VMEM((slots, KF, BP, 128), jnp.bfloat16),
             pltpu.VMEM((slots, 128, KR), jnp.bfloat16),
-            pltpu.VMEM((slots, 2, BP, 128), jnp.bfloat16),
-            pltpu.VMEM((9, KR, QR), jnp.float32),
+            pltpu.VMEM((10, KR, QR), jnp.float32),
             pltpu.VMEM((slots, KR, 128), jnp.float32),
-            pltpu.VMEM((9, KR, QR), jnp.float32),
-            pltpu.VMEM((9, KR, QR), jnp.float32),
-            pltpu.VMEM((9, KR, QR), jnp.bfloat16),
-            pltpu.VMEM((slots, 2, BP, 128), jnp.bfloat16),
-            pltpu.VMEM((slots, KF, BP, 128), jnp.bfloat16),
+            pltpu.VMEM(store, jnp.float32),
+            pltpu.VMEM(store, jnp.float32),
+            pltpu.VMEM(store, jnp.bfloat16),
+            pltpu.VMEM((slots, 128, 2 * QR), jnp.bfloat16),
+            pltpu.VMEM((slots, 2 * QR, 128), jnp.bfloat16),
+            pltpu.VMEM((slots, 8, QR), jnp.float32),
+            pltpu.VMEM((slots, 8, QR), jnp.float32),
+            pltpu.VMEM((slots, 8, QR), jnp.float32),
+            pltpu.VMEM((slots, HD, QR), jnp.float32),
+            pltpu.VMEM((slots, HD, QR), jnp.float32),
             pltpu.SMEM((16,), jnp.int32),
-            pltpu.SMEM((16,), jnp.int32),
-            pltpu.SMEM((16,), jnp.int32),
-            pltpu.SemaphoreType.DMA((4,)),
+            pltpu.SMEM((17,), jnp.int32),
+            pltpu.SMEM((PAIRS + UNROLL,), jnp.int32),
+            pltpu.SMEM((PAIRS + UNROLL,), jnp.int32),
+            pltpu.SMEM((PAIRS + UNROLL,), jnp.int32),
+            pltpu.SemaphoreType.DMA,
         ],
         compiler_params=pltpu.CompilerParams(vmem_limit_bytes=56 << 20),
         name="attend",
-    )(block_table, brain_mask, main, halo, jnp.asarray(window_bias()))
+    )(block_table, brain_mask, q, kv, jnp.asarray(window_bias()))
 
 
 ROWS = 9216
@@ -387,9 +435,9 @@
 
 
 def finish_kernel(
-    slots, tm_size, main, halo, tok_hbm, gout_hbm, wqkv_hbm, tg_ref, out,
-    got, got_halo, tok, gout, wqkv, grads, att, src, b0, hs, b1, s1, b2, b3,
-    lsem, cs, ch, cr, crh, ss0, r0, ss1, r1, ss2, r2, ss3, r3, ss4, r4, ss5, r5,
+    slots, tm_size, res_q, res_kv, tok_hbm, gout_hbm, wqkv_hbm, tg_ref, out,
+    got_q, got_kv, got_halo, tok, gout, wqkv, grads, att, src, b0, hs, b1, s1, b2, b3,
+    lsem, cq, cs, ch, cqr, cr, crh, ss0, r0, ss1, r1, ss2, r2, ss3, r3, ss4, r4, ss5, r5,
 ):
     s = lax.axis_index("space")
     t = lax.axis_index("tm")
@@ -456,43 +504,66 @@
 
     pl.semaphore_wait(barrier, is_worker * (2 * slots - 1) + 15 + 4 * core)
 
-    def main_copy(i):
-        return remote(
-            main.at[i], got.at[half, head], cs.at[i], cr, {"space": i, "tm": t}
-        )
+    def query_refs(i):
+        return res_q.at[i], got_q.at[half, head]
+
+    def key_refs(i):
+        return res_kv.at[i, pl.ds(2 - 2 * half, 4)], got_kv.at[half, head]
+
+    def query_copy(i):
+        a, b = query_refs(i)
+        return remote(a, b, cq.at[i], cqr, {"space": i, "tm": t})
+
+    def key_copy(i):
+        a, b = key_refs(i)
+        return remote(a, b, cs.at[i], cr, {"space": i, "tm": t})
 
     def halo_copy(i):
         return remote(
-            halo.at[i], got_halo.at[half, head], ch.at[i], crh, {"space": i, "tm": other}
+            res_kv.at[i, pl.ds(4 * half, 2)], got_halo.at[half, head], ch.at[i], crh,
+            {"space": i, "tm": other},
         )
 
     @pl.when(is_worker == 1)
     def _():
-        def send_halo(i, carry):
-            halo_copy(lax.rem(i + s, slots)).start()
-            return carry
-
-        def send(i, carry):
+        def send_queries(i, carry):
             to = lax.rem(i + s, slots)
 
             @pl.when(to != s)
             def _():
-                main_copy(to).start()
+                query_copy(to).start()
 
             @pl.when(to == s)
             def _():
-                pltpu.make_async_copy(main.at[to], got.at[half, head], cr).start()
-
-            return carry
-
-        lax.fori_loop(0, slots, send_halo, 0)
-        lax.fori_loop(0, slots, send, 0)
+                a, b = query_refs(to)
+                pltpu.make_async_copy(a, b, cqr).start()
+
+            return carry
+
+        def send_keys(i, carry):
+            to = lax.rem(i + s, slots)
+            halo_copy(to).start()
+
+            @pl.when(to != s)
+            def _():
+                key_copy(to).start()
+
+            @pl.when(to == s)
+            def _():
+                a, b = key_refs(to)
+                pltpu.make_async_copy(a, b, cr).start()
+
+            return carry
+
+        lax.fori_loop(0, slots, send_queries, 0)
+        lax.fori_loop(0, slots, send_keys, 0)
 
     for load in loads:
         load.wait()
     tok_t = tok[...].T
+    pltpu.make_async_copy(got_q, got_q, cqr).wait()
     pltpu.make_async_copy(got_halo, got_halo, crh).wait()
-    pltpu.make_async_copy(got, got, cr).wait()
+    pltpu.make_async_copy(got_kv, got_kv, cr).wait()
 
     def pair(a, b):
         low = where_lane(a, pltpu.roll(b, HD, 1))
@@ -503,11 +574,12 @@
         at = 128 * i
         kvs, qas = [], []
         for h in (2 * i, 2 * i + 1):
-            low = got[0, h].astype(jnp.float32)
-            high = got[1, h].astype(jnp.float32)
+            low = got_kv[0, h].astype(jnp.float32)
+            high = got_kv[1, h].astype(jnp.float32)
             edge = jnp.concatenate([got_halo[1, h], got_halo[0, h]], axis=0).astype(jnp.float32)
-            kvs.append((low[2:6] + high[0:4] + edge).reshape(LF * BP, 128))
-            qas.append(jnp.concatenate([low[0:2], high[4:6]], axis=0).reshape(LF * BP, 128))
+            kvs.append((low + high + edge).reshape(LF * BP, 128))
+            rows = jnp.concatenate([got_q[0, h], got_q[1, h]], axis=0).astype(jnp.float32)
+            qas.append(rows.reshape(LF * BP, 128))
         dk, dv = pair(*kvs)
         dq, da = pair(*qas)
         grads[:, at : at + 128] = dq
@@ -688,14 +760,15 @@
 
             @pl.when(i != s)
             def _():
-                main_copy(i).wait_send()
+                query_copy(i).wait_send()
+                key_copy(i).wait_send()
 
             return carry
 
         lax.fori_loop(0, slots, finish, 0)
 
 
-def finish(main, halo, tokens, grad_out, w_qkv, slots, tm_size):
+def finish(res_q, res_kv, tokens, grad_out, w_qkv, slots, tm_size):
     any_spec = pl.BlockSpec(memory_space=ANY)
     vmem = pl.BlockSpec(memory_space=pltpu.VMEM)
     dma = pltpu.SemaphoreType.DMA
@@ -705,10 +778,11 @@
             jax.ShapeDtypeStruct((LF * BP, D), jnp.bfloat16),
             jax.ShapeDtypeStruct((ROWS, 128), jnp.bfloat16),
         ),
-        in_specs=[any_spec] * 5,
+        in_specs=[vmem, vmem] + [any_spec] * 3,
         out_specs=(vmem, vmem),
         scratch_shapes=[
-            pltpu.VMEM((2, HEADS, 6, BP, 128), jnp.bfloat16),
+            pltpu.VMEM((2, HEADS, 2, BP, 128), jnp.bfloat16),
+            pltpu.VMEM((2, HEADS, LF, BP, 128), jnp.bfloat16),
             pltpu.VMEM((2, HEADS, 2, BP, 128), jnp.bfloat16),
             pltpu.VMEM(tokens.shape, jnp.bfloat16),
             pltpu.VMEM(grad_out.shape, jnp.bfloat16),
@@ -722,15 +796,15 @@
             pltpu.VMEM((16, PIECE, 128), jnp.float32),
             pltpu.VMEM((16, PIECE, 128), jnp.float32),
             pltpu.VMEM((16, PIECE, 128), jnp.float32),
-            dma((3,)), dma((slots,)), dma((slots,)), dma, dma,
+            dma((3,)), dma((slots,)), dma((slots,)), dma((slots,)), dma, dma, dma,
             dma((8,)), dma((8,)), dma((8,)), dma((8,)), dma((16,)), dma((16,)),
             dma((16,)), dma((16,)), dma((8,)), dma((8,)), dma((8,)), dma((8,)),
         ],
         compiler_params=pltpu.CompilerParams(
-            has_side_effects=True, collective_id=2, vmem_limit_bytes=60 << 20
+            has_side_effects=True, collective_id=2, vmem_limit_bytes=32 << 20
         ),
         name="finish",
-    )(main, halo, tokens, grad_out, w_qkv)
+    )(res_q, res_kv, tokens, grad_out, w_qkv)
 
 
 def widen_kernel(src, qkv, out):
@@ -761,9 +835,9 @@
     tm_size = lax.axis_size("tm")
     flat_tokens = tokens.reshape(-1, D)
     flat_grad = grad_out.reshape(-1, D)
-    main, halo = spread(flat_tokens, flat_grad, w_qkv, w_out, slots, tm_size)
-    main, halo = attend(block_table, brain_mask, main, halo, tm_size)
-    token_grads, terms = finish(main, halo, flat_tokens, flat_grad, w_qkv, slots, tm_size)
+    q, kv = spread(flat_tokens, flat_grad, w_qkv, w_out, slots, tm_size)
+    res_q, res_kv = attend(block_table, brain_mask, q, kv, tm_size)
+    token_grads, terms = finish(res_q, res_kv, flat_tokens, flat_grad, w_qkv, slots, tm_size)
     qkv_grads, out_grads = widen(terms)
     return (token_grads.reshape(tokens.shape), qkv_grads, out_grads)
 

time: 139 us -> 141 us (1.014); the launches traced: 137 us -> 141 us
  local copies, waits for them, and re-layouts: 2.41 us -> 9.65 us
  Pallas kernels: 134 us -> 131 us
    unnamed x5 -> x23, local copies, waits for them, and re-layouts: 2.41 us -> 9.65 us
    pallas_call x1, Pallas kernels: 73.7 us -> 70.8 us  [finish(): pl.pallas_call(functools.partial(finish_kernel, slots, tm_size), out_shap...]
where the time goes in v4:
time: 141 us
  Pallas kernels  131 us (93%)
  local copies, waits for them, and re-layouts  9.65 us (7%)
    pallas_call x1, Pallas kernels, finish(): pl.pallas_call(functools.partial(finish_kernel, slots, tm_size), out_shap...  70.8 us
    pallas_call x1, Pallas kernels, spread(): pl.pallas_call(functools.partial(spread_kernel, slots, tm_size), out_shap...  34.9 us
    pallas_call x1, Pallas kernels, attend(): pl.pallas_call(functools.partial(attend_kernel, tm_size), out_shape=(jax....  22.6 us
    unnamed x23, local copies, waits for them, and re-layouts  9.65 us

profile of v4, /device:TPU:1, one launch (start us, length us, event | category | flops | bytes accessed | tf_op | source)
XLA Modules:
  0.0 141.0 jit_solution(3124187272836678211)
XLA Ops:
  0.6 0.0 copy-start
  0.6 1.5 %copy-done = bf16[768,1152]{1,0:T(8,128)(2,1)S(1)} copy-done((bf16[768,1152]{1,0:T(8,128)(2,1)S(1)}, bf16[768,1152]{1,0:T(8,128)(2,1)}, u32[]{:S(2)}) %copy-start) | copy-done | bytes 1769496
  2.1 0.0 copy-start.2
  2.1 1.0 copy-done.2
  3.1 0.0 copy-start.4
  3.1 1.0 copy-done.4
  4.1 0.0 copy-start.8
  4.1 1.1 copy-done.8
  5.2 34.9 %spread.1 = (bf16[16,2,64,128]{3,2,1,0:T(8,128)(2,1)S(1)}, bf16[16,6,64,128]{3,2,1,0:T(8,128)(2,1)S(1)}) custom-call(bf16[256,768]{1,0:T(8,128)(2,1)S(1)} %bitcast.3, bf16[256,768]{1,0:T(8,128)(2,1)S(1)} %bitcast.5, bf16[768,1152]{1,0:T(8,128)(2,1)S(1)} %copy-done, bf16[384,768]{1,0:T(8,128)(2,1)S(1)} %copy-done.8), custom_call_target="tpu_custom_call" | custom-call | tf_op jit(solution)/shard_map/spread/pallas_call | solution.py:183
  40.0 0.0 copy-start.6
  40.0 1.1 copy-done.6
  41.2 0.0 copy-start.10
  41.2 0.8 copy-done.10
  42.0 0.0 copy-start.1
  42.0 0.0 copy-start.3
  42.0 0.0 copy-start.5
  42.0 22.6 %attend.1 = (bf16[16,2,64,128]{3,2,1,0:T(8,128)(2,1)}, bf16[16,6,64,128]{3,2,1,0:T(8,128)(2,1)}) custom-call(s32[16]{0:T(128)} %table.1, s32[16]{0:T(128)} %mask.1, bf16[16,2,64,128]{3,2,1,0:T(8,128)(2,1)} %copy-done.10, bf16[16,6,64,128]{3,2,1,0:T(8,128)(2,1)} %copy-done.6, f32[10,384,128]{2,1,0:T(8,128)} %constant.2.clone.bias_hbm), custom_call_target="tpu_custom_call" | custom-call | tf_op jit(solution)/shard_map/attend/pallas_call | solution.py:394
  64.6 0.0 copy-done.1
  64.6 0.0 copy-done.3
  64.6 0.0 copy-done.5
  64.6 0.0 copy-start.7
  64.6 1.4 copy-done.7
  66.0 0.0 copy-start.9
  66.0 1.0 copy-done.9
  67.0 70.8 %finish.1 = (bf16[256,768]{1,0:T(8,128)(2,1)S(1)}, bf16[9216,128]{1,0:T(8,128)(2,1)S(1)}) custom-call(bf16[16,2,64,128]{3,2,1,0:T(8,128)(2,1)S(1)} %copy-done.9, bf16[16,6,64,128]{3,2,1,0:T(8,128)(2,1)S(1)} %copy-done.7, bf16[256,768]{1,0:T(8,128)(2,1)S(1)} %bitcast.4, bf16[256,768]{1,0:T(8,128)(2,1)S(1)} %bitcast.6, bf16[768,1152]{1,0:T(8,128)(2,1)S(1)} %copy-done.1), custom_call_target="tpu_custom_call" | custom-call | tf_op jit(solution)/shard_map/finish/pallas_call | solution.py:775
  137.9 2.4 %widen.1 = (f32[768,1152]{1,0:T(8,128)}, f32[384,768]{1,0:T(8,128)}) custom-call(bf16[9216,128]{1,0:T(8,128)(2,1)S(1)} %get-tuple-element.16.src), custom_call_target="tpu_custom_call" | custom-call | tf_op jit(solution)/shard_map/widen/pallas_call | solution.py:820
  140.3 0.7 copy.11
Async XLA Ops:
  0.6 1.5 %copy-start = (bf16[768,1152]{1,0:T(8,128)(2,1)S(1)}, bf16[768,1152]{1,0:T(8,128)(2,1)}, u32[]{:S(2)}) copy-start(bf16[768,1152]{1,0:T(8,128)(2,1)} %wqkv_hbm.3) | copy-start | bytes 5308420
  2.1 1.0 copy-start.2
  3.1 1.0 copy-start.4
  4.1 1.1 copy-start.8
  40.0 1.1 copy-start.6
  41.2 0.8 copy-start.10
  42.0 22.6 %copy-start.1 = (bf16[768,1152]{1,0:T(8,128)(2,1)S(1)}, bf16[768,1152]{1,0:T(8,128)(2,1)}, u32[]{:S(2)}) copy-start(bf16[768,1152]{1,0:T(8,128)(2,1)} %wqkv_hbm.3) | copy-start | bytes 5308420
  42.0 22.6 %copy-start.3 = (bf16[1,4,64,768]{3,2,1,0:T(8,128)(2,1)S(1)}, bf16[1,4,64,768]{3,2,1,0:T(8,128)(2,1)}, u32[]{:S(2)}) copy-start(bf16[1,4,64,768]{3,2,1,0:T(8,128)(2,1)} %param.7) | copy-start | bytes 1179652
  42.0 22.6 %copy-start.5 = (bf16[1,4,64,768]{3,2,1,0:T(8,128)(2,1)S(1)}, bf16[1,4,64,768]{3,2,1,0:T(8,128)(2,1)}, u32[]{:S(2)}) copy-start(bf16[1,4,64,768]{3,2,1,0:T(8,128)(2,1)} %param.8) | copy-start | bytes 1179652
  64.6 1.4 copy-start.7
  66.0 1.0 copy-start.9

commit v5 on v4

--- a/solution.py
+++ b/solution.py
@@ -21,7 +21,6 @@
 KR = KF * BP
 QR = 2 * BP
 WORKERS = 2 * HEADS
-ANY = pl.ANY
 
 
 def where_lane(low, high):
@@ -33,11 +32,15 @@
 
 
 def worker_space(w):
-    return w + (w // 8) * (w - 8)
+    row = w // 6
+    at = w - 6 * row
+    return 8 * row + at + (at + 2 * row) // 3
 
 
 def worker_of(space):
-    return 1 - (space // 8) * (space % 2), space - (space // 8) * ((space - 8) // 2)
+    row = space // 8
+    at = space - 8 * row
+    return ((at + 1 + 2 * row) % 4 + 3) // 4, 6 * row + at - (at + 2 * row) // 4
 
 
 def signal(semaphore, space, tm):
@@ -51,8 +54,8 @@
 
 
 def spread_kernel(
-    slots, tm_size, tok_hbm, gout_hbm, wqkv_hbm, wout_hbm, q, kv,
-    tok, gout, wqkv, wout, qpack, kpack, lsem, qsem, ssem, hsem, rqsem, rsem,
+    slots, tm_size, tok_hbm, gout_hbm, wqkv_hbm, wout_hbm, held,
+    tok, gout, wqkv, wout, packed, lsem, ssem, hsem, rsem,
 ):
     me = lax.axis_index("space")
     t = lax.axis_index("tm")
@@ -103,28 +106,23 @@
         keys = pair(proj[:, HW + at : HW + at + 128], proj[:, 2 * HW + at : 2 * HW + at + 128])
         queries = pair(proj[:, at : at + 128], gatt[:, at : at + 128])
         for j in range(2):
-            qpack[2 * i + j] = queries[j]
-            kpack[2 * i + j] = keys[j]
+            packed[2 * i + j, 0:2] = queries[j][2:4]
+            packed[2 * i + j, 2:6] = keys[j]
+            packed[2 * i + j, 6:8] = queries[j][0:2]
 
     pl.semaphore_wait(barrier, 2 * WORKERS - is_worker)
 
-    def query_refs(w):
-        return qpack.at[w // 2, pl.ds(2 * (w % 2), 2)], q.at[me]
-
-    def key_refs(w):
-        return kpack.at[w // 2], kv.at[me, pl.ds(2 - 2 * (w % 2), 4)]
-
-    def query_copy(w):
-        src, dst = query_refs(w)
-        return remote(src, dst, qsem.at[w], rqsem, {"space": worker_space(w), "tm": t})
-
-    def key_copy(w):
-        src, dst = key_refs(w)
+    def main_refs(w):
+        start = 2 - 2 * (w % 2)
+        return packed.at[w // 2, pl.ds(start, 6)], held.at[me, pl.ds(start, 6)]
+
+    def main_copy(w):
+        src, dst = main_refs(w)
         return remote(src, dst, ssem.at[w], rsem, {"space": worker_space(w), "tm": t})
 
     def halo_copy(h, half):
         return remote(
-            kpack.at[h, pl.ds(2 - 2 * half, 2)], kv.at[me, pl.ds(4 * half, 2)],
+            packed.at[h, pl.ds(4 - 2 * half, 2)], held.at[me, pl.ds(6 * half, 2)],
             hsem.at[2 * h + half], rsem,
             {"space": worker_space(2 * h + half), "tm": before if half else after},
         )
@@ -134,15 +132,12 @@
 
         @pl.when(worker_space(w) != me)
         def _():
-            key_copy(w).start()
-            query_copy(w).start()
+            main_copy(w).start()
 
         @pl.when(worker_space(w) == me)
         def _():
-            src, dst = key_refs(w)
+            src, dst = main_refs(w)
             pltpu.make_async_copy(src, dst, rsem).start()
-            src, dst = query_refs(w)
-            pltpu.make_async_copy(src, dst, rqsem).start()
 
         return carry
 
@@ -158,8 +153,7 @@
     def finish(w, carry):
         @pl.when(worker_space(w) != me)
         def _():
-            key_copy(w).wait_send()
-            query_copy(w).wait_send()
+            main_copy(w).wait_send()
 
         return carry
 
@@ -170,36 +164,29 @@
 
     @pl.when(is_worker == 1)
     def _():
-        pltpu.make_async_copy(kv, kv, rsem).wait()
-        pltpu.make_async_copy(q, q, rqsem).wait()
+        pltpu.make_async_copy(held, held, rsem).wait()
 
     lax.fori_loop(0, HEADS, finish_halo, 0)
     lax.fori_loop(0, WORKERS, finish, 0)
 
 
 def spread(tokens, grad_out, w_qkv, w_out, slots, tm_size):
-    any_spec = pl.BlockSpec(memory_space=ANY)
+    hbm = pl.BlockSpec(memory_space=pltpu.HBM)
     vmem = pl.BlockSpec(memory_space=pltpu.VMEM)
     return pl.pallas_call(
         functools.partial(spread_kernel, slots, tm_size),
-        out_shape=(
-            jax.ShapeDtypeStruct((slots, 2, BP, 128), jnp.bfloat16),
-            jax.ShapeDtypeStruct((slots, KF, BP, 128), jnp.bfloat16),
-        ),
-        in_specs=[any_spec] * 4,
-        out_specs=(vmem, vmem),
+        out_shape=jax.ShapeDtypeStruct((slots, 8, BP, 128), jnp.bfloat16),
+        in_specs=[hbm] * 4,
+        out_specs=vmem,
         scratch_shapes=[
             pltpu.VMEM(tokens.shape, jnp.bfloat16),
             pltpu.VMEM(grad_out.shape, jnp.bfloat16),
             pltpu.VMEM(w_qkv.shape, jnp.bfloat16),
             pltpu.VMEM(w_out.shape, jnp.bfloat16),
-            pltpu.VMEM((HEADS, LF, BP, 128), jnp.bfloat16),
-            pltpu.VMEM((HEADS, LF, BP, 128), jnp.bfloat16),
+            pltpu.VMEM((HEADS, 8, BP, 128), jnp.bfloat16),
             pltpu.SemaphoreType.DMA((4,)),
             pltpu.SemaphoreType.DMA((WORKERS,)),
             pltpu.SemaphoreType.DMA((WORKERS,)),
-            pltpu.SemaphoreType.DMA((WORKERS,)),
-            pltpu.SemaphoreType.DMA,
             pltpu.SemaphoreType.DMA,
         ],
         compiler_params=pltpu.CompilerParams(
@@ -230,16 +217,19 @@
 
 
 def attend_kernel(
-    tm_size, table, mask, q, kv, bias_hbm, res_q, res_kv,
-    kvt, bias, acc, scores, dots, low, rhs_a, rhs_d, total, inverse, delta, att, dq,
+    tm_size, table, mask, held, bias_hbm, res_q, res_kv,
+    kvt, bias, acc, scores, dots, rhs_a, rhs_d, total, inverse, delta, att, dq,
     slot_of, brain, pair_q, pair_k, pair_off, sem,
 ):
     me = lax.axis_index("space")
     t = lax.axis_index("tm")
     is_worker, worker = worker_of(me)
     half = worker % 2
-    slots = kv.shape[0]
+    slots = held.shape[0]
     scaling = HD ** (-0.5)
+
+    def keys_of(slot):
+        return held[slot, pl.ds(2 * half, KF)].reshape(KR, 128)
 
     @pl.when(is_worker == 1)
     def _():
@@ -286,8 +276,8 @@
 
         def prepare(b, carry):
             slot = brain[b]
-            kvt[slot] = kv[slot].reshape(KR, 128).T
-            rows = q[slot].reshape(QR, 128)
+            kvt[slot] = keys_of(slot).T
+            rows = held[slot, pl.ds(6 - 6 * half, 2)].reshape(QR, 128)
             cols = rows.T
             zero = jnp.zeros_like(cols)
             first = lax.broadcasted_iota(jnp.int32, cols.shape, 0) < HD
@@ -315,7 +305,7 @@
         def score(step, carry):
             for u in range(UNROLL):
                 p = step * UNROLL + u
-                keys = kv[pair_k[p]].reshape(KR, 128)
+                keys = keys_of(pair_k[p])
                 both = jnp.dot(keys, rhs_a[pair_q[p]], preferred_element_type=jnp.float32)
                 e = jnp.exp(both[:, :QR] + bias[pair_off[p]])
                 scores[p] = e
@@ -338,7 +328,6 @@
                 p = step * UNROLL + u
                 w = by_rows(scores[p]) * inverse[pair_q[p]][None]
                 w = w.reshape(KR, QR).astype(jnp.bfloat16)
-                low[p] = w
                 att[pair_q[p]] += jnp.dot(
                     kvt[pair_k[p], HD:, :], w, preferred_element_type=jnp.float32
                 )
@@ -361,9 +350,10 @@
             for u in range(UNROLL):
                 p = step * UNROLL + u
                 qs = pair_q[p]
-                ds = by_rows(scores[p]) * inverse[qs][None] * (by_rows(dots[p]) - delta[qs][None])
+                w = by_rows(scores[p]) * inverse[qs][None]
+                ds = w * (by_rows(dots[p]) - delta[qs][None])
                 ds = ds.reshape(KR, QR).astype(jnp.bfloat16)
-                lhs = jnp.concatenate([ds, low[p]], axis=1)
+                lhs = jnp.concatenate([ds, w.reshape(KR, QR).astype(jnp.bfloat16)], axis=1)
                 acc[pair_k[p]] += jnp.dot(lhs, rhs_d[qs], preferred_element_type=jnp.float32)
                 dq[qs] += jnp.dot(kvt[pair_k[p], :HD, :], ds, preferred_element_type=jnp.float32)
             return carry
@@ -386,8 +376,8 @@
         lax.fori_loop(0, slots, finish_keys, 0)
 
 
-def attend(block_table, brain_mask, q, kv, tm_size):
-    slots = q.shape[0]
+def attend(block_table, brain_mask, held, tm_size):
+    slots = held.shape[0]
     smem = pl.BlockSpec(memory_space=pltpu.SMEM)
     vmem = pl.BlockSpec(memory_space=pltpu.VMEM)
     store = (PAIRS + UNROLL, KR, QR)
@@ -397,7 +387,7 @@
             jax.ShapeDtypeStruct((slots, 2, BP, 128), jnp.bfloat16),
             jax.ShapeDtypeStruct((slots, KF, BP, 128), jnp.bfloat16),
         ),
-        in_specs=[smem, smem, vmem, vmem, pl.BlockSpec(memory_space=ANY)],
+        in_specs=[smem, smem, vmem, pl.BlockSpec(memory_space=pltpu.HBM)],
         out_specs=(vmem, vmem),
         scratch_shapes=[
             pltpu.VMEM((slots, 128, KR), jnp.bfloat16),
@@ -405,7 +395,6 @@
             pltpu.VMEM((slots, KR, 128), jnp.float32),
             pltpu.VMEM(store, jnp.float32),
             pltpu.VMEM(store, jnp.float32),
-            pltpu.VMEM(store, jnp.bfloat16),
             pltpu.VMEM((slots, 128, 2 * QR), jnp.bfloat16),
             pltpu.VMEM((slots, 2 * QR, 128), jnp.bfloat16),
             pltpu.VMEM((slots, 8, QR), jnp.float32),
@@ -420,23 +409,24 @@
             pltpu.SMEM((PAIRS + UNROLL,), jnp.int32),
             pltpu.SemaphoreType.DMA,
         ],
-        compiler_params=pltpu.CompilerParams(vmem_limit_bytes=56 << 20),
+        compiler_params=pltpu.CompilerParams(vmem_limit_bytes=47 << 20),
         name="attend",
-    )(block_table, brain_mask, q, kv, jnp.asarray(window_bias()))
+    )(block_table, brain_mask, held, jnp.asarray(window_bias()))
 
 
 ROWS = 9216
-HALF = ROWS // 2
-PART = 576
-PARTS = HALF // PART
-PIECE = 72
+KEYS_AT = 6 * D
+STARTS = (0, 4096)
+HALVES = (2048, 2560)
+PIECES = (32, 40)
+PARTS = 8
 FIRST = (8, 4)
 SECOND = (8, 16)
 
 
 def finish_kernel(
     slots, tm_size, res_q, res_kv, tok_hbm, gout_hbm, wqkv_hbm, tg_ref, out,
-    got_q, got_kv, got_halo, tok, gout, wqkv, grads, att, src, b0, hs, b1, s1, b2, b3,
+    got_q, got_kv, got_halo, tok, gout, wqkv, grads, att, src, early, late,
     lsem, cq, cs, ch, cqr, cr, crh, ss0, r0, ss1, r1, ss2, r2, ss3, r3, ss4, r4, ss5, r5,
 ):
     s = lax.axis_index("space")
@@ -561,194 +551,209 @@
     for load in loads:
         load.wait()
     tok_t = tok[...].T
-    pltpu.make_async_copy(got_q, got_q, cqr).wait()
-    pltpu.make_async_copy(got_halo, got_halo, crh).wait()
-    pltpu.make_async_copy(got_kv, got_kv, cr).wait()
 
     def pair(a, b):
         low = where_lane(a, pltpu.roll(b, HD, 1))
         high = where_lane(pltpu.roll(a, HD, 1), b)
         return low.astype(jnp.bfloat16), high.astype(jnp.bfloat16)
 
-    for i in range(HEADS // 2):
-        at = 128 * i
-        kvs, qas = [], []
-        for h in (2 * i, 2 * i + 1):
-            low = got_kv[0, h].astype(jnp.float32)
-            high = got_kv[1, h].astype(jnp.float32)
-            edge = jnp.concatenate([got_halo[1, h], got_halo[0, h]], axis=0).astype(jnp.float32)
-            kvs.append((low + high + edge).reshape(LF * BP, 128))
-            rows = jnp.concatenate([got_q[0, h], got_q[1, h]], axis=0).astype(jnp.float32)
-            qas.append(rows.reshape(LF * BP, 128))
-        dk, dv = pair(*kvs)
-        dq, da = pair(*qas)
-        grads[:, at : at + 128] = dq
-        grads[:, HW + at : HW + at + 128] = dk
-        grads[:, 2 * HW + at : 2 * HW + at + 128] = dv
-        att[:, at : at + 128] = da
-    for i in range(9):
-        src[D * i : D * (i + 1), :] = jnp.dot(
-            tok_t, grads[:, 128 * i : 128 * (i + 1)], preferred_element_type=jnp.float32
-        ).astype(jnp.bfloat16)
-    att_t = att[...].T
-    for i in range(6):
-        start = 9 * D + HW * i
-        src[start : start + HW, :] = jnp.dot(
-            att_t, gout[:, 128 * i : 128 * (i + 1)], preferred_element_type=jnp.float32
-        ).astype(jnp.bfloat16)
+    def query_terms():
+        pltpu.make_async_copy(got_q, got_q, cqr).wait()
+        for i in range(HEADS // 2):
+            at = 128 * i
+            both = []
+            for h in (2 * i, 2 * i + 1):
+                rows = jnp.concatenate([got_q[0, h], got_q[1, h]], axis=0).astype(jnp.float32)
+                both.append(rows.reshape(LF * BP, 128))
+            dq, da = pair(*both)
+            grads[:, at : at + 128] = dq
+            att[:, at : at + 128] = da
+            src[D * i : D * (i + 1), :] = jnp.dot(
+                tok_t, dq, preferred_element_type=jnp.float32
+            ).astype(jnp.bfloat16)
+        att_t = att[...].T
+        for i in range(6):
+            start = 3 * D + HW * i
+            src[start : start + HW, :] = jnp.dot(
+                att_t, gout[:, 128 * i : 128 * (i + 1)], preferred_element_type=jnp.float32
+            ).astype(jnp.bfloat16)
+
+    def key_terms():
+        pltpu.make_async_copy(got_halo, got_halo, crh).wait()
+        pltpu.make_async_copy(got_kv, got_kv, cr).wait()
+        for i in range(HEADS // 2):
+            both = []
+            for h in (2 * i, 2 * i + 1):
+                low = got_kv[0, h].astype(jnp.float32)
+                high = got_kv[1, h].astype(jnp.float32)
+                edge = jnp.concatenate([got_halo[1, h], got_halo[0, h]], axis=0).astype(jnp.float32)
+                both.append((low + high + edge).reshape(LF * BP, 128))
+            for k, value in enumerate(pair(*both)):
+                at = (1 + k) * HW + 128 * i
+                grads[:, at : at + 128] = value
+                start = KEYS_AT + D * (3 * k + i)
+                src[start : start + D, :] = jnp.dot(
+                    tok_t, value, preferred_element_type=jnp.float32
+                ).astype(jnp.bfloat16)
 
     def token_grads():
         tg_ref[...] = lax.dot_general(
             grads[...], wqkv[...], (((1,), (1,)), ((), ())), preferred_element_type=jnp.float32
         ).astype(jnp.bfloat16)
 
-    def sum_all(c):
+    def stages(c, p):
+        b0, hs, b1, s1, h2, b2, b3 = (early, late)[p]
         first, second = FIRST[c], SECOND[c]
-        length = HALF // first
+        half_rows, piece = HALVES[p], PIECES[p]
+        length = half_rows // first
+        step = half_rows // PARTS
         parts = PARTS // first
-        base = c * HALF
-        far = HALF - base
+        pieces = step // piece
+        base = STARTS[p] + c * half_rows
+        far = STARTS[p] + (1 - c) * half_rows
         here1, here2 = rank1(c), rank2(c)
 
-        def part(k):
-            return pl.ds(pl.multiple_of(k * PART, PART), PART)
-
         def rows(start, index, size):
-            return pl.ds(pl.multiple_of(start + index * size, PART), size)
+            return pl.ds(pl.multiple_of(start + index * size, 64), size)
 
         def copy0(k):
-            return remote(src.at[rows(far, k, PART)], b0.at[part(k)], ss0.at[k], r0.at[k], sibling)
+            return remote(
+                src.at[rows(far, k, step)], b0.at[rows(0, k, step)], ss0.at[p, k], r0.at[p, k], sibling
+            )
 
         def copy1(i, slot):
             return remote(
-                hs.at[rows(0, i, length)], b1.at[rows(0, slot, length)], ss1.at[i], r1.at[slot],
-                peer1(c, i),
+                hs.at[rows(0, i, length)], b1.at[rows(0, slot, length)], ss1.at[p, i],
+                r1.at[p, slot], peer1(c, i),
             )
 
         def copy2(j, slot):
-            return remote(s1.at[j], b2.at[slot], ss2.at[j], r2.at[slot], peer2(c, j))
+            return remote(h2.at[j], b2.at[slot], ss2.at[p, j], r2.at[p, slot], peer2(c, j))
 
         def copy3(j, slot):
-            return remote(b3.at[slot], b3.at[slot], ss3.at[j], r3.at[slot], peer2(c, j))
+            return remote(b3.at[slot], b3.at[slot], ss3.at[p, j], r3.at[p, slot], peer2(c, j))
 
         def copy4(i, chunk):
             where = rows(base, chunk, length)
-            return remote(out.at[where], out.at[where], ss4.at[i], r4.at[chunk], peer1(c, i))
+            return remote(out.at[where], out.at[where], ss4.at[p, i], r4.at[p, chunk], peer1(c, i))
 
         def copy5(chunk):
             where = rows(base, chunk, length)
-            return remote(out.at[where], out.at[where], ss5.at[chunk], r5.at[chunk], sibling)
+            return remote(out.at[where], out.at[where], ss5.at[p, chunk], r5.at[p, chunk], sibling)
 
         def from_sibling(chunk):
-            where = rows(far, chunk, HALF // FIRST[1 - c])
-            return remote(out.at[where], out.at[where], ss5.at[chunk], r5.at[chunk], sibling)
-
-        begin = ((rank1(1 - c) + 1) % FIRST[1 - c]) * (PARTS // FIRST[1 - c])
-
-        def start0(n, carry):
-            copy0((begin + n) % PARTS).start()
-            return carry
-
-        lax.fori_loop(0, PARTS, start0, 0)
-        token_grads()
+            where = rows(far, chunk, half_rows // FIRST[1 - c])
+            return remote(out.at[where], out.at[where], ss5.at[p, chunk], r5.at[p, chunk], sibling)
+
+        def loop(low, high, body):
+            def run(n, carry):
+                body(n)
+                return carry
+
+            lax.fori_loop(low, high, run, 0)
+
+        def send_pair():
+            begin = ((rank1(1 - c) + 1) % FIRST[1 - c]) * (PARTS // FIRST[1 - c])
+            loop(0, PARTS, lambda n: copy0((begin + n) % PARTS).start())
 
         def both(k):
             copy0(k).wait_recv()
-            return src[rows(base, k, PART), :].astype(jnp.float32) + b0[part(k), :].astype(jnp.float32)
-
-        def stage0(n, carry):
-            i = (here1 + n) % first
-            for p in range(parts):
-                hs[part(i * parts + p), :] = both(i * parts + p).astype(jnp.bfloat16)
-            copy1(i, here1).start()
-            return carry
-
-        lax.fori_loop(1, first, stage0, 0)
-        pieces = PART // PIECE
-        for p in range(parts):
-            s1[p * pieces : (p + 1) * pieces] = both(here1 * parts + p).reshape(pieces, PIECE, 128)
-
-        def stage1(n, carry):
-            i = (here1 + first - n) % first
-            copy1(i, i).wait_recv()
-            s1[0:second] += b1[rows(0, i, length), :].astype(jnp.float32).reshape(second, PIECE, 128)
-            return carry
-
-        lax.fori_loop(1, first, stage1, 0)
-
-        def start2(n, carry):
-            copy2((here2 + n) % second, here2).start()
-            return carry
-
-        lax.fori_loop(1, second, start2, 0)
-        b3[here2] = s1[here2]
-
-        def stage2(n, carry):
-            j = (here2 + second - n) % second
-            copy2(j, j).wait_recv()
-            b3[here2] += b2[j]
-            return carry
-
-        lax.fori_loop(1, second, stage2, 0)
-
-        def start3(n, carry):
-            copy3((here2 + n) % second, here2).start()
-            return carry
-
-        lax.fori_loop(1, second, start3, 0)
-
-        def stage3(n, carry):
-            j = (here2 + second - n) % second
-            copy3(j, j).wait_recv()
-            return carry
-
-        lax.fori_loop(1, second, stage3, 0)
-        out[rows(base, here1, length), :] = b3[0:second].reshape(length, 128).astype(jnp.bfloat16)
-
-        def start4(n, carry):
-            copy4((here1 + n) % first, here1).start()
-            return carry
-
-        lax.fori_loop(1, first, start4, 0)
-        copy5(here1).start()
-
-        def stage4(n, carry):
-            i = (here1 + first - n) % first
-            copy4(i, i).wait_recv()
-            copy5(i).start()
-            return carry
-
-        lax.fori_loop(1, first, stage4, 0)
-
-        def stage5(n, carry):
-            from_sibling(n).wait_recv()
-            return carry
-
-        lax.fori_loop(0, FIRST[1 - c], stage5, 0)
-
-        def sent0(n, carry):
-            copy0(n).wait_send()
-            return carry
-
-        lax.fori_loop(0, PARTS, sent0, 0)
-
-        def sent1(n, carry):
-            i = (here1 + n) % first
-            copy1(i, here1).wait_send()
-            copy4(i, here1).wait_send()
-            copy5(i).wait_send()
-            return carry
-
-        lax.fori_loop(1, first, sent1, 0)
-        copy5(here1).wait_send()
-
-        def sent2(n, carry):
-            j = (here2 + n) % second
-            copy2(j, here2).wait_send()
-            copy3(j, here2).wait_send()
-            return carry
-
-        lax.fori_loop(1, second, sent2, 0)
+            mine = src[rows(base, k, step), :].astype(jnp.float32)
+            return mine + b0[rows(0, k, step), :].astype(jnp.float32)
+
+        def send_first():
+            def one(n):
+                i = (here1 + n) % first
+                for e in range(parts):
+                    k = i * parts + e
+                    hs[rows(0, k, step), :] = both(k).astype(jnp.bfloat16)
+                copy1(i, here1).start()
+
+            loop(1, first, one)
+            for e in range(parts):
+                own = both(here1 * parts + e)
+                s1[e * pieces : (e + 1) * pieces] = own.reshape(pieces, piece, 128)
+
+        def send_second():
+            def one(n):
+                i = (here1 + first - n) % first
+                copy1(i, i).wait_recv()
+                more = b1[rows(0, i, length), :].astype(jnp.float32)
+                s1[0:second] += more.reshape(second, piece, 128)
+
+            loop(1, first, one)
+            h2[0:second] = s1[0:second].astype(jnp.bfloat16)
+            loop(1, second, lambda n: copy2((here2 + n) % second, here2).start())
+
+        def send_third():
+            def one(n, sum_so_far):
+                j = (here2 + second - n) % second
+                copy2(j, j).wait_recv()
+                return sum_so_far + b2[j].astype(jnp.float32)
+
+            b3[here2] = lax.fori_loop(1, second, one, s1[here2]).astype(jnp.bfloat16)
+            loop(1, second, lambda n: copy3((here2 + n) % second, here2).start())
+
+        def send_fourth():
+            def one(n):
+                j = (here2 + second - n) % second
+                copy3(j, j).wait_recv()
+
+            loop(1, second, one)
+            whole = b3[0:second].astype(jnp.float32).reshape(length, 128)
+            out[rows(base, here1, length), :] = whole.astype(jnp.bfloat16)
+            loop(1, first, lambda n: copy4((here1 + n) % first, here1).start())
+            copy5(here1).start()
+
+        def send_fifth():
+            def one(n):
+                i = (here1 + first - n) % first
+                copy4(i, i).wait_recv()
+                copy5(i).start()
+
+            loop(1, first, one)
+
+        def end():
+            loop(0, FIRST[1 - c], lambda n: from_sibling(n).wait_recv())
+            loop(0, PARTS, lambda n: copy0(n).wait_send())
+
+            def one(n):
+                i = (here1 + n) % first
+                copy1(i, here1).wait_send()
+                copy4(i, here1).wait_send()
+                copy5(i).wait_send()
+
+            loop(1, first, one)
+            copy5(here1).wait_send()
+
+            def two(n):
+                j = (here2 + n) % second
+                copy2(j, here2).wait_send()
+                copy3(j, here2).wait_send()
+
+            loop(1, second, two)
+
+        return send_pair, send_first, send_second, send_third, send_fourth, send_fifth, end
+
+    def sum_all(c):
+        a, b = stages(c, 0), stages(c, 1)
+        query_terms()
+        a[0]()
+        key_terms()
+        b[0]()
+        a[1]()
+        b[1]()
+        a[2]()
+        b[2]()
+        a[3]()
+        token_grads()
+        b[3]()
+        a[4]()
+        b[4]()
+        a[5]()
+        b[5]()
+        a[6]()
+        b[6]()
 
     for c in range(2):
         pl.when(core == c)(functools.partial(sum_all, c))
@@ -769,16 +774,22 @@
 
 
 def finish(res_q, res_kv, tokens, grad_out, w_qkv, slots, tm_size):
-    any_spec = pl.BlockSpec(memory_space=ANY)
+    hbm = pl.BlockSpec(memory_space=pltpu.HBM)
     vmem = pl.BlockSpec(memory_space=pltpu.VMEM)
     dma = pltpu.SemaphoreType.DMA
+    sums = [
+        [pltpu.VMEM((HALVES[p], 128), jnp.bfloat16)] * 3
+        + [pltpu.VMEM((16, PIECES[p], 128), jnp.float32)]
+        + [pltpu.VMEM((16, PIECES[p], 128), jnp.bfloat16)] * 3
+        for p in range(2)
+    ]
     return pl.pallas_call(
         functools.partial(finish_kernel, slots, tm_size),
         out_shape=(
             jax.ShapeDtypeStruct((LF * BP, D), jnp.bfloat16),
             jax.ShapeDtypeStruct((ROWS, 128), jnp.bfloat16),
         ),
-        in_specs=[vmem, vmem] + [any_spec] * 3,
+        in_specs=[vmem, vmem] + [hbm] * 3,
         out_specs=(vmem, vmem),
         scratch_shapes=[
             pltpu.VMEM((2, HEADS, 2, BP, 128), jnp.bfloat16),
@@ -790,15 +801,9 @@
             pltpu.VMEM((LF * BP, 3 * HW), jnp.bfloat16),
             pltpu.VMEM((LF * BP, HW), jnp.bfloat16),
             pltpu.VMEM((ROWS, 128), jnp.bfloat16),
-            pltpu.VMEM((HALF, 128), jnp.bfloat16),
-            pltpu.VMEM((HALF, 128), jnp.bfloat16),
-            pltpu.VMEM((HALF, 128), jnp.bfloat16),
-            pltpu.VMEM((16, PIECE, 128), jnp.float32),
-            pltpu.VMEM((16, PIECE, 128), jnp.float32),
-            pltpu.VMEM((16, PIECE, 128), jnp.float32),
+            *sums,
             dma((3,)), dma((slots,)), dma((slots,)), dma((slots,)), dma, dma, dma,
-            dma((8,)), dma((8,)), dma((8,)), dma((8,)), dma((16,)), dma((16,)),
-            dma((16,)), dma((16,)), dma((8,)), dma((8,)), dma((8,)), dma((8,)),
+            *[dma((2, size)) for size in (8, 8, 8, 8, 16, 16, 16, 16, 8, 8, 8, 8)],
         ],
         compiler_params=pltpu.CompilerParams(
             has_side_effects=True, collective_id=2, vmem_limit_bytes=32 << 20
@@ -809,9 +814,10 @@
 
 def widen_kernel(src, qkv, out):
     for i in range(9):
-        qkv[:, 128 * i : 128 * (i + 1)] = src[D * i : D * (i + 1), :].astype(jnp.float32)
+        start = D * i if i < 3 else KEYS_AT + D * (i - 3)
+        qkv[:, 128 * i : 128 * (i + 1)] = src[start : start + D, :].astype(jnp.float32)
     for i in range(6):
-        start = 9 * D + HW * i
+        start = 3 * D + HW * i
         out[:, 128 * i : 128 * (i + 1)] = src[start : start + HW, :].astype(jnp.float32)
 
 
@@ -835,8 +841,8 @@
     tm_size = lax.axis_size("tm")
     flat_tokens = tokens.reshape(-1, D)
     flat_grad = grad_out.reshape(-1, D)
-    q, kv = spread(flat_tokens, flat_grad, w_qkv, w_out, slots, tm_size)
-    res_q, res_kv = attend(block_table, brain_mask, q, kv, tm_size)
+    held = spread(flat_tokens, flat_grad, w_qkv, w_out, slots, tm_size)
+    res_q, res_kv = attend(block_table, brain_mask, held, tm_size)
     token_grads, terms = finish(res_q, res_kv, flat_tokens, flat_grad, w_qkv, slots, tm_size)
     qkv_grads, out_grads = widen(terms)
     return (token_grads.reshape(tokens.shape), qkv_grads, out_grads)

time: 141 us -> 119 us (0.84)
  Pallas kernels: 131 us -> 112 us
  local copies, waits for them, and re-layouts: 9.65 us -> 5.3 us
    pallas_call x1, Pallas kernels: 22.6 us -> 11.4 us  [attend(): pl.pallas_call(functools.partial(attend_kernel, tm_size), out_shape=(jax....]
    pallas_call x1, Pallas kernels: 70.8 us -> 62.7 us  [finish(): pl.pallas_call(functools.partial(finish_kernel, slots, tm_size), out_shap...]
    unnamed x23 -> x21, local copies, waits for them, and re-layouts: 9.65 us -> 5.3 us
where the time goes in v5:
time: 119 us; the launch traced here: 118 us
  Pallas kernels  112 us (94%)
  local copies, waits for them, and re-layouts  5.3 us (4%)
    pallas_call x1, Pallas kernels, finish(): pl.pallas_call(functools.partial(finish_kernel, slots, tm_size), out_shap...  62.7 us
    pallas_call x1, Pallas kernels, spread(): pl.pallas_call(functools.partial(spread_kernel, slots, tm_size), out_shap...  35.8 us
    pallas_call x1, Pallas kernels, attend(): pl.pallas_call(functools.partial(attend_kernel, tm_size), out_shape=(jax....  11.4 us
    unnamed x21, local copies, waits for them, and re-layouts  5.3 us
    pallas_call x1, Pallas kernels, widen(): pl.pallas_call(widen_kernel, out_shape=(jax.ShapeDtypeStruct((D, 3 * HW),...  2.41 us

profile of v5, /device:TPU:1, one launch (start us, length us, event | category | flops | bytes accessed | tf_op | source)
XLA Modules:
  0.0 118.3 jit_solution(13478035581164687387)
XLA Ops:
  0.6 0.0 copy-start
  0.6 1.5 %copy-done = bf16[768,1152]{1,0:T(8,128)(2,1)S(1)} copy-done((bf16[768,1152]{1,0:T(8,128)(2,1)S(1)}, bf16[768,1152]{1,0:T(8,128)(2,1)}, u32[]{:S(2)}) %copy-start) | copy-done | bytes 1769496
  2.1 0.0 copy-start.3
  2.1 1.0 copy-done.3
  3.1 0.0 copy-start.5
  3.1 1.0 copy-done.5
  4.1 0.0 copy-start.7
  4.1 1.1 copy-done.7
  5.2 0.0 copy-start.2
  5.2 0.0 copy-start.8
  5.2 0.0 copy-start.9
  5.2 35.8 %spread.1.held = bf16[16,8,64,128]{3,2,1,0:T(8,128)(2,1)S(1)} custom-call(bf16[256,768]{1,0:T(8,128)(2,1)S(1)} %bitcast.3, bf16[256,768]{1,0:T(8,128)(2,1)S(1)} %bitcast.5, bf16[768,1152]{1,0:T(8,128)(2,1)S(1)} %copy-done, bf16[384,768]{1,0:T(8,128)(2,1)S(1)} %copy-done.7), custom_call_target="tpu_custom_call" | custom-call | tf_op jit(solution)/shard_map/spread/pallas_call | solution.py:176
  40.9 0.0 copy-done.2
  41.0 0.0 copy-done.8
  41.0 0.0 copy-done.9
  41.0 0.0 copy-start.1
  41.0 0.0 copy-start.4
  41.0 0.0 copy-start.6
  41.0 11.4 %attend.1 = (bf16[16,2,64,128]{3,2,1,0:T(8,128)(2,1)S(1)}, bf16[16,6,64,128]{3,2,1,0:T(8,128)(2,1)S(1)}) custom-call(s32[16]{0:T(128)S(1)} %copy-done.8, s32[16]{0:T(128)S(1)} %copy-done.9, bf16[16,8,64,128]{3,2,1,0:T(8,128)(2,1)S(1)} %spread.1.held, f32[10,384,128]{2,1,0:T(8,128)S(1)} %copy-done.2), custom_call_target="tpu_custom_call" | custom-call | tf_op jit(solution)/shard_map/attend/pallas_call | solution.py:384
  52.4 0.0 copy-done.1
  52.4 0.0 copy-done.4
  52.4 0.0 copy-done.6
  52.4 62.7 %finish.1 = (bf16[256,768]{1,0:T(8,128)(2,1)S(1)}, bf16[9216,128]{1,0:T(8,128)(2,1)S(1)}) custom-call(bf16[16,2,64,128]{3,2,1,0:T(8,128)(2,1)S(1)} %get-tuple-element.9.res_q, bf16[16,6,64,128]{3,2,1,0:T(8,128)(2,1)S(1)} %get-tuple-element.10.res_kv, bf16[256,768]{1,0:T(8,128)(2,1)S(1)} %bitcast.4, bf16[256,768]{1,0:T(8,128)(2,1)S(1)} %bitcast.6, ...), custom_call_target="tpu_custom_call" | custom-call | tf_op jit(solution)/shard_map/finish/pallas_call | solution.py:786
  115.2 2.4 %widen.1 = (f32[768,1152]{1,0:T(8,128)}, f32[384,768]{1,0:T(8,128)}) custom-call(bf16[9216,128]{1,0:T(8,128)(2,1)S(1)} %get-tuple-element.12.src), custom_call_target="tpu_custom_call" | custom-call | tf_op jit(solution)/shard_map/widen/pallas_call | solution.py:826
  117.6 0.7 copy.11
Async XLA Ops:
  0.6 1.5 %copy-start = (bf16[768,1152]{1,0:T(8,128)(2,1)S(1)}, bf16[768,1152]{1,0:T(8,128)(2,1)}, u32[]{:S(2)}) copy-start(bf16[768,1152]{1,0:T(8,128)(2,1)} %wqkv_hbm.3) | copy-start | bytes 5308420
  2.1 1.0 copy-start.3
  3.1 1.0 copy-start.5
  4.1 1.1 copy-start.7
  5.2 35.8 %copy-start.2 = (f32[10,384,128]{2,1,0:T(8,128)S(1)}, f32[10,384,128]{2,1,0:T(8,128)}, u32[]{:S(2)}) copy-start(f32[10,384,128]{2,1,0:T(8,128)} %constant.2.clone.bias_hbm) | copy-start | bytes 5898244
  5.2 35.8 %copy-start.8 = (s32[16]{0:T(128)S(1)}, s32[16]{0:T(128)}, u32[]{:S(2)}) copy-start(s32[16]{0:T(128)} %table.1) | copy-start | bytes 196
  5.2 35.8 %copy-start.9 = (s32[16]{0:T(128)S(1)}, s32[16]{0:T(128)}, u32[]{:S(2)}) copy-start(s32[16]{0:T(128)} %mask.1) | copy-start | bytes 196
  41.0 11.4 %copy-start.1 = (bf16[768,1152]{1,0:T(8,128)(2,1)S(1)}, bf16[768,1152]{1,0:T(8,128)(2,1)}, u32[]{:S(2)}) copy-start(bf16[768,1152]{1,0:T(8,128)(2,1)} %wqkv_hbm.3) | copy-start | bytes 5308420
  41.0 11.4 %copy-start.4 = (bf16[1,4,64,768]{3,2,1,0:T(8,128)(2,1)S(1)}, bf16[1,4,64,768]{3,2,1,0:T(8,128)(2,1)}, u32[]{:S(2)}) copy-start(bf16[1,4,64,768]{3,2,1,0:T(8,128)(2,1)} %param.7) | copy-start | bytes 1179652
  41.0 11.4 %copy-start.6 = (bf16[1,4,64,768]{3,2,1,0:T(8,128)(2,1)S(1)}, bf16[1,4,64,768]{3,2,1,0:T(8,128)(2,1)}, u32[]{:S(2)}) copy-start(bf16[1,4,64,768]{3,2,1,0:T(8,128)(2,1)} %param.8) | copy-start | bytes 1179652

commit v6 on v5

--- a/solution.py
+++ b/solution.py
@@ -32,15 +32,11 @@
 
 
 def worker_space(w):
-    row = w // 6
-    at = w - 6 * row
-    return 8 * row + at + (at + 2 * row) // 3
+    return w
 
 
 def worker_of(space):
-    row = space // 8
-    at = space - 8 * row
-    return ((at + 1 + 2 * row) % 4 + 3) // 4, 6 * row + at - (at + 2 * row) // 4
+    return 1 - space // WORKERS, space
 
 
 def signal(semaphore, space, tm):
@@ -172,12 +168,11 @@
 
 def spread(tokens, grad_out, w_qkv, w_out, slots, tm_size):
     hbm = pl.BlockSpec(memory_space=pltpu.HBM)
-    vmem = pl.BlockSpec(memory_space=pltpu.VMEM)
     return pl.pallas_call(
         functools.partial(spread_kernel, slots, tm_size),
         out_shape=jax.ShapeDtypeStruct((slots, 8, BP, 128), jnp.bfloat16),
         in_specs=[hbm] * 4,
-        out_specs=vmem,
+        out_specs=hbm,
         scratch_shapes=[
             pltpu.VMEM(tokens.shape, jnp.bfloat16),
             pltpu.VMEM(grad_out.shape, jnp.bfloat16),
@@ -190,7 +185,7 @@
             pltpu.SemaphoreType.DMA,
         ],
         compiler_params=pltpu.CompilerParams(
-            has_side_effects=True, collective_id=1, vmem_limit_bytes=28 << 20
+            has_side_effects=True, collective_id=1, vmem_limit_bytes=60 << 20
         ),
         name="spread",
     )(tokens, grad_out, w_qkv, w_out)
@@ -217,8 +212,8 @@
 
 
 def attend_kernel(
-    tm_size, table, mask, held, bias_hbm, res_q, res_kv,
-    kvt, bias, acc, scores, dots, rhs_a, rhs_d, total, inverse, delta, att, dq,
+    tm_size, table, mask, held_hbm, bias_hbm, res_q, res_kv,
+    held, kvt, bias, acc, scores, dots, rhs_a, rhs_d, total, inverse, delta, att, dq,
     slot_of, brain, pair_q, pair_k, pair_off, sem,
 ):
     me = lax.axis_index("space")
@@ -233,8 +228,12 @@
 
     @pl.when(is_worker == 1)
     def _():
-        load = pltpu.make_async_copy(bias_hbm, bias, sem)
-        load.start()
+        loads = [
+            pltpu.make_async_copy(held_hbm, held, sem.at[0]),
+            pltpu.make_async_copy(bias_hbm, bias, sem.at[1]),
+        ]
+        for load in loads:
+            load.start()
 
         def place(s, carry):
             slot_of[table[s]] = s
@@ -288,8 +287,9 @@
             rhs_d[slot, QR:, :] = jnp.where(left, zero, rows)
             return carry
 
+        loads[0].wait()
         lax.fori_loop(0, blocks, prepare, 0)
-        load.wait()
+        loads[1].wait()
 
         @pl.when((t == 0) & (half == 0))
         def _():
@@ -380,6 +380,7 @@
     slots = held.shape[0]
     smem = pl.BlockSpec(memory_space=pltpu.SMEM)
     vmem = pl.BlockSpec(memory_space=pltpu.VMEM)
+    hbm = pl.BlockSpec(memory_space=pltpu.HBM)
     store = (PAIRS + UNROLL, KR, QR)
     return pl.pallas_call(
         functools.partial(attend_kernel, tm_size),
@@ -387,9 +388,10 @@
             jax.ShapeDtypeStruct((slots, 2, BP, 128), jnp.bfloat16),
             jax.ShapeDtypeStruct((slots, KF, BP, 128), jnp.bfloat16),
         ),
-        in_specs=[smem, smem, vmem, pl.BlockSpec(memory_space=pltpu.HBM)],
+        in_specs=[smem, smem, hbm, hbm],
         out_specs=(vmem, vmem),
         scratch_shapes=[
+            pltpu.VMEM(held.shape, jnp.bfloat16),
             pltpu.VMEM((slots, 128, KR), jnp.bfloat16),
             pltpu.VMEM((10, KR, QR), jnp.float32),
             pltpu.VMEM((slots, KR, 128), jnp.float32),
@@ -407,9 +409,9 @@
             pltpu.SMEM((PAIRS + UNROLL,), jnp.int32),
             pltpu.SMEM((PAIRS + UNROLL,), jnp.int32),
             pltpu.SMEM((PAIRS + UNROLL,), jnp.int32),
-            pltpu.SemaphoreType.DMA,
+            pltpu.SemaphoreType.DMA((2,)),
         ],
-        compiler_params=pltpu.CompilerParams(vmem_limit_bytes=47 << 20),
+        compiler_params=pltpu.CompilerParams(vmem_limit_bytes=50 << 20),
         name="attend",
     )(block_table, brain_mask, held, jnp.asarray(window_bias()))
 
@@ -426,8 +428,8 @@
 
 def finish_kernel(
     slots, tm_size, res_q, res_kv, tok_hbm, gout_hbm, wqkv_hbm, tg_ref, out,
-    got_q, got_kv, got_halo, tok, gout, wqkv, grads, att, src, early, late,
-    lsem, cq, cs, ch, cqr, cr, crh, ss0, r0, ss1, r1, ss2, r2, ss3, r3, ss4, r4, ss5, r5,
+    got_q, got_kv, got_halo, pair_in, summed, tok, gout, wqkv, grads, att, src, early, late,
+    lsem, psem, cq, cs, ch, cqr, cr, crh, ss0, r0, ss1, r1, ss2, r2, ss3, r3, ss4, r4, ss5, r5,
 ):
     s = lax.axis_index("space")
     t = lax.axis_index("tm")
@@ -494,11 +496,17 @@
 
     pl.semaphore_wait(barrier, is_worker * (2 * slots - 1) + 15 + 4 * core)
 
+    each = slots // 2
+    pair_copy = remote(
+        res_kv.at[pl.ds(each * (1 - half), each), pl.ds(2 - 2 * half, 4)], pair_in,
+        psem.at[0], psem.at[1], sibling,
+    )
+
     def query_refs(i):
         return res_q.at[i], got_q.at[half, head]
 
     def key_refs(i):
-        return res_kv.at[i, pl.ds(2 - 2 * half, 4)], got_kv.at[half, head]
+        return summed.at[i % each], got_kv.at[head]
 
     def query_copy(i):
         a, b = query_refs(i)
@@ -530,9 +538,15 @@
 
             return carry
 
+        def send_halo(i, carry):
+            halo_copy(lax.rem(i + s, slots)).start()
+            return carry
+
         def send_keys(i, carry):
-            to = lax.rem(i + s, slots)
-            halo_copy(to).start()
+            at = lax.rem(i + s, each)
+            to = each * half + at
+            mine = res_kv[to, pl.ds(2 - 2 * half, 4)].astype(jnp.float32)
+            summed[at] = (mine + pair_in[at].astype(jnp.float32)).astype(jnp.bfloat16)
 
             @pl.when(to != s)
             def _():
@@ -545,8 +559,11 @@
 
             return carry
 
+        pair_copy.start()
         lax.fori_loop(0, slots, send_queries, 0)
-        lax.fori_loop(0, slots, send_keys, 0)
+        lax.fori_loop(0, slots, send_halo, 0)
+        pair_copy.wait_recv()
+        lax.fori_loop(0, each, send_keys, 0)
 
     for load in loads:
         load.wait()
@@ -584,10 +601,8 @@
         for i in range(HEADS // 2):
             both = []
             for h in (2 * i, 2 * i + 1):
-                low = got_kv[0, h].astype(jnp.float32)
-                high = got_kv[1, h].astype(jnp.float32)
                 edge = jnp.concatenate([got_halo[1, h], got_halo[0, h]], axis=0).astype(jnp.float32)
-                both.append((low + high + edge).reshape(LF * BP, 128))
+                both.append((got_kv[h].astype(jnp.float32) + edge).reshape(LF * BP, 128))
             for k, value in enumerate(pair(*both)):
                 at = (1 + k) * HW + 128 * i
                 grads[:, at : at + 128] = value
@@ -766,11 +781,21 @@
             @pl.when(i != s)
             def _():
                 query_copy(i).wait_send()
-                key_copy(i).wait_send()
+
+            return carry
+
+        def finish_keys(i, carry):
+            to = each * half + i
+
+            @pl.when(to != s)
+            def _():
+                key_copy(to).wait_send()
 
             return carry
 
         lax.fori_loop(0, slots, finish, 0)
+        lax.fori_loop(0, each, finish_keys, 0)
+        pair_copy.wait_send()
 
 
 def finish(res_q, res_kv, tokens, grad_out, w_qkv, slots, tm_size):
@@ -793,8 +818,10 @@
         out_specs=(vmem, vmem),
         scratch_shapes=[
             pltpu.VMEM((2, HEADS, 2, BP, 128), jnp.bfloat16),
-            pltpu.VMEM((2, HEADS, LF, BP, 128), jnp.bfloat16),
+            pltpu.VMEM((HEADS, LF, BP, 128), jnp.bfloat16),
             pltpu.VMEM((2, HEADS, 2, BP, 128), jnp.bfloat16),
+            pltpu.VMEM((slots // 2, LF, BP, 128), jnp.bfloat16),
+            pltpu.VMEM((slots // 2, LF, BP, 128), jnp.bfloat16),
             pltpu.VMEM(tokens.shape, jnp.bfloat16),
             pltpu.VMEM(grad_out.shape, jnp.bfloat16),
             pltpu.VMEM(w_qkv.shape, jnp.bfloat16),
@@ -802,7 +829,7 @@
             pltpu.VMEM((LF * BP, HW), jnp.bfloat16),
             pltpu.VMEM((ROWS, 128), jnp.bfloat16),
             *sums,
-            dma((3,)), dma((slots,)), dma((slots,)), dma((slots,)), dma, dma, dma,
+            dma((3,)), dma((2,)), dma((slots,)), dma((slots,)), dma((slots,)), dma, dma, dma,
             *[dma((2, size)) for size in (8, 8, 8, 8, 16, 16, 16, 16, 8, 8, 8, 8)],
         ],
         compiler_params=pltpu.CompilerParams(

time: 119 us -> 114 us (0.958)
  local copies, waits for them, and re-layouts: 5.3 us -> 0.78 us
    pallas_call x1, Pallas kernels: 62.7 us -> 56.6 us  [finish(): pl.pallas_call(functools.partial(finish_kernel, slots, tm_size), out_shap...]
    unnamed x21 -> x13, local copies, waits for them, and re-layouts: 5.3 us -> 0.78 us
    pallas_call x1, Pallas kernels: 35.8 us -> 38.3 us  [spread(): pl.pallas_call(functools.partial(spread_kernel, slots, tm_size), out_shap...]
    pallas_call x1, Pallas kernels: 11.4 us -> 13.5 us  [attend(): pl.pallas_call(functools.partial(attend_kernel, tm_size), out_shape=(jax....]
where the time goes in v6:
time: 114 us; the launch traced here: 112 us
  Pallas kernels  111 us (97%)
    pallas_call x1, Pallas kernels, finish(): pl.pallas_call(functools.partial(finish_kernel, slots, tm_size), out_shap...  56.6 us
    pallas_call x1, Pallas kernels, spread(): pl.pallas_call(functools.partial(spread_kernel, slots, tm_size), out_shap...  38.3 us
    pallas_call x1, Pallas kernels, attend(): pl.pallas_call(functools.partial(attend_kernel, tm_size), out_shape=(jax....  13.5 us
    pallas_call x1, Pallas kernels, widen(): pl.pallas_call(widen_kernel, out_shape=(jax.ShapeDtypeStruct((D, 3 * HW),...  2.41 us

profile of v6, /device:TPU:1, one launch (start us, length us, event | category | flops | bytes accessed | tf_op | source)
XLA Modules:
  0.0 112.3 jit_solution(18426177184542056652)
XLA Ops:
  0.6 0.0 copy-start.1
  0.6 0.0 copy-start.4
  0.7 0.0 copy-start.5
  0.7 38.3 %spread.1.held_hbm = bf16[16,8,64,128]{3,2,1,0:T(8,128)(2,1)} custom-call(bf16[256,768]{1,0:T(8,128)(2,1)} %bitcast.3, bf16[256,768]{1,0:T(8,128)(2,1)} %bitcast.5, bf16[768,1152]{1,0:T(8,128)(2,1)} %wqkv_hbm.3, bf16[384,768]{1,0:T(8,128)(2,1)} %wout_hbm.1), custom_call_target="tpu_custom_call" | custom-call | tf_op jit(solution)/shard_map/spread/pallas_call | solution.py:171
  38.9 0.0 copy-done.1
  38.9 0.0 copy-done.4
  39.0 0.0 copy-done.5
  39.0 0.0 copy-start
  39.0 0.0 copy-start.2
  39.0 0.0 copy-start.3
  39.0 13.5 %attend.1 = (bf16[16,2,64,128]{3,2,1,0:T(8,128)(2,1)S(1)}, bf16[16,6,64,128]{3,2,1,0:T(8,128)(2,1)S(1)}) custom-call(s32[16]{0:T(128)S(1)} %copy-done.4, s32[16]{0:T(128)S(1)} %copy-done.5, bf16[16,8,64,128]{3,2,1,0:T(8,128)(2,1)} %spread.1.held_hbm, f32[10,384,128]{2,1,0:T(8,128)S(1)} %copy-done.1), custom_call_target="tpu_custom_call" | custom-call | tf_op jit(solution)/shard_map/attend/pallas_call | solution.py:385
  52.5 0.0 copy-done
  52.5 0.0 copy-done.2
  52.5 0.0 copy-done.3
  52.5 56.6 %finish.1 = (bf16[256,768]{1,0:T(8,128)(2,1)S(1)}, bf16[9216,128]{1,0:T(8,128)(2,1)S(1)}) custom-call(bf16[16,2,64,128]{3,2,1,0:T(8,128)(2,1)S(1)} %get-tuple-element.9.res_q, bf16[16,6,64,128]{3,2,1,0:T(8,128)(2,1)S(1)} %get-tuple-element.10.res_kv, bf16[256,768]{1,0:T(8,128)(2,1)S(1)} %bitcast.4, bf16[256,768]{1,0:T(8,128)(2,1)S(1)} %bitcast.6, ...), custom_call_target="tpu_custom_call" | custom-call | tf_op jit(solution)/shard_map/finish/pallas_call | solution.py:811
  109.1 2.4 %widen.1 = (f32[768,1152]{1,0:T(8,128)}, f32[384,768]{1,0:T(8,128)}) custom-call(bf16[9216,128]{1,0:T(8,128)(2,1)S(1)} %get-tuple-element.12.src), custom_call_target="tpu_custom_call" | custom-call | tf_op jit(solution)/shard_map/widen/pallas_call | solution.py:853
  111.5 0.7 copy.11
Async XLA Ops:
  0.6 38.3 %copy-start.1 = (f32[10,384,128]{2,1,0:T(8,128)S(1)}, f32[10,384,128]{2,1,0:T(8,128)}, u32[]{:S(2)}) copy-start(f32[10,384,128]{2,1,0:T(8,128)} %constant.2.clone.bias_hbm) | copy-start | bytes 5898244
  0.6 38.3 %copy-start.4 = (s32[16]{0:T(128)S(1)}, s32[16]{0:T(128)}, u32[]{:S(2)}) copy-start(s32[16]{0:T(128)} %table.1) | copy-start | bytes 196
  0.7 38.3 %copy-start.5 = (s32[16]{0:T(128)S(1)}, s32[16]{0:T(128)}, u32[]{:S(2)}) copy-start(s32[16]{0:T(128)} %mask.1) | copy-start | bytes 196
  39.0 13.5 %copy-start = (bf16[768,1152]{1,0:T(8,128)(2,1)S(1)}, bf16[768,1152]{1,0:T(8,128)(2,1)}, u32[]{:S(2)}) copy-start(bf16[768,1152]{1,0:T(8,128)(2,1)} %wqkv_hbm.3) | copy-start | bytes 5308420
  39.0 13.5 %copy-start.2 = (bf16[1,4,64,768]{3,2,1,0:T(8,128)(2,1)S(1)}, bf16[1,4,64,768]{3,2,1,0:T(8,128)(2,1)}, u32[]{:S(2)}) copy-start(bf16[1,4,64,768]{3,2,1,0:T(8,128)(2,1)} %param.7) | copy-start | bytes 1179652
  39.0 13.5 %copy-start.3 = (bf16[1,4,64,768]{3,2,1,0:T(8,128)(2,1)S(1)}, bf16[1,4,64,768]{3,2,1,0:T(8,128)(2,1)}, u32[]{:S(2)}) copy-start(bf16[1,4,64,768]{3,2,1,0:T(8,128)(2,1)} %param.8) | copy-start | bytes 1179652

commit v7 on v6

--- a/solution.py
+++ b/solution.py
@@ -87,26 +87,11 @@
 
     for load in loads:
         load.wait()
-    proj = jnp.dot(tok[...], wqkv[...], preferred_element_type=jnp.float32)
-    gatt = lax.dot_general(
-        gout[...], wout[...], (((1,), (1,)), ((), ())), preferred_element_type=jnp.float32
-    )
 
     def pair(low, high):
         first = where_lane(low, pltpu.roll(high, HD, 1)).astype(jnp.bfloat16)
         second = where_lane(pltpu.roll(low, HD, 1), high).astype(jnp.bfloat16)
         return first.reshape(LF, BP, 128), second.reshape(LF, BP, 128)
-
-    for i in range(HEADS // 2):
-        at = 128 * i
-        keys = pair(proj[:, HW + at : HW + at + 128], proj[:, 2 * HW + at : 2 * HW + at + 128])
-        queries = pair(proj[:, at : at + 128], gatt[:, at : at + 128])
-        for j in range(2):
-            packed[2 * i + j, 0:2] = queries[j][2:4]
-            packed[2 * i + j, 2:6] = keys[j]
-            packed[2 * i + j, 6:8] = queries[j][0:2]
-
-    pl.semaphore_wait(barrier, 2 * WORKERS - is_worker)
 
     def main_refs(w):
         start = 2 - 2 * (w % 2)
@@ -123,28 +108,46 @@
             {"space": worker_space(2 * h + half), "tm": before if half else after},
         )
 
-    def send(i, carry):
-        w = lax.rem(i + me, WORKERS)
-
-        @pl.when(worker_space(w) != me)
-        def _():
-            main_copy(w).start()
-
-        @pl.when(worker_space(w) == me)
-        def _():
-            src, dst = main_refs(w)
-            pltpu.make_async_copy(src, dst, rsem).start()
-
-        return carry
-
-    def send_halo(i, carry):
-        h = lax.rem(i + me // 2, HEADS)
-        halo_copy(h, 0).start()
-        halo_copy(h, 1).start()
-        return carry
-
-    lax.fori_loop(0, HEADS, send_halo, 0)
-    lax.fori_loop(0, WORKERS, send, 0)
+    for turn in range(HEADS // 2):
+        i = (me // 2 + turn) % (HEADS // 2)
+
+        def columns(start):
+            return pl.ds(pl.multiple_of(start + 128 * i, 128), 128)
+
+        def product(start):
+            return jnp.dot(tok[...], wqkv[:, columns(start)], preferred_element_type=jnp.float32)
+
+        gatt = lax.dot_general(
+            gout[...], wout[columns(0), :], (((1,), (1,)), ((), ())),
+            preferred_element_type=jnp.float32,
+        )
+        keys = pair(product(HW), product(2 * HW))
+        queries = pair(product(0), gatt)
+        for j in range(2):
+            packed[2 * i + j, 0:2] = queries[j][2:4]
+            packed[2 * i + j, 2:6] = keys[j]
+            packed[2 * i + j, 6:8] = queries[j][0:2]
+        if turn == 0:
+            pl.semaphore_wait(barrier, 2 * WORKERS - is_worker)
+
+        def send(k, carry):
+            w = 4 * i + (k + me) % 4
+
+            @pl.when(worker_space(w) != me)
+            def _():
+                main_copy(w).start()
+
+            @pl.when(worker_space(w) == me)
+            def _():
+                src, dst = main_refs(w)
+                pltpu.make_async_copy(src, dst, rsem).start()
+
+            return carry
+
+        for j in range(2):
+            halo_copy(2 * i + j, 0).start()
+            halo_copy(2 * i + j, 1).start()
+        lax.fori_loop(0, 4, send, 0)
 
     def finish(w, carry):
         @pl.when(worker_space(w) != me)
@@ -191,7 +194,7 @@
     )(tokens, grad_out, w_qkv, w_out)
 
 
-UNROLL = 8
+UNROLL = 12
 MOST = 12
 PAIRS = 72
 
@@ -243,22 +246,27 @@
 
         def list_block(g, carry):
             blocks, pairs = carry
-            inside_brain = mask[g] == 1
-            slot = slot_of[g]
-            brain[blocks] = slot
-            row = g // SIDE
-            col = g % SIDE
-            for n in range(9):
-                nr = row + (n // 3 - 1)
-                nc = col + (n % 3 - 1)
-                inside = (nr >= 0) & (nr < SIDE) & (nc >= 0) & (nc < SIDE)
-                nb = jnp.clip(nr, 0, SIDE - 1) * SIDE + jnp.clip(nc, 0, SIDE - 1)
-                valid = inside_brain & inside & (mask[nb] == 1)
-                pair_q[pairs] = slot
-                pair_k[pairs] = slot_of[nb]
-                pair_off[pairs] = n
-                pairs = jnp.minimum(pairs + valid.astype(jnp.int32), PAIRS)
-            return (blocks + inside_brain.astype(jnp.int32), pairs)
+
+            def add(g, blocks, pairs):
+                slot = slot_of[g]
+                brain[blocks] = slot
+                row = g // SIDE
+                col = g % SIDE
+                for n in range(9):
+                    nr = row + (n // 3 - 1)
+                    nc = col + (n % 3 - 1)
+                    inside = (nr >= 0) & (nr < SIDE) & (nc >= 0) & (nc < SIDE)
+                    nb = jnp.clip(nr, 0, SIDE - 1) * SIDE + jnp.clip(nc, 0, SIDE - 1)
+                    valid = inside & (mask[nb] == 1)
+                    pair_q[pairs] = slot
+                    pair_k[pairs] = slot_of[nb]
+                    pair_off[pairs] = n
+                    pairs = jnp.minimum(pairs + valid.astype(jnp.int32), PAIRS)
+                return (blocks + 1, pairs)
+
+            return lax.cond(
+                mask[g] == 1, functools.partial(add, g, blocks, pairs), lambda: (blocks, pairs)
+            )
 
         blocks, pairs = lax.fori_loop(0, slots, list_block, (jnp.int32(0), jnp.int32(0)))
         for n in range(UNROLL):
@@ -411,7 +419,7 @@
             pltpu.SMEM((PAIRS + UNROLL,), jnp.int32),
             pltpu.SemaphoreType.DMA((2,)),
         ],
-        compiler_params=pltpu.CompilerParams(vmem_limit_bytes=50 << 20),
+        compiler_params=pltpu.CompilerParams(vmem_limit_bytes=48 << 20),
         name="attend",
     )(block_table, brain_mask, held, jnp.asarray(window_bias()))
 
@@ -839,28 +847,50 @@
     )(res_q, res_kv, tokens, grad_out, w_qkv)
 
 
-def widen_kernel(src, qkv, out):
-    for i in range(9):
-        start = D * i if i < 3 else KEYS_AT + D * (i - 3)
-        qkv[:, 128 * i : 128 * (i + 1)] = src[start : start + D, :].astype(jnp.float32)
-    for i in range(6):
-        start = 3 * D + HW * i
-        out[:, 128 * i : 128 * (i + 1)] = src[start : start + HW, :].astype(jnp.float32)
-
-
-def widen(terms):
+def widen_kernel(src, tg, qkv, out, tg_out, wide, wide_out, sem):
+    step = 96
+    copies = [pltpu.make_async_copy(tg, tg_out, sem.at[0])]
+    copies[0].start()
+    for k in range(D // step):
+        rows = pl.ds(step * k, step)
+        for i in range(9):
+            start = D * i if i < 3 else KEYS_AT + D * (i - 3)
+            part = src[start + step * k : start + step * (k + 1), :]
+            wide[rows, 128 * i : 128 * (i + 1)] = part.astype(jnp.float32)
+        copies.append(pltpu.make_async_copy(wide.at[rows], qkv.at[rows], sem.at[len(copies)]))
+        copies[-1].start()
+    for k in range(HW // step):
+        rows = pl.ds(step * k, step)
+        for i in range(6):
+            start = 3 * D + HW * i
+            part = src[start + step * k : start + step * (k + 1), :]
+            wide_out[rows, 128 * i : 128 * (i + 1)] = part.astype(jnp.float32)
+        copies.append(pltpu.make_async_copy(wide_out.at[rows], out.at[rows], sem.at[len(copies)]))
+        copies[-1].start()
+    for copy in copies:
+        copy.wait()
+
+
+def widen(terms, token_grads):
     vmem = pl.BlockSpec(memory_space=pltpu.VMEM)
+    hbm = pl.BlockSpec(memory_space=pltpu.HBM)
     return pl.pallas_call(
         widen_kernel,
         out_shape=(
             jax.ShapeDtypeStruct((D, 3 * HW), jnp.float32),
             jax.ShapeDtypeStruct((HW, D), jnp.float32),
+            jax.ShapeDtypeStruct(token_grads.shape, jnp.bfloat16),
         ),
-        in_specs=[vmem],
-        out_specs=(vmem, vmem),
+        in_specs=[vmem, vmem],
+        out_specs=(hbm, hbm, hbm),
+        scratch_shapes=[
+            pltpu.VMEM((D, 3 * HW), jnp.float32),
+            pltpu.VMEM((HW, D), jnp.float32),
+            pltpu.SemaphoreType.DMA((1 + (D + HW) // 96,)),
+        ],
         compiler_params=pltpu.CompilerParams(vmem_limit_bytes=32 << 20),
         name="widen",
-    )(terms)
+    )(terms, token_grads)
 
 
 def shards(tokens, grad_out, w_qkv, w_out, brain_mask, block_table):
@@ -871,7 +901,7 @@
     held = spread(flat_tokens, flat_grad, w_qkv, w_out, slots, tm_size)
     res_q, res_kv = attend(block_table, brain_mask, held, tm_size)
     token_grads, terms = finish(res_q, res_kv, flat_tokens, flat_grad, w_qkv, slots, tm_size)
-    qkv_grads, out_grads = widen(terms)
+    qkv_grads, out_grads, token_grads = widen(terms, token_grads)
     return (token_grads.reshape(tokens.shape), qkv_grads, out_grads)
 
 

time: 114 us -> 108 us (0.947); the launches traced: 112 us -> 108 us
  Pallas kernels: 111 us -> 106 us
    pallas_call x1, Pallas kernels: 13.5 us -> 8.91 us  [attend(): pl.pallas_call(functools.partial(attend_kernel, tm_size), out_shape=(jax....]
    pallas_call x1, Pallas kernels: 38.3 us -> 34.5 us  [spread(): pl.pallas_call(functools.partial(spread_kernel, slots, tm_size), out_shap...]
    pallas_call x1, Pallas kernels: 56.6 us -> 60.1 us  [finish(): pl.pallas_call(functools.partial(finish_kernel, slots, tm_size), out_shap...]
where the time goes in v7:
time: 108 us
  Pallas kernels  106 us (98%)
  local copies, waits for them, and re-layouts  1.61 us (1%)
    pallas_call x1, Pallas kernels, finish(): pl.pallas_call(functools.partial(finish_kernel, slots, tm_size), out_shap...  60.1 us
    pallas_call x1, Pallas kernels, spread(): pl.pallas_call(functools.partial(spread_kernel, slots, tm_size), out_shap...  34.5 us
    pallas_call x1, Pallas kernels, attend(): pl.pallas_call(functools.partial(attend_kernel, tm_size), out_shape=(jax....  8.91 us
    pallas_call x1, Pallas kernels, widen(): pl.pallas_call(widen_kernel, out_shape=(jax.ShapeDtypeStruct((D, 3 * HW),...  2.4 us

profile of v7, /device:TPU:1, one launch (start us, length us, event | category | flops | bytes accessed | tf_op | source)
XLA Modules:
  0.0 108.2 jit_solution(14049320750817730492)
XLA Ops:
  0.6 0.0 copy-start.2
  0.6 0.0 copy-start.5
  0.7 0.0 copy-start.6
  0.7 34.5 %spread.1.held_hbm = bf16[16,8,64,128]{3,2,1,0:T(8,128)(2,1)} custom-call(bf16[256,768]{1,0:T(8,128)(2,1)} %bitcast.3, bf16[256,768]{1,0:T(8,128)(2,1)} %bitcast.5, bf16[768,1152]{1,0:T(8,128)(2,1)} %wqkv_hbm.3, bf16[384,768]{1,0:T(8,128)(2,1)} %wout_hbm.1), custom_call_target="tpu_custom_call" | custom-call | tf_op jit(solution)/shard_map/spread/pallas_call | solution.py:174
  35.1 0.0 copy-done.2
  35.1 0.0 copy-done.5
  35.1 0.0 copy-done.6
  35.2 0.0 copy-start
  35.2 1.6 %copy-done = bf16[16,8,64,128]{3,2,1,0:T(8,128)(2,1)S(1)} copy-done((bf16[16,8,64,128]{3,2,1,0:T(8,128)(2,1)S(1)}, bf16[16,8,64,128]{3,2,1,0:T(8,128)(2,1)}, u32[]{:S(2)}) %copy-start) | copy-done | bytes 2097176
  36.7 0.0 copy-start.1
  36.7 0.0 copy-start.3
  36.8 0.0 copy-start.4
  36.8 8.9 %attend.1 = (bf16[16,2,64,128]{3,2,1,0:T(8,128)(2,1)S(1)}, bf16[16,6,64,128]{3,2,1,0:T(8,128)(2,1)S(1)}) custom-call(s32[16]{0:T(128)S(1)} %copy-done.5, s32[16]{0:T(128)S(1)} %copy-done.6, bf16[16,8,64,128]{3,2,1,0:T(8,128)(2,1)S(1)} %copy-done, f32[10,384,128]{2,1,0:T(8,128)S(1)} %copy-done.2), custom_call_target="tpu_custom_call" | custom-call | tf_op jit(solution)/shard_map/attend/pallas_call | solution.py:393
  45.7 0.0 copy-done.1
  45.7 0.0 copy-done.3
  45.7 0.0 copy-done.4
  45.7 60.1 %finish.1 = (bf16[256,768]{1,0:T(8,128)(2,1)S(1)}, bf16[9216,128]{1,0:T(8,128)(2,1)S(1)}) custom-call(bf16[16,2,64,128]{3,2,1,0:T(8,128)(2,1)S(1)} %get-tuple-element.10.res_q, bf16[16,6,64,128]{3,2,1,0:T(8,128)(2,1)S(1)} %get-tuple-element.11.res_kv, bf16[256,768]{1,0:T(8,128)(2,1)S(1)} %bitcast.4, bf16[256,768]{1,0:T(8,128)(2,1)S(1)} %bitcast.6, ...), custom_call_target="tpu_custom_call" | custom-call | tf_op jit(solution)/shard_map/finish/pallas_call | solution.py:819
  105.8 2.4 %widen.1 = (f32[768,1152]{1,0:T(8,128)}, f32[384,768]{1,0:T(8,128)}, bf16[256,768]{1,0:T(8,128)(2,1)}) custom-call(bf16[9216,128]{1,0:T(8,128)(2,1)S(1)} %get-tuple-element.12.src, bf16[256,768]{1,0:T(8,128)(2,1)S(1)} %get-tuple-element.13.tg), custom_call_target="tpu_custom_call" | custom-call | tf_op jit(solution)/shard_map/widen/pallas_call | solution.py:877
Async XLA Ops:
  0.6 34.5 %copy-start.2 = (f32[10,384,128]{2,1,0:T(8,128)S(1)}, f32[10,384,128]{2,1,0:T(8,128)}, u32[]{:S(2)}) copy-start(f32[10,384,128]{2,1,0:T(8,128)} %constant.2.clone.bias_hbm) | copy-start | bytes 5898244
  0.6 34.5 %copy-start.5 = (s32[16]{0:T(128)S(1)}, s32[16]{0:T(128)}, u32[]{:S(2)}) copy-start(s32[16]{0:T(128)} %table.1) | copy-start | bytes 196
  0.7 34.5 %copy-start.6 = (s32[16]{0:T(128)S(1)}, s32[16]{0:T(128)}, u32[]{:S(2)}) copy-start(s32[16]{0:T(128)} %mask.1) | copy-start | bytes 196
  35.2 1.6 %copy-start = (bf16[16,8,64,128]{3,2,1,0:T(8,128)(2,1)S(1)}, bf16[16,8,64,128]{3,2,1,0:T(8,128)(2,1)}, u32[]{:S(2)}) copy-start(bf16[16,8,64,128]{3,2,1,0:T(8,128)(2,1)} %spread.1.held_hbm) | copy-start | bytes 6291460
  36.7 8.9 %copy-start.1 = (bf16[768,1152]{1,0:T(8,128)(2,1)S(1)}, bf16[768,1152]{1,0:T(8,128)(2,1)}, u32[]{:S(2)}) copy-start(bf16[768,1152]{1,0:T(8,128)(2,1)} %wqkv_hbm.3) | copy-start | bytes 5308420
  36.7 8.9 %copy-start.3 = (bf16[1,4,64,768]{3,2,1,0:T(8,128)(2,1)S(1)}, bf16[1,4,64,768]{3,2,1,0:T(8,128)(2,1)}, u32[]{:S(2)}) copy-start(bf16[1,4,64,768]{3,2,1,0:T(8,128)(2,1)} %param.7) | copy-start | bytes 1179652
  36.8 8.9 %copy-start.4 = (bf16[1,4,64,768]{3,2,1,0:T(8,128)(2,1)S(1)}, bf16[1,4,64,768]{3,2,1,0:T(8,128)(2,1)}, u32[]{:S(2)}) copy-start(bf16[1,4,64,768]{3,2,1,0:T(8,128)(2,1)} %param.8) | copy-start | bytes 1179652

commit v8 on v7

--- a/solution.py
+++ b/solution.py
@@ -109,7 +109,7 @@
         )
 
     for turn in range(HEADS // 2):
-        i = (me // 2 + turn) % (HEADS // 2)
+        i = (me + t + turn) % (HEADS // 2)
 
         def columns(start):
             return pl.ds(pl.multiple_of(start + 128 * i, 128), 128)
@@ -419,7 +419,7 @@
             pltpu.SMEM((PAIRS + UNROLL,), jnp.int32),
             pltpu.SemaphoreType.DMA((2,)),
         ],
-        compiler_params=pltpu.CompilerParams(vmem_limit_bytes=48 << 20),
+        compiler_params=pltpu.CompilerParams(vmem_limit_bytes=51 << 20),
         name="attend",
     )(block_table, brain_mask, held, jnp.asarray(window_bias()))
 

time: 108 us -> 107 us (level); the launches traced: 108 us -> 106 us
  local copies, waits for them, and re-layouts: 1.61 us -> 0.03 us
    unnamed x14 -> x10, local copies, waits for them, and re-layouts: 1.61 us -> 0.03 us
    pallas_call x1, Pallas kernels: 60.1 us -> 58.7 us  [finish(): pl.pallas_call(functools.partial(finish_kernel, slots, tm_size), out_shap...]
where the time goes in v8:
time: 107 us; the launch traced here: 106 us
  Pallas kernels  105 us (98%)
    pallas_call x1, Pallas kernels, finish(): pl.pallas_call(functools.partial(finish_kernel, slots, tm_size), out_shap...  58.7 us
    pallas_call x1, Pallas kernels, spread(): pl.pallas_call(functools.partial(spread_kernel, slots, tm_size), out_shap...  35 us
    pallas_call x1, Pallas kernels, attend(): pl.pallas_call(functools.partial(attend_kernel, tm_size), out_shape=(jax....  8.95 us
    pallas_call x1, Pallas kernels, widen(): pl.pallas_call(widen_kernel, out_shape=(jax.ShapeDtypeStruct((D, 3 * HW),...  2.4 us

profile of v8, /device:TPU:1, one launch (start us, length us, event | category | flops | bytes accessed | tf_op | source)
XLA Modules:
  0.0 105.9 jit_solution(12919986290815627070)
XLA Ops:
  0.6 0.0 copy-start.3
  0.6 0.0 copy-start.4
  0.7 35.0 %spread.1.held_hbm = bf16[16,8,64,128]{3,2,1,0:T(8,128)(2,1)} custom-call(bf16[256,768]{1,0:T(8,128)(2,1)} %bitcast.3, bf16[256,768]{1,0:T(8,128)(2,1)} %bitcast.5, bf16[768,1152]{1,0:T(8,128)(2,1)} %wqkv_hbm.3, bf16[384,768]{1,0:T(8,128)(2,1)} %wout_hbm.1), custom_call_target="tpu_custom_call" | custom-call | tf_op jit(solution)/shard_map/spread/pallas_call | solution.py:174
  35.7 0.0 copy-done.3
  35.7 0.0 copy-done.4
  35.7 0.0 copy-start
  35.7 0.0 copy-start.1
  35.7 0.0 copy-start.2
  35.7 8.9 %attend.1 = (bf16[16,2,64,128]{3,2,1,0:T(8,128)(2,1)S(1)}, bf16[16,6,64,128]{3,2,1,0:T(8,128)(2,1)S(1)}) custom-call(s32[16]{0:T(128)S(1)} %copy-done.3, s32[16]{0:T(128)S(1)} %copy-done.4, bf16[16,8,64,128]{3,2,1,0:T(8,128)(2,1)} %spread.1.held_hbm, f32[10,384,128]{2,1,0:T(8,128)} %constant.2.clone.bias_hbm), custom_call_target="tpu_custom_call" | custom-call | tf_op jit(solution)/shard_map/attend/pallas_call | solution.py:393
  44.7 0.0 copy-done
  44.7 0.0 copy-done.1
  44.7 0.0 copy-done.2
  44.7 58.7 %finish.1 = (bf16[256,768]{1,0:T(8,128)(2,1)S(1)}, bf16[9216,128]{1,0:T(8,128)(2,1)S(1)}) custom-call(bf16[16,2,64,128]{3,2,1,0:T(8,128)(2,1)S(1)} %get-tuple-element.10.res_q, bf16[16,6,64,128]{3,2,1,0:T(8,128)(2,1)S(1)} %get-tuple-element.11.res_kv, bf16[256,768]{1,0:T(8,128)(2,1)S(1)} %bitcast.4, bf16[256,768]{1,0:T(8,128)(2,1)S(1)} %bitcast.6, ...), custom_call_target="tpu_custom_call" | custom-call | tf_op jit(solution)/shard_map/finish/pallas_call | solution.py:819
  103.5 2.4 %widen.1 = (f32[768,1152]{1,0:T(8,128)}, f32[384,768]{1,0:T(8,128)}, bf16[256,768]{1,0:T(8,128)(2,1)}) custom-call(bf16[9216,128]{1,0:T(8,128)(2,1)S(1)} %get-tuple-element.12.src, bf16[256,768]{1,0:T(8,128)(2,1)S(1)} %get-tuple-element.13.tg), custom_call_target="tpu_custom_call" | custom-call | tf_op jit(solution)/shard_map/widen/pallas_call | solution.py:877
Async XLA Ops:
  0.6 35.0 %copy-start.3 = (s32[16]{0:T(128)S(1)}, s32[16]{0:T(128)}, u32[]{:S(2)}) copy-start(s32[16]{0:T(128)} %table.1) | copy-start | bytes 196
  0.6 35.0 %copy-start.4 = (s32[16]{0:T(128)S(1)}, s32[16]{0:T(128)}, u32[]{:S(2)}) copy-start(s32[16]{0:T(128)} %mask.1) | copy-start | bytes 196
  35.7 9.0 %copy-start = (bf16[768,1152]{1,0:T(8,128)(2,1)S(1)}, bf16[768,1152]{1,0:T(8,128)(2,1)}, u32[]{:S(2)}) copy-start(bf16[768,1152]{1,0:T(8,128)(2,1)} %wqkv_hbm.3) | copy-start | bytes 5308420
  35.7 9.0 %copy-start.1 = (bf16[1,4,64,768]{3,2,1,0:T(8,128)(2,1)S(1)}, bf16[1,4,64,768]{3,2,1,0:T(8,128)(2,1)}, u32[]{:S(2)}) copy-start(bf16[1,4,64,768]{3,2,1,0:T(8,128)(2,1)} %param.7) | copy-start | bytes 1179652
  35.7 9.0 %copy-start.2 = (bf16[1,4,64,768]{3,2,1,0:T(8,128)(2,1)S(1)}, bf16[1,4,64,768]{3,2,1,0:T(8,128)(2,1)}, u32[]{:S(2)}) copy-start(bf16[1,4,64,768]{3,2,1,0:T(8,128)(2,1)} %param.8) | copy-start | bytes 1179652
